TPU v7x, 768 devices: a whole 4x8x12 slice. The times are simulated.
768 devices in a mesh: height: 64 (over y, x, core), plan: 12 (over z).
Axes of the slice: x: 4, y: 8, z: 12, core: 2. Of those that a mesh axis runs over, the one named last changes fastest.
Arguments:
- divergence: float32 [256, 192, 512], P('height', 'plan'), may hold values from -8 to 8
- density: float32 [256, 192, 512], P('height', 'plan'), may hold values from 0.5 to 2
- zones: int32 [256, 192, 512], P('height', 'plan'), may hold values from 0 to 4
Outputs:
- pressure: float32 [256, 192, 512], P('height', 'plan')
Inputs may be any that keep to these rules, and one draw needn't show every extreme that they name: `zones`: zone 0 open air, 1 wall, 2 stairwell, 3 open door, 4 closed door.
All inputs are finite; a program needn't handle non-finite values.
Results may differ from a plain program's by a relative error of at most 0.00002.
Values sent between devices are 32-bit elements; how exact they have to be, the bound alone decides.
No kernel may reach another device: no remote copies, remote signals or barrier semaphores. Data moves between devices by JAX's collectives and lax.ppermute only.
A program may use at most 32 MiB of HBM per device.

v0:
```python
import jax
import jax.numpy as jnp
from jax import lax
from jax.sharding import PartitionSpec as P

PRE = 2
POST = 2
COARSE = 4


PERMEABILITY = (1.0, 0.1, 0.6, 0.8, 0.25)
OMEGA = 2.0 / 3.0


def padded_2(cells, sides, width):
    for axis, dim in sides:
        count = lax.axis_size(axis)
        ends = count - 1
        head = lax.slice_in_dim(cells, 0, width, axis=dim)
        tail = lax.slice_in_dim(cells, cells.shape[dim] - width, cells.shape[dim], axis=dim)
        cells = jnp.concatenate(
            [
                lax.ppermute(tail, axis, [(i, (i + 1) % count) for i in range(ends)]),
                cells,
                lax.ppermute(head, axis, [((i + 1) % count, i) for i in range(ends)]),
            ],
            axis=dim,
        )
    return cells


def conduct(zones, density):
    perm = jnp.zeros(density.shape, jnp.float32)
    for zone_id, value in enumerate(PERMEABILITY):
        perm = perm + jnp.where(zones == zone_id, jnp.float32(value), jnp.float32(0.0))
    return perm / density


def harmonic(first, second):
    return 2.0 * first * second / (first + second)


def neighbours(padded):
    return [
        padded[:-2, 1:-1, 1:-1],
        padded[2:, 1:-1, 1:-1],
        padded[1:-1, :-2, 1:-1],
        padded[1:-1, 2:, 1:-1],
        padded[1:-1, 1:-1, :-2],
        padded[1:-1, 1:-1, 2:],
    ]


def setup(cond, padder):
    padded = padder(cond - 1.0) + 1.0
    coeffs = [harmonic(cond, other) for other in neighbours(padded)]
    diag = coeffs[0] + coeffs[1] + coeffs[2] + coeffs[3] + coeffs[4] + coeffs[5]
    return (coeffs, diag)


def stencil(field, coeffs, padder):
    others = neighbours(padder(field))
    total = coeffs[0] * (field - others[0])
    for index in range(1, 6):
        total = total + coeffs[index] * (field - others[index])
    return total


def smooth(field, source, coeffs, diag, padder, count):
    for sweep in range(count):
        field = field + OMEGA * (source - stencil(field, coeffs, padder)) / diag
    return field


def block_sum(field):
    depth, across, along = field.shape
    return field.reshape(depth // 2, 2, across // 2, 2, along // 2, 2).sum(axis=(1, 3, 5))


def prolong(field):
    depth, across, along = field.shape
    wide = jnp.broadcast_to(field[:, None, :, None, :, None], (depth, 2, across, 2, along, 2))
    return wide.reshape(depth * 2, across * 2, along * 2)


def pad_spread(field):
    framed = padded_2(field, (("height", 0), ("plan", 1)), 1)
    return jnp.pad(framed, ((0, 0), (0, 0), (1, 1)))


def pad_column(field):
    framed = padded_2(field, (("height", 0),), 1)
    return jnp.pad(framed, ((0, 0), (1, 1), (1, 1)))


def agglomerate(source, cond):
    return (
        lax.all_gather(source, "plan", axis=1, tiled=True),
        lax.all_gather(cond, "plan", axis=1, tiled=True),
    )


def own_tile(field, width):
    return lax.dynamic_slice_in_dim(field, lax.axis_index("plan") * width, width, 1)


def coarsest(f2, cond2):
    coeffs2, diag2 = setup(cond2, pad_column)
    p2 = OMEGA * f2 / diag2
    p2 = smooth(p2, f2, coeffs2, diag2, pad_column, COARSE - 1)
    leftover = f2 - stencil(p2, coeffs2, pad_column)
    line = jnp.sum(leftover, axis=1, keepdims=True) / jnp.sum(diag2, axis=1, keepdims=True)
    return p2 + line


def on_device(divergence, density, zones):
    cond0 = conduct(zones, density)
    coeffs0, diag0 = setup(cond0, pad_spread)
    p0 = OMEGA * divergence / diag0
    p0 = smooth(p0, divergence, coeffs0, diag0, pad_spread, PRE - 1)
    f1 = 0.5 * block_sum(divergence - stencil(p0, coeffs0, pad_spread))
    cond1 = 0.125 * block_sum(cond0)
    coeffs1, diag1 = setup(cond1, pad_spread)
    p1 = OMEGA * f1 / diag1
    p1 = smooth(p1, f1, coeffs1, diag1, pad_spread, PRE - 1)
    f2 = 0.5 * block_sum(f1 - stencil(p1, coeffs1, pad_spread))
    cond2 = 0.125 * block_sum(cond1)
    width2 = f2.shape[1]
    f2, cond2 = agglomerate(f2, cond2)
    p2 = own_tile(coarsest(f2, cond2), width2)
    p1 = smooth(p1 + prolong(p2), f1, coeffs1, diag1, pad_spread, POST)
    return smooth(p0 + prolong(p1), divergence, coeffs0, diag0, pad_spread, POST)


def solution(mesh):
    return jax.shard_map(
        on_device,
        mesh=mesh,
        in_specs=(P("height", "plan", None), P("height", "plan", None), P("height", "plan", None)),
        out_specs=P("height", "plan", None),
        check_vma=False,
    )
```

profile of v0, /device:TPU:31, one launch (start us, length us, event | category | flops | bytes accessed | tf_op | source)
XLA Modules:
  0.0 331.1 jit_solution(12853921377574772214)
XLA Ops:
  1.1 4.9 %collective-permute-start = (f32[1,16,512]{2,1,0:T(8,128)S(1)}, f32[1,16,512]{2,1,0:T(8,128)S(1)}, u32[]{:S(2)}, u32[]{:S(2)}) collective-permute-start(f32[1,16,512]{2,1,0:T(8,128)S(1)} %get-tuple-element.48), channel_id=1, source_target_pairs={{0,12},{12,24},{24,36},{36,48},{48,60},{60,72},{72,84},{84,96},{96... | collective-permute-start | bytes 98312 | tf_op jit(solution)/shard_map/ppermute | solution.py:23
  7.9 6.6 %collective-permute-done.1 = f32[1,16,512]{2,1,0:T(8,128)S(1)} collective-permute-done((f32[1,16,512]{2,1,0:T(8,128)S(1)}, f32[1,16,512]{2,1,0:T(8,128)S(1)}, u32[]{:S(2)}, u32[]{:S(2)}) %collective-permute-start.1) | collective-permute-done | bytes 32800 | tf_op jit(solution)/shard_map/ppermute | solution.py:25
  14.5 4.0 %collective-permute-start.2 = (f32[6,1,512]{2,1,0:T(1,128)S(1)}, f32[6,1,512]{2,1,0:T(1,128)S(1)}, u32[]{:S(2)}, u32[]{:S(2)}) collective-permute-start(f32[6,1,512]{2,1,0:T(1,128)S(1)} %get-tuple-element.38), channel_id=1, source_target_pairs={{0,1},{1,2},{2,3},{3,4},{4,5},{5,6},{6,7},{7,8},{8,9},{9,10},{10,1... | collective-permute-start | bytes 36872 | tf_op jit(solution)/shard_map/ppermute | solution.py:23
  19.9 9.8 %reshape.57 = f32[2,2,8,2,256,2]{5,4,3,2,1,0:T(8,128)} reshape(f32[4,16,512]{2,1,0:T(8,128)S(1)} %get-tuple-element.29) | data formatting | bytes 262144 | tf_op jit(solution)/shard_map/reshape | solution.py:77
  29.7 4.0 %reduce_sum.69 = f32[2,8,256]{2,1,0:T(8,128)S(1)} reduce(f32[2,2,8,2,256,2]{5,4,3,2,1,0:T(8,128)} %reshape.57, f32[]{:T(128)} %constant.22.clone.1), dimensions={1,3,5}, to_apply=%region_1.2 | reduce | flops 28672 | bytes 147460 | tf_op jit(solution)/shard_map/reduce_sum | solution.py:77
  34.2 2.2 collective-permute-start.4
  38.6 6.4 %collective-permute-done.5 = f32[1,16,512]{2,1,0:T(8,128)S(1)} collective-permute-done((f32[1,16,512]{2,1,0:T(8,128)S(1)}, f32[1,16,512]{2,1,0:T(8,128)S(1)}, u32[]{:S(2)}, u32[]{:S(2)}) %collective-permute-start.5) | collective-permute-done | bytes 32800 | tf_op jit(solution)/shard_map/ppermute | solution.py:25
  45.0 4.6 %collective-permute-start.6 = (f32[6,1,512]{2,1,0:T(1,128)S(1)}, f32[6,1,512]{2,1,0:T(1,128)S(1)}, u32[]{:S(2)}, u32[]{:S(2)}) collective-permute-start(f32[6,1,512]{2,1,0:T(1,128)S(1)} %get-tuple-element.36), channel_id=1, source_target_pairs={{0,1},{1,2},{2,3},{3,4},{4,5},{5,6},{6,7},{7,8},{8,9},{9,10},{10,1... | collective-permute-start | bytes 36872 | tf_op jit(solution)/shard_map/ppermute | solution.py:23
  51.0 2.2 collective-permute-start.12
  55.8 6.7 %collective-permute-start.8 = (f32[1,16,512]{2,1,0:T(8,128)S(1)}, f32[1,16,512]{2,1,0:T(8,128)S(1)}, u32[]{:S(2)}, u32[]{:S(2)}) collective-permute-start(f32[1,16,512]{2,1,0:T(8,128)S(1)} %get-tuple-element.44), channel_id=1, source_target_pairs={{0,12},{12,24},{24,36},{36,48},{48,60},{60,72},{72,84},{84,96},{96... | collective-permute-start | bytes 98312 | tf_op jit(solution)/shard_map/ppermute | solution.py:23
  64.5 4.6 %collective-permute-start.14 = (f32[4,1,256]{2,1,0:T(1,128)S(1)}, f32[4,1,256]{2,1,0:T(1,128)S(1)}, u32[]{:S(2)}, u32[]{:S(2)}) collective-permute-start(f32[4,1,256]{2,1,0:T(1,128)S(1)} %get-tuple-element.58), channel_id=1, source_target_pairs={{0,1},{1,2},{2,3},{3,4},{4,5},{5,6},{6,7},{7,8},{8,9},{9,10},{10,1... | collective-permute-start | bytes 12296 | tf_op jit(solution)/shard_map/ppermute | solution.py:23
  71.1 5.2 %collective-permute-start.10 = (f32[6,1,512]{2,1,0:T(1,128)S(1)}, f32[6,1,512]{2,1,0:T(1,128)S(1)}, u32[]{:S(2)}, u32[]{:S(2)}) collective-permute-start(f32[6,1,512]{2,1,0:T(1,128)S(1)} %get-tuple-element.34), channel_id=1, source_target_pairs={{0,1},{1,2},{2,3},{3,4},{4,5},{5,6},{6,7},{7,8},{8,9},{9,10},{10,1... | collective-permute-start | bytes 36872 | tf_op jit(solution)/shard_map/ppermute | solution.py:23
  77.8 4.5 %collective-permute-done.11 = f32[6,1,512]{2,1,0:T(1,128)S(1)} collective-permute-done((f32[6,1,512]{2,1,0:T(1,128)S(1)}, f32[6,1,512]{2,1,0:T(1,128)S(1)}, u32[]{:S(2)}, u32[]{:S(2)}) %collective-permute-start.11) | collective-permute-done | bytes 12320 | tf_op jit(solution)/shard_map/ppermute | solution.py:25
  82.6 9.8 %reshape.56 = f32[2,2,8,2,256,2]{5,4,3,2,1,0:T(8,128)} reshape(f32[4,16,512]{2,1,0:T(8,128)S(1)} %fusion.46) | data formatting | bytes 262144 | tf_op jit(solution)/shard_map/reshape | solution.py:77
  92.4 4.0 %reduce_sum.68 = f32[2,8,256]{2,1,0:T(8,128)S(1)} reduce(f32[2,2,8,2,256,2]{5,4,3,2,1,0:T(8,128)} %reshape.56, f32[]{:T(128)} %constant.22.clone.1), dimensions={1,3,5}, to_apply=%region_0.1 | reduce | flops 28672 | bytes 147460 | tf_op jit(solution)/shard_map/reduce_sum | solution.py:77
  96.6 8.4 %collective-permute-start.16 = (f32[1,8,256]{2,1,0:T(8,128)S(1)}, f32[1,8,256]{2,1,0:T(8,128)S(1)}, u32[]{:S(2)}, u32[]{:S(2)}) collective-permute-start(f32[1,8,256]{2,1,0:T(8,128)S(1)} %get-tuple-element.67), channel_id=1, source_target_pairs={{0,12},{12,24},{24,36},{36,48},{48,60},{60,72},{72,84},{84,96},{96... | collective-permute-start | bytes 24584 | tf_op jit(solution)/shard_map/ppermute | solution.py:23
  107.6 5.7 %collective-permute-done.17 = f32[1,8,256]{2,1,0:T(8,128)S(1)} collective-permute-done((f32[1,8,256]{2,1,0:T(8,128)S(1)}, f32[1,8,256]{2,1,0:T(8,128)S(1)}, u32[]{:S(2)}, u32[]{:S(2)}) %collective-permute-start.17) | collective-permute-done | bytes 8224 | tf_op jit(solution)/shard_map/ppermute | solution.py:25
  113.3 4.8 %collective-permute-start.18 = (f32[4,1,256]{2,1,0:T(1,128)S(1)}, f32[4,1,256]{2,1,0:T(1,128)S(1)}, u32[]{:S(2)}, u32[]{:S(2)}) collective-permute-start(f32[4,1,256]{2,1,0:T(1,128)S(1)} %get-tuple-element.56), channel_id=1, source_target_pairs={{0,1},{1,2},{2,3},{3,4},{4,5},{5,6},{6,7},{7,8},{8,9},{9,10},{10,1... | collective-permute-start | bytes 12296 | tf_op jit(solution)/shard_map/ppermute | solution.py:23
  119.4 23.9 %all-gather.3 = f32[12,4,128]{2,1,0:T(4,128)S(1)} all-gather(f32[1,4,128]{2,1,0:T(4,128)S(1)} %multiply_bitcast_fusion), channel_id=3, replica_groups=mesh['height'=64,'plan'=12] {'plan'}, dimensions={0}, use_global_device_ids=true | all-gather | bytes 26624 | tf_op jit(solution)/shard_map/all_gather | solution.py:99
  143.5 7.5 %collective-permute-start.20 = (f32[1,8,256]{2,1,0:T(8,128)S(1)}, f32[1,8,256]{2,1,0:T(8,128)S(1)}, u32[]{:S(2)}, u32[]{:S(2)}) collective-permute-start(f32[1,8,256]{2,1,0:T(8,128)S(1)} %get-tuple-element.65), channel_id=1, source_target_pairs={{0,12},{12,24},{24,36},{36,48},{48,60},{60,72},{72,84},{84,96},{96... | collective-permute-start | bytes 24584 | tf_op jit(solution)/shard_map/ppermute | solution.py:23
  153.0 7.0 %collective-permute-start.24 = (f32[1,48,128]{2,1,0:T(8,128)S(1)}, f32[1,48,128]{2,1,0:T(8,128)S(1)}, u32[]{:S(2)}, u32[]{:S(2)}) collective-permute-start(f32[1,48,128]{2,1,0:T(8,128)S(1)} %bitcast_add_fusion.6), channel_id=1, source_target_pairs={{0,12},{12,24},{24,36},{36,48},{48,60},{60,72},{72,84},{84,96},{96... | collective-permute-start | bytes 73736 | tf_op jit(solution)/shard_map/ppermute | solution.py:23
  164.9 3.5 %collective-permute-done.25 = f32[1,48,128]{2,1,0:T(8,128)S(1)} collective-permute-done((f32[1,48,128]{2,1,0:T(8,128)S(1)}, f32[1,48,128]{2,1,0:T(8,128)S(1)}, u32[]{:S(2)}, u32[]{:S(2)}) %collective-permute-start.25) | collective-permute-done | bytes 24608 | tf_op jit(solution)/shard_map/ppermute | solution.py:25
  169.5 18.5 %all-gather.2 = f32[12,4,128]{2,1,0:T(4,128)S(1)} all-gather(f32[1,4,128]{2,1,0:T(4,128)S(1)} %multiply_bitcast_fusion.1), channel_id=2, replica_groups=mesh['height'=64,'plan'=12] {'plan'}, dimensions={0}, use_global_device_ids=true | all-gather | bytes 26624 | tf_op jit(solution)/shard_map/all_gather | solution.py:98
  188.1 13.3 %collective-permute-start.26 = (f32[1,48,128]{2,1,0:T(8,128)S(1)}, f32[1,48,128]{2,1,0:T(8,128)S(1)}, u32[]{:S(2)}, u32[]{:S(2)}) collective-permute-start(f32[1,48,128]{2,1,0:T(8,128)S(1)} %get-tuple-element.7), channel_id=1, source_target_pairs={{0,12},{12,24},{24,36},{36,48},{48,60},{60,72},{72,84},{84,96},{96... | collective-permute-start | bytes 73736 | tf_op jit(solution)/shard_map/ppermute | solution.py:23
  203.4 6.5 %collective-permute-done.27 = f32[1,48,128]{2,1,0:T(8,128)S(1)} collective-permute-done((f32[1,48,128]{2,1,0:T(8,128)S(1)}, f32[1,48,128]{2,1,0:T(8,128)S(1)}, u32[]{:S(2)}, u32[]{:S(2)}) %collective-permute-start.27) | collective-permute-done | bytes 24608 | tf_op jit(solution)/shard_map/ppermute | solution.py:25
  212.1 2.4 collective-permute-start.29
  214.5 6.0 %collective-permute-done.29 = f32[1,48,128]{2,1,0:T(8,128)S(1)} collective-permute-done((f32[1,48,128]{2,1,0:T(8,128)S(1)}, f32[1,48,128]{2,1,0:T(8,128)S(1)}, u32[]{:S(2)}, u32[]{:S(2)}) %collective-permute-start.29) | collective-permute-done | bytes 24608 | tf_op jit(solution)/shard_map/ppermute | solution.py:25
  222.7 2.4 collective-permute-start.31
  225.2 6.0 %collective-permute-done.31 = f32[1,48,128]{2,1,0:T(8,128)S(1)} collective-permute-done((f32[1,48,128]{2,1,0:T(8,128)S(1)}, f32[1,48,128]{2,1,0:T(8,128)S(1)}, u32[]{:S(2)}, u32[]{:S(2)}) %collective-permute-start.31) | collective-permute-done | bytes 24608 | tf_op jit(solution)/shard_map/ppermute | solution.py:25
  233.3 2.4 collective-permute-start.33
  235.8 6.0 %collective-permute-done.33 = f32[1,48,128]{2,1,0:T(8,128)S(1)} collective-permute-done((f32[1,48,128]{2,1,0:T(8,128)S(1)}, f32[1,48,128]{2,1,0:T(8,128)S(1)}, u32[]{:S(2)}, u32[]{:S(2)}) %collective-permute-start.33) | collective-permute-done | bytes 24608 | tf_op jit(solution)/shard_map/ppermute | solution.py:25
  244.4 2.4 collective-permute-start.35
  246.9 5.9 %collective-permute-done.35 = f32[1,8,256]{2,1,0:T(8,128)S(1)} collective-permute-done((f32[1,8,256]{2,1,0:T(8,128)S(1)}, f32[1,8,256]{2,1,0:T(8,128)S(1)}, u32[]{:S(2)}, u32[]{:S(2)}) %collective-permute-start.35) | collective-permute-done | bytes 8224 | tf_op jit(solution)/shard_map/ppermute | solution.py:25
  255.3 3.0 collective-permute-done.37
  258.6 3.1 collective-permute-start.38
  263.6 6.4 %collective-permute-done.39 = f32[1,8,256]{2,1,0:T(8,128)S(1)} collective-permute-done((f32[1,8,256]{2,1,0:T(8,128)S(1)}, f32[1,8,256]{2,1,0:T(8,128)S(1)}, u32[]{:S(2)}, u32[]{:S(2)}) %collective-permute-start.39) | collective-permute-done | bytes 8224 | tf_op jit(solution)/shard_map/ppermute | solution.py:25
  270.0 3.1 collective-permute-start.40
  274.5 3.0 collective-permute-done.41
  277.7 3.9 %broadcast_in_dim.54 = f32[2,2,8,2,256,2]{5,4,3,2,1,0:T(8,128)} broadcast(f32[2,8,256]{2,1,0:T(8,128)S(1)} %fusion.140), dimensions={0,2,4} | broadcast | bytes 147456 | tf_op jit(solution)/shard_map/broadcast_in_dim | solution.py:82
  281.6 6.9 %reshape.58 = f32[4,16,512]{2,1,0:T(8,128)S(1)} reshape(f32[2,2,8,2,256,2]{5,4,3,2,1,0:T(8,128)} %broadcast_in_dim.54) | data formatting | bytes 262144 | tf_op jit(solution)/shard_map/reshape | solution.py:83
  288.6 3.3 collective-permute-start.42
  293.8 6.6 %collective-permute-done.43 = f32[1,16,512]{2,1,0:T(8,128)S(1)} collective-permute-done((f32[1,16,512]{2,1,0:T(8,128)S(1)}, f32[1,16,512]{2,1,0:T(8,128)S(1)}, u32[]{:S(2)}, u32[]{:S(2)}) %collective-permute-start.43) | collective-permute-done | bytes 32800 | tf_op jit(solution)/shard_map/ppermute | solution.py:25
  300.4 4.7 %collective-permute-start.44 = (f32[6,1,512]{2,1,0:T(1,128)S(1)}, f32[6,1,512]{2,1,0:T(1,128)S(1)}, u32[]{:S(2)}, u32[]{:S(2)}) collective-permute-start(f32[6,1,512]{2,1,0:T(1,128)S(1)} %get-tuple-element.32), channel_id=1, source_target_pairs={{0,1},{1,2},{2,3},{3,4},{4,5},{5,6},{6,7},{7,8},{8,9},{9,10},{10,1... | collective-permute-start | bytes 36872 | tf_op jit(solution)/shard_map/ppermute | solution.py:23
  306.4 3.4 %collective-permute-done.45 = f32[6,1,512]{2,1,0:T(1,128)S(1)} collective-permute-done((f32[6,1,512]{2,1,0:T(1,128)S(1)}, f32[6,1,512]{2,1,0:T(1,128)S(1)}, u32[]{:S(2)}, u32[]{:S(2)}) %collective-permute-start.45) | collective-permute-done | bytes 12320 | tf_op jit(solution)/shard_map/ppermute | solution.py:25
  310.3 3.1 collective-permute-start.46
  315.3 6.6 %collective-permute-done.47 = f32[1,16,512]{2,1,0:T(8,128)S(1)} collective-permute-done((f32[1,16,512]{2,1,0:T(8,128)S(1)}, f32[1,16,512]{2,1,0:T(8,128)S(1)}, u32[]{:S(2)}, u32[]{:S(2)}) %collective-permute-start.47) | collective-permute-done | bytes 32800 | tf_op jit(solution)/shard_map/ppermute | solution.py:25
  321.9 3.6 %collective-permute-start.48 = (f32[6,1,512]{2,1,0:T(1,128)S(1)}, f32[6,1,512]{2,1,0:T(1,128)S(1)}, u32[]{:S(2)}, u32[]{:S(2)}) collective-permute-start(f32[6,1,512]{2,1,0:T(1,128)S(1)} %get-tuple-element.30), channel_id=1, source_target_pairs={{0,1},{1,2},{2,3},{3,4},{4,5},{5,6},{6,7},{7,8},{8,9},{9,10},{10,1... | collective-permute-start | bytes 36872 | tf_op jit(solution)/shard_map/ppermute | solution.py:23
  326.9 3.1 collective-permute-done.49
  (127 shorter events, 53.8 us)
Async XLA Ops:
  1.1 6.8 %collective-permute-start = (f32[1,16,512]{2,1,0:T(8,128)S(1)}, f32[1,16,512]{2,1,0:T(8,128)S(1)}, u32[]{:S(2)}, u32[]{:S(2)}) collective-permute-start(f32[1,16,512]{2,1,0:T(8,128)S(1)} %get-tuple-element.48), channel_id=1, source_target_pairs={{0,12},{12,24},{24,36},{36,48},{48,60},{60,72},{72,84},{84,96},{96... | collective-permute-start | bytes 98312 | tf_op jit(solution)/shard_map/ppermute | solution.py:23
  6.0 8.6 %collective-permute-start.1 = (f32[1,16,512]{2,1,0:T(8,128)S(1)}, f32[1,16,512]{2,1,0:T(8,128)S(1)}, u32[]{:S(2)}, u32[]{:S(2)}) collective-permute-start(f32[1,16,512]{2,1,0:T(8,128)S(1)} %get-tuple-element.49), channel_id=1, source_target_pairs={{12,0},{24,12},{36,24},{48,36},{60,48},{72,60},{84,72},{96,84},{10... | collective-permute-start | bytes 98312 | tf_op jit(solution)/shard_map/ppermute | solution.py:25
  14.5 19.1 %collective-permute-start.2 = (f32[6,1,512]{2,1,0:T(1,128)S(1)}, f32[6,1,512]{2,1,0:T(1,128)S(1)}, u32[]{:S(2)}, u32[]{:S(2)}) collective-permute-start(f32[6,1,512]{2,1,0:T(1,128)S(1)} %get-tuple-element.38), channel_id=1, source_target_pairs={{0,1},{1,2},{2,3},{3,4},{4,5},{5,6},{6,7},{7,8},{8,9},{9,10},{10,1... | collective-permute-start | bytes 36872 | tf_op jit(solution)/shard_map/ppermute | solution.py:23
  18.5 15.1 %collective-permute-start.3 = (f32[6,1,512]{2,1,0:T(1,128)S(1)}, f32[6,1,512]{2,1,0:T(1,128)S(1)}, u32[]{:S(2)}, u32[]{:S(2)}) collective-permute-start(f32[6,1,512]{2,1,0:T(1,128)S(1)} %get-tuple-element.39), channel_id=1, source_target_pairs={{1,0},{2,1},{3,2},{4,3},{5,4},{6,5},{7,6},{8,7},{9,8},{10,9},{11,1... | collective-permute-start | bytes 36872 | tf_op jit(solution)/shard_map/ppermute | solution.py:25
  34.2 4.4 %collective-permute-start.4 = (f32[1,16,512]{2,1,0:T(8,128)S(1)}, f32[1,16,512]{2,1,0:T(8,128)S(1)}, u32[]{:S(2)}, u32[]{:S(2)}) collective-permute-start(f32[1,16,512]{2,1,0:T(8,128)S(1)} %get-tuple-element.46), channel_id=1, source_target_pairs={{0,12},{12,24},{24,36},{36,48},{48,60},{60,72},{72,84},{84,96},{96... | collective-permute-start | bytes 98312 | tf_op jit(solution)/shard_map/ppermute | solution.py:23
  36.4 8.6 %collective-permute-start.5 = (f32[1,16,512]{2,1,0:T(8,128)S(1)}, f32[1,16,512]{2,1,0:T(8,128)S(1)}, u32[]{:S(2)}, u32[]{:S(2)}) collective-permute-start(f32[1,16,512]{2,1,0:T(8,128)S(1)} %get-tuple-element.47), channel_id=1, source_target_pairs={{12,0},{24,12},{36,24},{48,36},{60,48},{72,60},{84,72},{96,84},{10... | collective-permute-start | bytes 98312 | tf_op jit(solution)/shard_map/ppermute | solution.py:25
  45.0 10.3 %collective-permute-start.6 = (f32[6,1,512]{2,1,0:T(1,128)S(1)}, f32[6,1,512]{2,1,0:T(1,128)S(1)}, u32[]{:S(2)}, u32[]{:S(2)}) collective-permute-start(f32[6,1,512]{2,1,0:T(1,128)S(1)} %get-tuple-element.36), channel_id=1, source_target_pairs={{0,1},{1,2},{2,3},{3,4},{4,5},{5,6},{6,7},{7,8},{8,9},{9,10},{10,1... | collective-permute-start | bytes 36872 | tf_op jit(solution)/shard_map/ppermute | solution.py:23
  49.7 5.7 %collective-permute-start.7 = (f32[6,1,512]{2,1,0:T(1,128)S(1)}, f32[6,1,512]{2,1,0:T(1,128)S(1)}, u32[]{:S(2)}, u32[]{:S(2)}) collective-permute-start(f32[6,1,512]{2,1,0:T(1,128)S(1)} %get-tuple-element.37), channel_id=1, source_target_pairs={{1,0},{2,1},{3,2},{4,3},{5,4},{6,5},{7,6},{8,7},{9,8},{10,9},{11,1... | collective-permute-start | bytes 36872 | tf_op jit(solution)/shard_map/ppermute | solution.py:25
  51.0 13.5 %collective-permute-start.12 = (f32[1,8,256]{2,1,0:T(8,128)S(1)}, f32[1,8,256]{2,1,0:T(8,128)S(1)}, u32[]{:S(2)}, u32[]{:S(2)}) collective-permute-start(f32[1,8,256]{2,1,0:T(8,128)S(1)} %get-tuple-element.69), channel_id=1, source_target_pairs={{0,12},{12,24},{24,36},{36,48},{48,60},{60,72},{72,84},{84,96},{96... | collective-permute-start | bytes 24584 | tf_op jit(solution)/shard_map/ppermute | solution.py:23
  53.2 11.3 %collective-permute-start.13 = (f32[1,8,256]{2,1,0:T(8,128)S(1)}, f32[1,8,256]{2,1,0:T(8,128)S(1)}, u32[]{:S(2)}, u32[]{:S(2)}) collective-permute-start(f32[1,8,256]{2,1,0:T(8,128)S(1)} %get-tuple-element.70), channel_id=1, source_target_pairs={{12,0},{24,12},{36,24},{48,36},{60,48},{72,60},{84,72},{96,84},{10... | collective-permute-start | bytes 24584 | tf_op jit(solution)/shard_map/ppermute | solution.py:25
  55.8 14.7 %collective-permute-start.8 = (f32[1,16,512]{2,1,0:T(8,128)S(1)}, f32[1,16,512]{2,1,0:T(8,128)S(1)}, u32[]{:S(2)}, u32[]{:S(2)}) collective-permute-start(f32[1,16,512]{2,1,0:T(8,128)S(1)} %get-tuple-element.44), channel_id=1, source_target_pairs={{0,12},{12,24},{24,36},{36,48},{48,60},{60,72},{72,84},{84,96},{96... | collective-permute-start | bytes 98312 | tf_op jit(solution)/shard_map/ppermute | solution.py:23
  62.5 8.6 %collective-permute-start.9 = (f32[1,16,512]{2,1,0:T(8,128)S(1)}, f32[1,16,512]{2,1,0:T(8,128)S(1)}, u32[]{:S(2)}, u32[]{:S(2)}) collective-permute-start(f32[1,16,512]{2,1,0:T(8,128)S(1)} %get-tuple-element.45), channel_id=1, source_target_pairs={{12,0},{24,12},{36,24},{48,36},{60,48},{72,60},{84,72},{96,84},{10... | collective-permute-start | bytes 98312 | tf_op jit(solution)/shard_map/ppermute | solution.py:25
  64.5 13.1 %collective-permute-start.14 = (f32[4,1,256]{2,1,0:T(1,128)S(1)}, f32[4,1,256]{2,1,0:T(1,128)S(1)}, u32[]{:S(2)}, u32[]{:S(2)}) collective-permute-start(f32[4,1,256]{2,1,0:T(1,128)S(1)} %get-tuple-element.58), channel_id=1, source_target_pairs={{0,1},{1,2},{2,3},{3,4},{4,5},{5,6},{6,7},{7,8},{8,9},{9,10},{10,1... | collective-permute-start | bytes 12296 | tf_op jit(solution)/shard_map/ppermute | solution.py:23
  69.1 8.5 %collective-permute-start.15 = (f32[4,1,256]{2,1,0:T(1,128)S(1)}, f32[4,1,256]{2,1,0:T(1,128)S(1)}, u32[]{:S(2)}, u32[]{:S(2)}) collective-permute-start(f32[4,1,256]{2,1,0:T(1,128)S(1)} %get-tuple-element.59), channel_id=1, source_target_pairs={{1,0},{2,1},{3,2},{4,3},{5,4},{6,5},{7,6},{8,7},{9,8},{10,9},{11,1... | collective-permute-start | bytes 12296 | tf_op jit(solution)/shard_map/ppermute | solution.py:25
  71.1 6.7 %collective-permute-start.10 = (f32[6,1,512]{2,1,0:T(1,128)S(1)}, f32[6,1,512]{2,1,0:T(1,128)S(1)}, u32[]{:S(2)}, u32[]{:S(2)}) collective-permute-start(f32[6,1,512]{2,1,0:T(1,128)S(1)} %get-tuple-element.34), channel_id=1, source_target_pairs={{0,1},{1,2},{2,3},{3,4},{4,5},{5,6},{6,7},{7,8},{8,9},{9,10},{10,1... | collective-permute-start | bytes 36872 | tf_op jit(solution)/shard_map/ppermute | solution.py:23
  76.3 5.9 %collective-permute-start.11 = (f32[6,1,512]{2,1,0:T(1,128)S(1)}, f32[6,1,512]{2,1,0:T(1,128)S(1)}, u32[]{:S(2)}, u32[]{:S(2)}) collective-permute-start(f32[6,1,512]{2,1,0:T(1,128)S(1)} %get-tuple-element.35), channel_id=1, source_target_pairs={{1,0},{2,1},{3,2},{4,3},{5,4},{6,5},{7,6},{8,7},{9,8},{10,9},{11,1... | collective-permute-start | bytes 36872 | tf_op jit(solution)/shard_map/ppermute | solution.py:25
  96.6 11.0 %collective-permute-start.16 = (f32[1,8,256]{2,1,0:T(8,128)S(1)}, f32[1,8,256]{2,1,0:T(8,128)S(1)}, u32[]{:S(2)}, u32[]{:S(2)}) collective-permute-start(f32[1,8,256]{2,1,0:T(8,128)S(1)} %get-tuple-element.67), channel_id=1, source_target_pairs={{0,12},{12,24},{24,36},{36,48},{48,60},{60,72},{72,84},{84,96},{96... | collective-permute-start | bytes 24584 | tf_op jit(solution)/shard_map/ppermute | solution.py:23
  105.0 8.3 %collective-permute-start.17 = (f32[1,8,256]{2,1,0:T(8,128)S(1)}, f32[1,8,256]{2,1,0:T(8,128)S(1)}, u32[]{:S(2)}, u32[]{:S(2)}) collective-permute-start(f32[1,8,256]{2,1,0:T(8,128)S(1)} %get-tuple-element.68), channel_id=1, source_target_pairs={{12,0},{24,12},{36,24},{48,36},{60,48},{72,60},{84,72},{96,84},{10... | collective-permute-start | bytes 24584 | tf_op jit(solution)/shard_map/ppermute | solution.py:25
  113.3 30.0 %collective-permute-start.18 = (f32[4,1,256]{2,1,0:T(1,128)S(1)}, f32[4,1,256]{2,1,0:T(1,128)S(1)}, u32[]{:S(2)}, u32[]{:S(2)}) collective-permute-start(f32[4,1,256]{2,1,0:T(1,128)S(1)} %get-tuple-element.56), channel_id=1, source_target_pairs={{0,1},{1,2},{2,3},{3,4},{4,5},{5,6},{6,7},{7,8},{8,9},{9,10},{10,1... | collective-permute-start | bytes 12296 | tf_op jit(solution)/shard_map/ppermute | solution.py:23
  118.1 25.2 %collective-permute-start.19 = (f32[4,1,256]{2,1,0:T(1,128)S(1)}, f32[4,1,256]{2,1,0:T(1,128)S(1)}, u32[]{:S(2)}, u32[]{:S(2)}) collective-permute-start(f32[4,1,256]{2,1,0:T(1,128)S(1)} %get-tuple-element.57), channel_id=1, source_target_pairs={{1,0},{2,1},{3,2},{4,3},{5,4},{6,5},{7,6},{8,7},{9,8},{10,9},{11,1... | collective-permute-start | bytes 12296 | tf_op jit(solution)/shard_map/ppermute | solution.py:25
  143.5 18.4 %collective-permute-start.20 = (f32[1,8,256]{2,1,0:T(8,128)S(1)}, f32[1,8,256]{2,1,0:T(8,128)S(1)}, u32[]{:S(2)}, u32[]{:S(2)}) collective-permute-start(f32[1,8,256]{2,1,0:T(8,128)S(1)} %get-tuple-element.65), channel_id=1, source_target_pairs={{0,12},{12,24},{24,36},{36,48},{48,60},{60,72},{72,84},{84,96},{96... | collective-permute-start | bytes 24584 | tf_op jit(solution)/shard_map/ppermute | solution.py:23
  151.1 10.9 %collective-permute-start.21 = (f32[1,8,256]{2,1,0:T(8,128)S(1)}, f32[1,8,256]{2,1,0:T(8,128)S(1)}, u32[]{:S(2)}, u32[]{:S(2)}) collective-permute-start(f32[1,8,256]{2,1,0:T(8,128)S(1)} %get-tuple-element.66), channel_id=1, source_target_pairs={{12,0},{24,12},{36,24},{48,36},{60,48},{72,60},{84,72},{96,84},{10... | collective-permute-start | bytes 24584 | tf_op jit(solution)/shard_map/ppermute | solution.py:25
  153.0 11.9 %collective-permute-start.24 = (f32[1,48,128]{2,1,0:T(8,128)S(1)}, f32[1,48,128]{2,1,0:T(8,128)S(1)}, u32[]{:S(2)}, u32[]{:S(2)}) collective-permute-start(f32[1,48,128]{2,1,0:T(8,128)S(1)} %bitcast_add_fusion.6), channel_id=1, source_target_pairs={{0,12},{12,24},{24,36},{36,48},{48,60},{60,72},{72,84},{84,96},{96... | collective-permute-start | bytes 73736 | tf_op jit(solution)/shard_map/ppermute | solution.py:23
  160.0 8.5 %collective-permute-start.25 = (f32[1,48,128]{2,1,0:T(8,128)S(1)}, f32[1,48,128]{2,1,0:T(8,128)S(1)}, u32[]{:S(2)}, u32[]{:S(2)}) collective-permute-start(f32[1,48,128]{2,1,0:T(8,128)S(1)} %bitcast_add_fusion.6), channel_id=1, source_target_pairs={{12,0},{24,12},{36,24},{48,36},{60,48},{72,60},{84,72},{96,84},{10... | collective-permute-start | bytes 73736 | tf_op jit(solution)/shard_map/ppermute | solution.py:25
  162.0 6.6 %collective-permute-start.22 = (f32[4,1,256]{2,1,0:T(1,128)S(1)}, f32[4,1,256]{2,1,0:T(1,128)S(1)}, u32[]{:S(2)}, u32[]{:S(2)}) collective-permute-start(f32[4,1,256]{2,1,0:T(1,128)S(1)} %get-tuple-element.54), channel_id=1, source_target_pairs={{0,1},{1,2},{2,3},{3,4},{4,5},{5,6},{6,7},{7,8},{8,9},{9,10},{10,1... | collective-permute-start | bytes 12296 | tf_op jit(solution)/shard_map/ppermute | solution.py:23
  163.6 5.0 %collective-permute-start.23 = (f32[4,1,256]{2,1,0:T(1,128)S(1)}, f32[4,1,256]{2,1,0:T(1,128)S(1)}, u32[]{:S(2)}, u32[]{:S(2)}) collective-permute-start(f32[4,1,256]{2,1,0:T(1,128)S(1)} %get-tuple-element.55), channel_id=1, source_target_pairs={{1,0},{2,1},{3,2},{4,3},{5,4},{6,5},{7,6},{8,7},{9,8},{10,9},{11,1... | collective-permute-start | bytes 12296 | tf_op jit(solution)/shard_map/ppermute | solution.py:25
  188.1 15.3 %collective-permute-start.26 = (f32[1,48,128]{2,1,0:T(8,128)S(1)}, f32[1,48,128]{2,1,0:T(8,128)S(1)}, u32[]{:S(2)}, u32[]{:S(2)}) collective-permute-start(f32[1,48,128]{2,1,0:T(8,128)S(1)} %get-tuple-element.7), channel_id=1, source_target_pairs={{0,12},{12,24},{24,36},{36,48},{48,60},{60,72},{72,84},{84,96},{96... | collective-permute-start | bytes 73736 | tf_op jit(solution)/shard_map/ppermute | solution.py:23
  201.5 8.5 %collective-permute-start.27 = (f32[1,48,128]{2,1,0:T(8,128)S(1)}, f32[1,48,128]{2,1,0:T(8,128)S(1)}, u32[]{:S(2)}, u32[]{:S(2)}) collective-permute-start(f32[1,48,128]{2,1,0:T(8,128)S(1)} %get-tuple-element.7), channel_id=1, source_target_pairs={{12,0},{24,12},{36,24},{48,36},{60,48},{72,60},{84,72},{96,84},{10... | collective-permute-start | bytes 73736 | tf_op jit(solution)/shard_map/ppermute | solution.py:25
  210.2 4.3 %collective-permute-start.28 = (f32[1,48,128]{2,1,0:T(8,128)S(1)}, f32[1,48,128]{2,1,0:T(8,128)S(1)}, u32[]{:S(2)}, u32[]{:S(2)}) collective-permute-start(f32[1,48,128]{2,1,0:T(8,128)S(1)} %fusion.121), channel_id=1, source_target_pairs={{0,12},{12,24},{24,36},{36,48},{48,60},{60,72},{72,84},{84,96},{96... | collective-permute-start | bytes 73736 | tf_op jit(solution)/shard_map/ppermute | solution.py:23
  212.1 8.5 %collective-permute-start.29 = (f32[1,48,128]{2,1,0:T(8,128)S(1)}, f32[1,48,128]{2,1,0:T(8,128)S(1)}, u32[]{:S(2)}, u32[]{:S(2)}) collective-permute-start(f32[1,48,128]{2,1,0:T(8,128)S(1)} %fusion.121), channel_id=1, source_target_pairs={{12,0},{24,12},{36,24},{48,36},{60,48},{72,60},{84,72},{96,84},{10... | collective-permute-start | bytes 73736 | tf_op jit(solution)/shard_map/ppermute | solution.py:25
  220.8 4.3 %collective-permute-start.30 = (f32[1,48,128]{2,1,0:T(8,128)S(1)}, f32[1,48,128]{2,1,0:T(8,128)S(1)}, u32[]{:S(2)}, u32[]{:S(2)}) collective-permute-start(f32[1,48,128]{2,1,0:T(8,128)S(1)} %fusion.109), channel_id=1, source_target_pairs={{0,12},{12,24},{24,36},{36,48},{48,60},{60,72},{72,84},{84,96},{96... | collective-permute-start | bytes 73736 | tf_op jit(solution)/shard_map/ppermute | solution.py:23
  222.7 8.5 %collective-permute-start.31 = (f32[1,48,128]{2,1,0:T(8,128)S(1)}, f32[1,48,128]{2,1,0:T(8,128)S(1)}, u32[]{:S(2)}, u32[]{:S(2)}) collective-permute-start(f32[1,48,128]{2,1,0:T(8,128)S(1)} %fusion.109), channel_id=1, source_target_pairs={{12,0},{24,12},{36,24},{48,36},{60,48},{72,60},{84,72},{96,84},{10... | collective-permute-start | bytes 73736 | tf_op jit(solution)/shard_map/ppermute | solution.py:25
  231.4 4.4 %collective-permute-start.32 = (f32[1,48,128]{2,1,0:T(8,128)S(1)}, f32[1,48,128]{2,1,0:T(8,128)S(1)}, u32[]{:S(2)}, u32[]{:S(2)}) collective-permute-start(f32[1,48,128]{2,1,0:T(8,128)S(1)} %fusion.97), channel_id=1, source_target_pairs={{0,12},{12,24},{24,36},{36,48},{48,60},{60,72},{72,84},{84,96},{96... | collective-permute-start | bytes 73736 | tf_op jit(solution)/shard_map/ppermute | solution.py:23
  233.3 8.5 %collective-permute-start.33 = (f32[1,48,128]{2,1,0:T(8,128)S(1)}, f32[1,48,128]{2,1,0:T(8,128)S(1)}, u32[]{:S(2)}, u32[]{:S(2)}) collective-permute-start(f32[1,48,128]{2,1,0:T(8,128)S(1)} %fusion.97), channel_id=1, source_target_pairs={{12,0},{24,12},{36,24},{48,36},{60,48},{72,60},{84,72},{96,84},{10... | collective-permute-start | bytes 73736 | tf_op jit(solution)/shard_map/ppermute | solution.py:25
  244.4 8.3 %collective-permute-start.35 = (f32[1,8,256]{2,1,0:T(8,128)S(1)}, f32[1,8,256]{2,1,0:T(8,128)S(1)}, u32[]{:S(2)}, u32[]{:S(2)}) collective-permute-start(f32[1,8,256]{2,1,0:T(8,128)S(1)} %get-tuple-element.63), channel_id=1, source_target_pairs={{12,0},{24,12},{36,24},{48,36},{60,48},{72,60},{84,72},{96,84},{10... | collective-permute-start | bytes 24584 | tf_op jit(solution)/shard_map/ppermute | solution.py:25
  254.0 4.4 %collective-permute-start.37 = (f32[4,1,256]{2,1,0:T(1,128)S(1)}, f32[4,1,256]{2,1,0:T(1,128)S(1)}, u32[]{:S(2)}, u32[]{:S(2)}) collective-permute-start(f32[4,1,256]{2,1,0:T(1,128)S(1)} %get-tuple-element.53), channel_id=1, source_target_pairs={{1,0},{2,1},{3,2},{4,3},{5,4},{6,5},{7,6},{8,7},{9,8},{10,9},{11,1... | collective-permute-start | bytes 12296 | tf_op jit(solution)/shard_map/ppermute | solution.py:25
  258.6 5.0 %collective-permute-start.38 = (f32[1,8,256]{2,1,0:T(8,128)S(1)}, f32[1,8,256]{2,1,0:T(8,128)S(1)}, u32[]{:S(2)}, u32[]{:S(2)}) collective-permute-start(f32[1,8,256]{2,1,0:T(8,128)S(1)} %get-tuple-element.60), channel_id=1, source_target_pairs={{0,12},{12,24},{24,36},{36,48},{48,60},{60,72},{72,84},{84,96},{96... | collective-permute-start | bytes 24584 | tf_op jit(solution)/shard_map/ppermute | solution.py:23
  261.7 8.3 %collective-permute-start.39 = (f32[1,8,256]{2,1,0:T(8,128)S(1)}, f32[1,8,256]{2,1,0:T(8,128)S(1)}, u32[]{:S(2)}, u32[]{:S(2)}) collective-permute-start(f32[1,8,256]{2,1,0:T(8,128)S(1)} %get-tuple-element.61), channel_id=1, source_target_pairs={{12,0},{24,12},{36,24},{48,36},{60,48},{72,60},{84,72},{96,84},{10... | collective-permute-start | bytes 24584 | tf_op jit(solution)/shard_map/ppermute | solution.py:25
  270.0 4.5 %collective-permute-start.40 = (f32[4,1,256]{2,1,0:T(1,128)S(1)}, f32[4,1,256]{2,1,0:T(1,128)S(1)}, u32[]{:S(2)}, u32[]{:S(2)}) collective-permute-start(f32[4,1,256]{2,1,0:T(1,128)S(1)} %get-tuple-element.50), channel_id=1, source_target_pairs={{0,1},{1,2},{2,3},{3,4},{4,5},{5,6},{6,7},{7,8},{8,9},{9,10},{10,1... | collective-permute-start | bytes 12296 | tf_op jit(solution)/shard_map/ppermute | solution.py:23
  273.1 4.5 %collective-permute-start.41 = (f32[4,1,256]{2,1,0:T(1,128)S(1)}, f32[4,1,256]{2,1,0:T(1,128)S(1)}, u32[]{:S(2)}, u32[]{:S(2)}) collective-permute-start(f32[4,1,256]{2,1,0:T(1,128)S(1)} %get-tuple-element.51), channel_id=1, source_target_pairs={{1,0},{2,1},{3,2},{4,3},{5,4},{6,5},{7,6},{8,7},{9,8},{10,9},{11,1... | collective-permute-start | bytes 12296 | tf_op jit(solution)/shard_map/ppermute | solution.py:25
  288.6 5.2 %collective-permute-start.42 = (f32[1,16,512]{2,1,0:T(8,128)S(1)}, f32[1,16,512]{2,1,0:T(8,128)S(1)}, u32[]{:S(2)}, u32[]{:S(2)}) collective-permute-start(f32[1,16,512]{2,1,0:T(8,128)S(1)} %get-tuple-element.42), channel_id=1, source_target_pairs={{0,12},{12,24},{24,36},{36,48},{48,60},{60,72},{72,84},{84,96},{96... | collective-permute-start | bytes 98312 | tf_op jit(solution)/shard_map/ppermute | solution.py:23
  291.8 8.6 %collective-permute-start.43 = (f32[1,16,512]{2,1,0:T(8,128)S(1)}, f32[1,16,512]{2,1,0:T(8,128)S(1)}, u32[]{:S(2)}, u32[]{:S(2)}) collective-permute-start(f32[1,16,512]{2,1,0:T(8,128)S(1)} %get-tuple-element.43), channel_id=1, source_target_pairs={{12,0},{24,12},{36,24},{48,36},{60,48},{72,60},{84,72},{96,84},{10... | collective-permute-start | bytes 98312 | tf_op jit(solution)/shard_map/ppermute | solution.py:25
  300.4 6.0 %collective-permute-start.44 = (f32[6,1,512]{2,1,0:T(1,128)S(1)}, f32[6,1,512]{2,1,0:T(1,128)S(1)}, u32[]{:S(2)}, u32[]{:S(2)}) collective-permute-start(f32[6,1,512]{2,1,0:T(1,128)S(1)} %get-tuple-element.32), channel_id=1, source_target_pairs={{0,1},{1,2},{2,3},{3,4},{4,5},{5,6},{6,7},{7,8},{8,9},{9,10},{10,1... | collective-permute-start | bytes 36872 | tf_op jit(solution)/shard_map/ppermute | solution.py:23
  305.1 4.7 %collective-permute-start.45 = (f32[6,1,512]{2,1,0:T(1,128)S(1)}, f32[6,1,512]{2,1,0:T(1,128)S(1)}, u32[]{:S(2)}, u32[]{:S(2)}) collective-permute-start(f32[6,1,512]{2,1,0:T(1,128)S(1)} %get-tuple-element.33), channel_id=1, source_target_pairs={{1,0},{2,1},{3,2},{4,3},{5,4},{6,5},{7,6},{8,7},{9,8},{10,9},{11,1... | collective-permute-start | bytes 36872 | tf_op jit(solution)/shard_map/ppermute | solution.py:25
  310.3 5.0 %collective-permute-start.46 = (f32[1,16,512]{2,1,0:T(8,128)S(1)}, f32[1,16,512]{2,1,0:T(8,128)S(1)}, u32[]{:S(2)}, u32[]{:S(2)}) collective-permute-start(f32[1,16,512]{2,1,0:T(8,128)S(1)} %get-tuple-element.40), channel_id=1, source_target_pairs={{0,12},{12,24},{24,36},{36,48},{48,60},{60,72},{72,84},{84,96},{96... | collective-permute-start | bytes 98312 | tf_op jit(solution)/shard_map/ppermute | solution.py:23
  313.3 8.6 %collective-permute-start.47 = (f32[1,16,512]{2,1,0:T(8,128)S(1)}, f32[1,16,512]{2,1,0:T(8,128)S(1)}, u32[]{:S(2)}, u32[]{:S(2)}) collective-permute-start(f32[1,16,512]{2,1,0:T(8,128)S(1)} %get-tuple-element.41), channel_id=1, source_target_pairs={{12,0},{24,12},{36,24},{48,36},{60,48},{72,60},{84,72},{96,84},{10... | collective-permute-start | bytes 98312 | tf_op jit(solution)/shard_map/ppermute | solution.py:25
  321.9 4.9 %collective-permute-start.48 = (f32[6,1,512]{2,1,0:T(1,128)S(1)}, f32[6,1,512]{2,1,0:T(1,128)S(1)}, u32[]{:S(2)}, u32[]{:S(2)}) collective-permute-start(f32[6,1,512]{2,1,0:T(1,128)S(1)} %get-tuple-element.30), channel_id=1, source_target_pairs={{0,1},{1,2},{2,3},{3,4},{4,5},{5,6},{6,7},{7,8},{8,9},{9,10},{10,1... | collective-permute-start | bytes 36872 | tf_op jit(solution)/shard_map/ppermute | solution.py:23
  325.5 4.4 %collective-permute-start.49 = (f32[6,1,512]{2,1,0:T(1,128)S(1)}, f32[6,1,512]{2,1,0:T(1,128)S(1)}, u32[]{:S(2)}, u32[]{:S(2)}) collective-permute-start(f32[6,1,512]{2,1,0:T(1,128)S(1)} %get-tuple-element.31), channel_id=1, source_target_pairs={{1,0},{2,1},{3,2},{4,3},{5,4},{6,5},{7,6},{8,7},{9,8},{10,9},{11,1... | collective-permute-start | bytes 36872 | tf_op jit(solution)/shard_map/ppermute | solution.py:25
  (3 other events, 21.0 us)
where the time goes:
time: 333 us; the launch traced here: 331 us
  starting transfers between devices  151 us (45%)
  waiting for transfers between devices  90.1 us (27%)
  blocking collectives  42.4 us (13%)
  local copies, waits for them, and re-layouts  31.8 us (10%)
  other arithmetic  14.5 us (4%)
    ppermute x25, starting transfers between devices, padded_2(): lax.ppermute(tail, axis, [(i, (i + 1) % count) for i in range(ends)])  107 us
    ppermute x25, waiting for transfers between devices, padded_2(): lax.ppermute(head, axis, [((i + 1) % count, i) for i in range(ends)])  90 us
    ppermute x25, starting transfers between devices, padded_2(): lax.ppermute(head, axis, [((i + 1) % count, i) for i in range(ends)])  44.3 us
    all_gather x1, blocking collectives, agglomerate(): lax.all_gather(cond, 'plan', axis=1, tiled=True)  23.9 us
    reshape x2, local copies, waits for them, and re-layouts, block_sum(): field.reshape(depth // 2, 2, across // 2, 2, along // 2, 2)  19.6 us
    all_gather x1, blocking collectives, agglomerate(): lax.all_gather(source, 'plan', axis=1, tiled=True)  18.5 us
    reduce_sum x5, other arithmetic, block_sum(): field.reshape(depth // 2, 2, across // 2, 2, along // 2, 2)  8.43 us
    reshape x1, local copies, waits for them, and re-layouts, prolong(): return wide.reshape(depth * 2, across * 2, along * 2)  6.94 us
  transfers between devices with their start and end apart: 50, of which 18 were waited for; matrix products, arithmetic and copies ran while one was open for 5% of the time, Pallas kernels for 0%

commit v1 on v0

v1 whole, which is shorter than its diff:
```python
import jax
import jax.numpy as jnp
from jax import lax
from jax.experimental import pallas as pl
from jax.experimental.pallas import tpu as pltpu
from jax.sharding import PartitionSpec as P

PERMEABILITY = (1.0, 0.1, 0.6, 0.8, 0.25)
OMEGA = 2.0 / 3.0
F32 = jnp.float32


def vmem(count):
    return [pl.BlockSpec(memory_space=pltpu.VMEM)] * count


def smem():
    return pl.BlockSpec(memory_space=pltpu.SMEM)


def call(body, outs, scratch, where, *arrays, flops=1000000):
    many = isinstance(outs, list)
    shapes = [jax.ShapeDtypeStruct(s, F32) for s in (outs if many else [outs])]
    return pl.pallas_call(
        body,
        out_shape=shapes if many else shapes[0],
        in_specs=([] if where is None else [smem()]) + vmem(len(arrays)),
        out_specs=vmem(len(shapes)) if many else vmem(1)[0],
        scratch_shapes=[pltpu.VMEM(s, F32) for s in scratch],
        compiler_params=pltpu.CompilerParams(vmem_limit_bytes=40 << 20),
    )(*(() if where is None else (where,)), *arrays)


def harmonic(a, b):
    return 2.0 * a * b / (a + b)


def iota(shape, dim):
    return lax.broadcasted_iota(jnp.int32, shape, dim)


def ahead(x, axis):
    return pltpu.roll(x, x.shape[axis] - 1, axis)


def behind(x, axis):
    return pltpu.roll(x, 1, axis)


def y_faces(c):
    lane = iota(c.shape, 1)
    last = c.shape[1] - 1
    full = harmonic(c, jnp.where(lane == last, 1.0, ahead(c, 1)))
    link = jnp.where(lane == last, 0.0, full)
    first = jnp.where(lane == 0, harmonic(c, 1.0), 0.0)
    return link, full + behind(link, 1) + first


def spread(p, below, above, cz0, cz1, cx, cy):
    total = cz0 * below + cz1 * above
    total = total + cx * ahead(p, 0) + behind(cx * p, 0)
    return total + cy * ahead(p, 1) + behind(cy * p, 1)


def pair_matrix(wide):
    shape = (wide, wide // 2)
    return (lax.shift_right_logical(iota(shape, 0), 1) == iota(shape, 1)).astype(F32)


def copy_matrix(narrow):
    shape = (narrow, narrow * 2)
    return (iota(shape, 0) == lax.shift_right_logical(iota(shape, 1), 1)).astype(F32)


def dot(a, b):
    return jnp.dot(a, b, precision=lax.Precision.HIGHEST, preferred_element_type=F32)


def pair_rows(s, x, start, count):
    tiles = x.shape[1] // 128
    for t in range(tiles):
        s[t, 0 : x.shape[0]] = x[:, 128 * t : 128 * t + 128]
    parts = [s[t, pl.ds(start, count, stride=2), :] + s[t, pl.ds(start + 1, count, stride=2), :] for t in range(tiles)]
    return jnp.concatenate(parts, axis=1)


def copy_rows(s, x):
    tiles, count = x.shape[1] // 128, x.shape[0]
    for t in range(tiles):
        s[t, pl.ds(0, count, stride=2), :] = x[:, 128 * t : 128 * t + 128]
        s[t, pl.ds(1, count, stride=2), :] = x[:, 128 * t : 128 * t + 128]
    return jnp.concatenate([s[t, 0 : 2 * count] for t in range(tiles)], axis=1)


def inside(first, index, count):
    at = first + index
    return jnp.logical_and(at >= 0, at < count)


def k_conduct(div, density, zones, out):
    for z in range(4):
        zone = zones[z]
        perm = jnp.where(zone == 0, PERMEABILITY[0], 0.0)
        for zone_id in range(1, 5):
            perm = jnp.where(zone == zone_id, PERMEABILITY[zone_id], perm)
        out[0, z] = perm / density[z]
        out[1, z] = div[z]


def k_rows0(where, own, core, link, cond, div, left, right):
    h, high = where[0], where[2]
    odd = lax.rem(h, 2)
    cond[4:8] = own[0]
    div[4:8] = own[1]

    @pl.when(odd == 0)
    def _():
        cond[0:4] = link[0, 0]
        div[0:4] = link[0, 1]
        cond[8:12] = core[1, 0]
        div[8:12] = core[1, 1]

    @pl.when(odd == 1)
    def _():
        cond[0:4] = core[0, 0]
        div[0:4] = core[0, 1]
        cond[8:12] = link[1, 0]
        div[8:12] = link[1, 1]

    @pl.when(h == 0)
    def _():
        cond[0:4] = jnp.ones((4, 16, 512), F32)

    @pl.when(h == high - 1)
    def _():
        cond[8:12] = jnp.ones((4, 16, 512), F32)

    for z in range(10):
        left[z, 0:4] = cond[z + 1, 0:4]
        left[z, 4:8] = div[z + 1, 0:4]
        right[z, 0:4] = cond[z + 1, 12:16]
        right[z, 4:8] = div[z + 1, 12:16]


def k_level0(where, cond, div, low, high, pre, w_out, g_out, cx_out, cy_out, cz_out, pack, c, g, w, cx, cy, cz, dg, p, rs, c1, st):
    h, plan, n_h, n_p = where[0], where[1], where[2], where[3]
    for z in range(12):
        c[z, 4:20] = cond[z]
        if 1 <= z <= 10:
            c[z, 0:4] = jnp.where(plan == 0, 1.0, low[z - 1, 0:4])
            c[z, 20:24] = jnp.where(plan == n_p - 1, 1.0, high[z - 1, 0:4])
        else:
            c[z, 0:4] = jnp.ones((4, 512), F32)
            c[z, 20:24] = jnp.ones((4, 512), F32)
    for z in range(1, 11):
        g[z, 4:20] = div[z]
        g[z, 0:4] = low[z - 1, 4:8]
        g[z, 20:24] = high[z - 1, 4:8]
    row = iota((24, 512), 0) + (plan * 16 - 4)
    row_in = jnp.logical_and(row >= 0, row < n_p * 16).astype(F32) * OMEGA
    for z in range(11):
        cz[z] = harmonic(c[z], c[z + 1])
    for z in range(1, 11):
        here = c[z]
        fx = harmonic(here, ahead(here, 0))
        link, both = y_faces(here)
        diag = cz[z - 1] + cz[z] + fx + behind(fx, 0) + both
        weight = jnp.where(inside(h * 4 - 4, z, n_h * 4), row_in, 0.0) / diag
        cx[z] = fx
        cy[z] = link
        w[z] = weight
        if 4 <= z <= 7:
            dg[z - 4] = diag
            rs[z - 4] = g[z]
        g[z] = weight * g[z]
    for z in range(2, 10):
        here = g[z]
        total = spread(here, g[z - 1], g[z + 1], cz[z - 1], cz[z], cx[z], cy[z])
        p[z] = here * (1.0 / 3.0) + here + w[z] * total
    for z in range(4, 8):
        here = p[z]
        total = spread(here, p[z - 1], p[z + 1], cz[z - 1], cz[z], cx[z], cy[z])
        rs[z - 4] = rs[z - 4] - dg[z - 4] * here + total
    for z in range(2, 10):
        pre[z - 2] = p[z]
    for z in range(3, 9):
        w_out[z - 3] = w[z]
        g_out[z - 3] = g[z]
        cx_out[z - 3] = cx[z]
        cy_out[z - 3] = cy[z]
    for z in range(2, 9):
        cz_out[z - 2] = cz[z]
    rows = [pair_rows(st.at[z], rs[2 * z] + rs[2 * z + 1], 4, 8) for z in range(2)]
    for z in range(4):
        sums = c[2 * z + 2] + c[2 * z + 3]
        c1[z, 0:8] = pair_rows(st.at[2 + 2 * z], sums, 0, 8)
        c1[z, 8:12] = pair_rows(st.at[3 + 2 * z], sums[16:24], 0, 4)
        c1[z, 12:16] = jnp.full((4, 512), 4.0, F32)
    pairs = pair_matrix(512)
    f1 = 0.5 * dot(jnp.concatenate(rows, axis=0), pairs)
    k1 = 0.125 * dot(jnp.concatenate([c1[z] for z in range(4)], axis=0), pairs)
    k1 = [k1[16 * z : 16 * z + 16] for z in range(4)]
    for z in range(2):
        here = k1[z + 1]
        fx = harmonic(here, ahead(here, 0))
        link, both = y_faces(here)
        diag = harmonic(here, k1[z]) + harmonic(here, k1[z + 2]) + fx + behind(fx, 0) + both
        c1[z, :, 0:256] = here
        c1[z, :, 256:512] = diag
        pack[z, 0:8] = OMEGA * f1[8 * z : 8 * z + 8] / c1[z, 2:10, 256:512]
        pack[z, 8:16] = c1[z, 2:10, 0:256]


def k_rows1(where, chip, link, third, g, c, left, right, s):
    h, high = where[0], where[2]
    odd = lax.rem(h, 2)

    @pl.when(odd == 0)
    def _():
        s[0:4] = link[0]
        s[4:8] = chip[...]
        s[8:10] = third[1]

    @pl.when(odd == 1)
    def _():
        s[0:2] = third[0]
        s[2:6] = chip[...]
        s[6:10] = link[1]

    for z in range(10):
        keep = inside(h * 2 - 4, z, high * 2)
        g[z] = jnp.where(keep, s[z, 0:8], 0.0)
        c[z] = jnp.where(keep, s[z, 8:16], 1.0)
    for z in range(10):
        left[z, 0:4] = g[z, 0:4]
        left[z, 4:8] = c[z, 0:4]
        right[z, 0:4] = g[z, 4:8]
        right[z, 4:8] = c[z, 4:8]


def k_level1(where, g_in, c_in, low, high, pre, w_out, g_out, cx_out, cy_out, cz_out, copies, c, g, w, cx, cy, cz, dg, rs, st):
    h, plan, n_h, n_p = where[0], where[1], where[2], where[3]
    for z in range(10):
        g[z, 4:12] = g_in[z]
        c[z, 4:12] = c_in[z]
        g[z, 0:4] = jnp.where(plan == 0, 0.0, low[z, 0:4])
        c[z, 0:4] = jnp.where(plan == 0, 1.0, low[z, 4:8])
        g[z, 12:16] = jnp.where(plan == n_p - 1, 0.0, high[z, 0:4])
        c[z, 12:16] = jnp.where(plan == n_p - 1, 1.0, high[z, 4:8])
    row = iota((16, 256), 0) + (plan * 8 - 4)
    row_in = jnp.logical_and(row >= 0, row < n_p * 8).astype(F32) * OMEGA
    for z in range(9):
        cz[z] = harmonic(c[z], c[z + 1])
    for z in range(1, 9):
        here = c[z]
        fx = harmonic(here, ahead(here, 0))
        link, both = y_faces(here)
        diag = cz[z - 1] + cz[z] + fx + behind(fx, 0) + both
        cx[z] = fx
        cy[z] = link
        w[z] = jnp.where(inside(h * 2 - 4, z, n_h * 2), row_in, 0.0) / diag
        if 4 <= z <= 5:
            dg[z - 4] = diag
    for z in range(1, 9):
        here = g[z]
        total = spread(here, g[z - 1], g[z + 1], cz[z - 1], cz[z], cx[z], cy[z])
        pre[z - 1] = here * (1.0 / 3.0) + here + w[z] * total
    for z in range(4, 6):
        here = pre[z - 1]
        total = spread(here, pre[z - 2], pre[z], cz[z - 1], cz[z], cx[z], cy[z])
        rs[z - 4] = (g[z] - OMEGA * here + w[z] * total) * dg[z - 4] * 1.5
    for z in range(2, 8):
        w_out[z - 2] = w[z]
        g_out[z - 2] = g[z]
        cx_out[z - 2] = cx[z]
        cy_out[z - 2] = cy[z]
    for z in range(1, 8):
        cz_out[z - 1] = cz[z]
    rows = [pair_rows(st.at[0], rs[0] + rs[1], 0, 8)]
    rows += [pair_rows(st.at[z + 1], c[2 * z + 2] + c[2 * z + 3], 0, 8) for z in range(3)]
    pairs = pair_matrix(256)
    both = jnp.concatenate(rows, axis=0)
    down = dot(both, pairs)
    f2 = 0.5 * down[0:8]
    k2 = [0.125 * down[8 * z + 8 : 8 * z + 16] for z in range(3)]
    here = k2[1]
    fx = harmonic(here, ahead(here, 0))
    link, share = y_faces(here)
    diag = harmonic(here, k2[0]) + harmonic(here, k2[2]) + fx + behind(fx, 0) + share
    dg[0, 0:8, 0:128] = diag
    dg[0, 8:16, 0:128] = here
    tile_g = OMEGA * f2[2:6] / dg[0, 2:6, 0:128]
    tile_c = dg[0, 10:14, 0:128]
    for i in range(copies.shape[0]):
        copies[i, 0:4] = tile_g
        copies[i, 4:8] = tile_c


def k_wide(tiles, copies):
    n = tiles.shape[0]
    for t in range(n):
        copies[0, 4 * t : 4 * t + 4] = tiles[t, 0:4]
        copies[0, 4 * n + 4 * t : 4 * n + 4 * t + 4] = tiles[t, 4:8]
    for i in range(1, copies.shape[0]):
        copies[i] = copies[0]


def k_up(where, block, outer, pre1, w1, g1, cx1, cy1, cz1, pre0, w0, g0, cx0, cy0, cz0, out, s, c, g, w, cx, cy, cz, dg, pa, pb, p2, u1, q1, u0, q0, s1, s0):
    h, plan, n_h = where[0], where[1], where[2]
    wide = s.shape[1] // 2
    s[0:6] = outer[0]
    s[6:14] = block[...]
    s[14:20] = outer[1]
    q = lax.rem(h, 8)
    for z in range(13):
        keep = inside(h - 6, z, n_h)
        g[z] = jnp.where(keep, s[q + z, 0:wide], 0.0)
        c[z] = jnp.where(keep, s[q + z, wide : 2 * wide], 1.0)
    row = iota((wide, 128), 0)
    for z in range(12):
        cz[z] = harmonic(c[z], c[z + 1])
    for z in range(1, 12):
        here = c[z]
        full = harmonic(here, jnp.where(row == wide - 1, 1.0, ahead(here, 0)))
        fx = jnp.where(row == wide - 1, 0.0, full)
        first = jnp.where(row == 0, harmonic(here, 1.0), 0.0)
        link, both = y_faces(here)
        diag = cz[z - 1] + cz[z] + full + behind(fx, 0) + first + both
        cx[z] = fx
        cy[z] = link
        w[z] = jnp.where(inside(h - 6, z, n_h), OMEGA, 0.0) / diag
        dg[z] = diag

    def step(source, z):
        here = source[z]
        total = spread(here, source[z - 1], source[z + 1], cz[z - 1], cz[z], cx[z], cy[z])
        return here * (1.0 / 3.0) + g[z] + w[z] * total

    for z in range(1, 12):
        pa[z] = step(g, z)
    for z in range(2, 11):
        pb[z] = step(pa, z)
    for z in range(3, 10):
        pa[z] = step(pb, z)
    for z in range(4, 9):
        here = pa[z]
        extra = (step(pa, z) - here) * dg[z] * 1.5
        line = jnp.sum(extra, axis=0, keepdims=True) / jnp.sum(dg[z], axis=0, keepdims=True)
        p2[z - 4, 0:8] = jnp.zeros((8, 128), F32)
        p2[z - 4, wide + 8 : wide + 16] = jnp.zeros((8, 128), F32)
        p2[z - 4, 8 : wide + 8] = here + line
    rows = jnp.concatenate([p2[z, pl.ds(plan * 4 + 6, 8), :] for z in range(5)], axis=0)
    rows = dot(rows, copy_matrix(128))
    for z in range(5):
        u1[z] = copy_rows(s1.at[z], rows[8 * z : 8 * z + 8])
    for z in range(1, 9):
        q1[z - 1] = pre1[z - 1] + u1[z // 2]
    mid = []
    for z in range(2, 8):
        here = q1[z - 1]
        total = spread(here, q1[z - 2], q1[z], cz1[z - 2], cz1[z - 1], cx1[z - 2], cy1[z - 2])
        pb_rows = here * (1.0 / 3.0) + g1[z - 2] + w1[z - 2] * total
        mid.append(pb_rows)
    for z in range(6):
        q1[z] = mid[z]
    low = []
    for z in range(3, 7):
        here = q1[z - 2]
        total = spread(here, q1[z - 3], q1[z - 1], cz1[z - 2], cz1[z - 1], cx1[z - 2], cy1[z - 2])
        low.append(here * (1.0 / 3.0) + g1[z - 2] + w1[z - 2] * total)
    for z in range(4):
        q1[z] = low[z]
    rows = jnp.concatenate([q1[z] for z in range(4)], axis=0)
    rows = dot(rows, copy_matrix(256))
    for z in range(4):
        u0[z] = copy_rows(s0.at[z], rows[16 * z : 16 * z + 16])
    for z in range(2, 10):
        q0[z - 2] = pre0[z - 2] + u0[z // 2 - 1, 4:28]
    for z in range(3, 9):
        here = q0[z - 2]
        total = spread(here, q0[z - 3], q0[z - 1], cz0[z - 3], cz0[z - 2], cx0[z - 3], cy0[z - 3])
        u0[z - 3, 0:24] = here * (1.0 / 3.0) + g0[z - 3] + w0[z - 3] * total
    for z in range(4, 8):
        here = u0[z - 3, 0:24]
        total = spread(here, u0[z - 4, 0:24], u0[z - 2, 0:24], cz0[z - 3], cz0[z - 2], cx0[z - 3], cy0[z - 3])
        q0[z - 4] = here * (1.0 / 3.0) + g0[z - 3] + w0[z - 3] * total
        out[z - 4] = q0[z - 4, 4:20]


def on_device(divergence, density, zones):
    n_h, n_p = lax.axis_size("height"), lax.axis_size("plan")
    h, plan = lax.axis_index("height"), lax.axis_index("plan")
    odd = lax.rem(h, 2)
    where = jnp.stack([h, plan, jnp.int32(n_h), jnp.int32(n_p)])
    cores = [[i, i + 1] for i in range(0, n_h, 2)]
    links = [[i, (i + 1) % n_h] for i in range(1, n_h, 2)]

    def pair(x, groups):
        return lax.all_gather(x, "height", axis=0, tiled=False, axis_index_groups=groups)

    def beside(low_rows, high_rows):
        up = [(i, i + 1) for i in range(n_p - 1)]
        down = [(i + 1, i) for i in range(n_p - 1)]
        return lax.ppermute(high_rows, "plan", up), lax.ppermute(low_rows, "plan", down)

    own = call(k_conduct, (2, 4, 16, 512), [], None, divergence, density, zones)
    core = pair(own, cores)
    link = pair(own, links)
    tall = (12, 16, 512)
    cond, div, left, right = call(k_rows0, [tall, tall, (10, 8, 512), (10, 8, 512)], [], where, own, core, link)
    low, high = beside(left, right)
    box = (12, 24, 512)
    eight, six, seven = (8, 24, 512), (6, 24, 512), (7, 24, 512)
    *level0, pack = call(
        k_level0,
        [eight, six, six, six, six, seven, (2, 16, 256)],
        [box] * 6 + [(4, 24, 512), box, (4, 24, 512), (4, 16, 512), (10, 4, 24, 128)],
        where, cond, div, low, high,
    )
    chip = pair(pack, cores).reshape(4, 16, 256)
    link = pair(chip, links)
    third = pair(jnp.where(odd == 0, link[0, 2:4], link[1, 0:2]), cores)
    g1, c1, left, right = call(k_rows1, [(10, 8, 256)] * 4, [(10, 16, 256)], where, chip, link, third)
    low, high = beside(left, right)
    box = (10, 16, 256)
    eight, six, seven = (8, 16, 256), (6, 16, 256), (7, 16, 256)
    *level1, tiles = call(
        k_level1,
        [eight, six, six, six, six, seven, (n_p, 8, 128)],
        [box] * 6 + [(2, 16, 256), (2, 16, 256), (4, 2, 16, 128)],
        where, g1, c1, low, high,
    )
    tiles = lax.all_to_all(tiles, "plan", split_axis=0, concat_axis=0, tiled=True)
    wide = n_p * 4
    block = call(k_wide, (8, 2 * wide, 128), [], None, tiles)
    rows = [[8 * y + i for i in range(8)] for y in range(n_h // 8)]
    block = lax.all_to_all(block, "height", split_axis=0, concat_axis=0, tiled=True, axis_index_groups=rows)
    cross = []
    for y in range(n_h // 8 - 1):
        for i in range(0, 8, 2):
            cross += [(8 * y + i + 1, 8 * y + 8 + i), (8 * y + 8 + i, 8 * y + i + 1)]
    part = lax.dynamic_slice_in_dim(block, 2 * odd, 6, 0)
    outer = pair(lax.ppermute(part, "height", cross), cores)
    flat = (13, wide, 128)
    return call(
        k_up,
        (4, 16, 512),
        [(20, 2 * wide, 128)] + [flat] * 9 + [(5, wide + 16, 128), (5, 16, 256), (8, 16, 256), (6, 32, 512), (8, 24, 512), (5, 2, 16, 128), (4, 4, 32, 128)],
        where, block, outer, *level1, *level0,
    )


def solution(mesh):
    return jax.shard_map(
        on_device,
        mesh=mesh,
        in_specs=(P("height", "plan", None), P("height", "plan", None), P("height", "plan", None)),
        out_specs=P("height", "plan", None),
        check_vma=False,
    )
```

time: 333 us -> 107 us (0.32)
  the two profiles are of different devices: /device:TPU:31 before, /device:TPU:33 now
where the time goes in v1:
time: 107 us
  blocking collectives  49.7 us (46%)
  waiting for transfers between devices  26 us (24%)
  starting transfers between devices  19 us (18%)
  Pallas kernels  8.91 us (8%)
  local copies, waits for them, and re-layouts  2.73 us (3%)
    all_gather x6, blocking collectives, pair(): lax.all_gather(x, 'height', axis=0, tiled=False, axis_index_groups=groups)  28.4 us
    all_to_all x1, blocking collectives, on_device(): lax.all_to_all(tiles, 'plan', split_axis=0, concat_axis=0, tiled=True)  21.2 us
    ppermute x2, waiting for transfers between devices, beside(): lax.ppermute(low_rows, 'plan', down)  10.4 us
    pallas_call x7, Pallas kernels, call(): pl.pallas_call(body, out_shape=shapes if many else shapes[0], in_specs=([...  8.91 us
    all_to_all x1, waiting for transfers between devices, on_device(): lax.all_to_all(block, 'height', split_axis=0, concat_axis=0, tiled=True,...  8.1 us
    ppermute x2, starting transfers between devices, beside(): lax.ppermute(high_rows, 'plan', up)  8.01 us
    all_to_all x1, starting transfers between devices, on_device(): lax.all_to_all(block, 'height', split_axis=0, concat_axis=0, tiled=True,...  6.53 us
    ppermute x1, waiting for transfers between devices, on_device(): outer = pair(lax.ppermute(part, 'height', cross), cores)  6.41 us
  transfers between devices with their start and end apart: 6, of which 6 were waited for; matrix products, arithmetic and copies ran while one was open for 0% of the time, Pallas kernels for 0%

profile of v1, /device:TPU:33, one launch (start us, length us, event | category | flops | bytes accessed | tf_op | source)
XLA Modules:
  0.0 106.5 jit_solution(7027715313514511975)
XLA Ops:
  0.0 0.0 copy-start
  0.0 0.9 copy-done
  0.9 0.0 copy-start.1
  0.9 0.9 copy-done.1
  1.8 0.0 copy-start.2
  1.8 0.9 copy-done.2
  2.7 0.1 shard_map.37.own
  2.8 2.5 %all-gather = f32[4,4,16,512]{3,2,1,0:T(8,128)S(1)} all-gather(f32[2,4,16,512]{3,2,1,0:T(8,128)S(1)} %shard_map.37.own), channel_id=2, replica_groups={{0,12},{24,36},{48,60},{72,84},{96,108},{120,132},{144,156},{168,180},{..., dimensions={0}, use_global_device_ids=true | all-gather | bytes 786432 | tf_op jit(solution)/shard_map/all_gather | solution.py:399
  5.3 6.8 %all-gather.1 = f32[4,4,16,512]{3,2,1,0:T(8,128)S(1)} all-gather(f32[2,4,16,512]{3,2,1,0:T(8,128)S(1)} %shard_map.37.own), channel_id=3, replica_groups={{12,24},{36,48},{60,72},{84,96},{108,120},{132,144},{156,168},{180,192}..., dimensions={0}, use_global_device_ids=true | all-gather | bytes 786432 | tf_op jit(solution)/shard_map/all_gather | solution.py:399
  12.0 0.1 pad_add_fusion.where
  12.1 0.7 shard_map.38
  12.8 4.0 %collective-permute-start = (f32[10,8,512]{2,1,0:T(8,128)S(1)}, f32[10,8,512]{2,1,0:T(8,128)S(1)}, u32[]{:S(2)}, u32[]{:S(2)}) collective-permute-start(f32[10,8,512]{2,1,0:T(8,128)S(1)} %get-tuple-element.29), channel_id=1, source_target_pairs={{0,1},{1,2},{2,3},{3,4},{4,5},{5,6},{6,7},{7,8},{8,9},{9,10},{10,1... | collective-permute-start | bytes 491528 | tf_op jit(solution)/shard_map/ppermute | solution.py:404
  16.8 1.3 %collective-permute-start.1 = (f32[10,8,512]{2,1,0:T(8,128)S(1)}, f32[10,8,512]{2,1,0:T(8,128)S(1)}, u32[]{:S(2)}, u32[]{:S(2)}) collective-permute-start(f32[10,8,512]{2,1,0:T(8,128)S(1)} %get-tuple-element.30), channel_id=1, source_target_pairs={{1,0},{2,1},{3,2},{4,3},{5,4},{6,5},{7,6},{8,7},{9,8},{10,9},{11,1... | collective-permute-start | bytes 491528 | tf_op jit(solution)/shard_map/ppermute | solution.py:404
  18.1 0.9 collective-permute-done.low
  19.0 4.5 %collective-permute-done.1.high = f32[10,8,512]{2,1,0:T(8,128)S(1)} collective-permute-done((f32[10,8,512]{2,1,0:T(8,128)S(1)}, f32[10,8,512]{2,1,0:T(8,128)S(1)}, u32[]{:S(2)}, u32[]{:S(2)}) %collective-permute-start.1) | collective-permute-done | bytes 163872 | tf_op jit(solution)/shard_map/ppermute | solution.py:404
  23.5 2.2 %shard_map.39 = (f32[8,24,512]{2,1,0:T(8,128)S(1)}, f32[6,24,512]{2,1,0:T(8,128)S(1)}, f32[6,24,512]{2,1,0:T(8,128)S(1)}, f32[6,24,512]{2,1,0:T(8,128)S(1)}, f32...) custom-call(s32[4]{0:T(128)S(1)} %pad_add_fusion.where, ...), custom_call_target="tpu_custom_call" | custom-call | tf_op jit(solution)/shard_map/pallas_call | solution.py:24
  25.7 6.1 %all-gather.2.chip = f32[4,16,256]{2,1,0:T(8,128)S(1)} all-gather(f32[2,16,256]{2,1,0:T(8,128)S(1)} %get-tuple-element.31), channel_id=4, replica_groups={{0,12},{24,36},{48,60},{72,84},{96,108},{120,132},{144,156},{168,180},{..., dimensions={0}, use_global_device_ids=true | all-gather | bytes 98304 | tf_op jit(solution)/shard_map/all_gather | solution.py:399
  31.7 4.4 %all-gather.4 = f32[8,16,256]{2,1,0:T(8,128)S(1)} all-gather(f32[4,16,256]{2,1,0:T(8,128)S(1)} %all-gather.2.chip), channel_id=6, replica_groups={{12,24},{36,48},{60,72},{84,96},{108,120},{132,144},{156,168},{180,192}..., dimensions={0}, use_global_device_ids=true | all-gather | bytes 196608 | tf_op jit(solution)/shard_map/all_gather | solution.py:399
  36.1 5.2 %all_gather.35.third = f32[2,2,16,256]{3,2,1,0:T(8,128)S(1)} all-gather(f32[1,2,16,256]{3,2,1,0:T(8,128)S(1)} %slice_select_fusion), channel_id=1, replica_groups={{0,12},{24,36},{48,60},{72,84},{96,108},{120,132},{144,156},{168,180},{..., dimensions={0}, use_global_device_ids=true | all-gather | bytes 98304 | tf_op jit(solution)/shard_map/all_gather | solution.py:399
  41.3 0.6 shard_map.40
  41.9 4.0 %collective-permute-start.2 = (f32[10,8,256]{2,1,0:T(8,128)S(1)}, f32[10,8,256]{2,1,0:T(8,128)S(1)}, u32[]{:S(2)}, u32[]{:S(2)}) collective-permute-start(f32[10,8,256]{2,1,0:T(8,128)S(1)} %get-tuple-element.34), channel_id=1, source_target_pairs={{0,1},{1,2},{2,3},{3,4},{4,5},{5,6},{6,7},{7,8},{8,9},{9,10},{10,1... | collective-permute-start | bytes 245768 | tf_op jit(solution)/shard_map/ppermute | solution.py:404
  45.9 1.3 %collective-permute-start.3 = (f32[10,8,256]{2,1,0:T(8,128)S(1)}, f32[10,8,256]{2,1,0:T(8,128)S(1)}, u32[]{:S(2)}, u32[]{:S(2)}) collective-permute-start(f32[10,8,256]{2,1,0:T(8,128)S(1)} %get-tuple-element.35), channel_id=1, source_target_pairs={{1,0},{2,1},{3,2},{4,3},{5,4},{6,5},{7,6},{8,7},{9,8},{10,9},{11,1... | collective-permute-start | bytes 245768 | tf_op jit(solution)/shard_map/ppermute | solution.py:404
  47.2 0.2 collective-permute-done.2.low
  47.4 6.0 %collective-permute-done.3.high = f32[10,8,256]{2,1,0:T(8,128)S(1)} collective-permute-done((f32[10,8,256]{2,1,0:T(8,128)S(1)}, f32[10,8,256]{2,1,0:T(8,128)S(1)}, u32[]{:S(2)}, u32[]{:S(2)}) %collective-permute-start.3) | collective-permute-done | bytes 81952 | tf_op jit(solution)/shard_map/ppermute | solution.py:404
  53.3 1.2 %shard_map.41 = (f32[8,16,256]{2,1,0:T(8,128)S(1)}, f32[6,16,256]{2,1,0:T(8,128)S(1)}, f32[6,16,256]{2,1,0:T(8,128)S(1)}, f32[6,16,256]{2,1,0:T(8,128)S(1)}, f32...) custom-call(s32[4]{0:T(128)S(1)} %pad_add_fusion.where, ...), custom_call_target="tpu_custom_call" | custom-call | tf_op jit(solution)/shard_map/pallas_call | solution.py:24
  54.5 21.2 %all_to_all.10.tiles = f32[12,8,128]{2,1,0:T(8,128)S(1)} all-to-all(f32[12,8,128]{2,1,0:T(8,128)S(1)} %get-tuple-element.36), channel_id=1, replica_groups=mesh['height'=64,'plan'=12] {'plan'}, dimensions={0} | all-to-all | bytes 98304 | tf_op jit(solution)/shard_map/all_to_all | solution.py:433
  75.7 0.8 shard_map.42
  76.5 6.5 %all-to-all-start.1 = ((f32[8,96,128]{2,1,0:T(8,128)}), f32[8,96,128]{2,1,0:T(8,128)S(1)}, u32[]{:S(2)}, u32[]{:S(2)}) async-start(f32[8,96,128]{2,1,0:T(8,128)} %shard_map.42), calls=%async_computation.1 | async-start | bytes 786432 | tf_op jit(solution)/shard_map/all_to_all | solution.py:437
  83.0 8.1 %all-to-all-done.1.block = f32[8,96,128]{2,1,0:T(8,128)S(1)} async-done(((f32[8,96,128]{2,1,0:T(8,128)}), f32[8,96,128]{2,1,0:T(8,128)S(1)}, u32[]{:S(2)}, u32[]{:S(2)}) %all-to-all-start.1) | async-done | bytes 393248 | tf_op jit(solution)/shard_map/all_to_all | solution.py:437
  91.2 1.9 %collective-permute-start.4 = (f32[6,96,128]{2,1,0:T(8,128)S(1)}, f32[6,96,128]{2,1,0:T(8,128)S(1)}, u32[]{:S(2)}, u32[]{:S(2)}) collective-permute-start(f32[6,96,128]{2,1,0:T(8,128)S(1)} %constant_dynamic-slice_fusion), channel_id=1, source_target_pairs={{12,96},{96,12},{36,120},{120,36},{60,144},{144,60},{84,168},{168,... | collective-permute-start | bytes 884744 | tf_op jit(solution)/shard_map/ppermute | solution.py:443
  93.1 6.4 %collective-permute-done.4 = f32[6,96,128]{2,1,0:T(8,128)S(1)} collective-permute-done((f32[6,96,128]{2,1,0:T(8,128)S(1)}, f32[6,96,128]{2,1,0:T(8,128)S(1)}, u32[]{:S(2)}, u32[]{:S(2)}) %collective-permute-start.4) | collective-permute-done | bytes 294944 | tf_op jit(solution)/shard_map/ppermute | solution.py:443
  99.5 3.6 %all-gather.3 = f32[12,96,128]{2,1,0:T(8,128)S(1)} all-gather(f32[6,96,128]{2,1,0:T(8,128)S(1)} %collective-permute-done.4), channel_id=5, replica_groups={{0,12},{24,36},{48,60},{72,84},{96,108},{120,132},{144,156},{168,180},{..., dimensions={0}, use_global_device_ids=true | all-gather | bytes 884736 | tf_op jit(solution)/shard_map/all_gather | solution.py:399
  103.1 3.4 %shard_map.43 = f32[4,16,512]{2,1,0:T(8,128)} custom-call(s32[4]{0:T(128)S(1)} %pad_add_fusion.where, f32[8,96,128]{2,1,0:T(8,128)S(1)} %all-to-all-done.1.block, f32[2,6,96,128]{3,2,1,0:T(8,128)S(1)} %bitcast.6, f32[8,16,256]{2,1,0:T(8,128)S(1)} %get-tuple-element.37.pre1, f32[6,16,256]{2,1,0:T(8,128)S(1)} %get-tuple-element.38.w1, ...), custom_call_target="tpu_custom_call" | custom-call | tf_op jit(solution)/shard_map/pallas_call | solution.py:24
  (2 shorter events, 0.0 us)
Async XLA Ops:
  0.0 0.9 copy-start
  0.9 0.9 copy-start.1
  1.8 0.9 copy-start.2
  12.8 6.2 %collective-permute-start = (f32[10,8,512]{2,1,0:T(8,128)S(1)}, f32[10,8,512]{2,1,0:T(8,128)S(1)}, u32[]{:S(2)}, u32[]{:S(2)}) collective-permute-start(f32[10,8,512]{2,1,0:T(8,128)S(1)} %get-tuple-element.29), channel_id=1, source_target_pairs={{0,1},{1,2},{2,3},{3,4},{4,5},{5,6},{6,7},{7,8},{8,9},{9,10},{10,1... | collective-permute-start | bytes 491528 | tf_op jit(solution)/shard_map/ppermute | solution.py:404
  16.8 6.7 %collective-permute-start.1 = (f32[10,8,512]{2,1,0:T(8,128)S(1)}, f32[10,8,512]{2,1,0:T(8,128)S(1)}, u32[]{:S(2)}, u32[]{:S(2)}) collective-permute-start(f32[10,8,512]{2,1,0:T(8,128)S(1)} %get-tuple-element.30), channel_id=1, source_target_pairs={{1,0},{2,1},{3,2},{4,3},{5,4},{6,5},{7,6},{8,7},{9,8},{10,9},{11,1... | collective-permute-start | bytes 491528 | tf_op jit(solution)/shard_map/ppermute | solution.py:404
  41.9 5.5 %collective-permute-start.2 = (f32[10,8,256]{2,1,0:T(8,128)S(1)}, f32[10,8,256]{2,1,0:T(8,128)S(1)}, u32[]{:S(2)}, u32[]{:S(2)}) collective-permute-start(f32[10,8,256]{2,1,0:T(8,128)S(1)} %get-tuple-element.34), channel_id=1, source_target_pairs={{0,1},{1,2},{2,3},{3,4},{4,5},{5,6},{6,7},{7,8},{8,9},{9,10},{10,1... | collective-permute-start | bytes 245768 | tf_op jit(solution)/shard_map/ppermute | solution.py:404
  45.9 7.4 %collective-permute-start.3 = (f32[10,8,256]{2,1,0:T(8,128)S(1)}, f32[10,8,256]{2,1,0:T(8,128)S(1)}, u32[]{:S(2)}, u32[]{:S(2)}) collective-permute-start(f32[10,8,256]{2,1,0:T(8,128)S(1)} %get-tuple-element.35), channel_id=1, source_target_pairs={{1,0},{2,1},{3,2},{4,3},{5,4},{6,5},{7,6},{8,7},{9,8},{10,9},{11,1... | collective-permute-start | bytes 245768 | tf_op jit(solution)/shard_map/ppermute | solution.py:404
  76.5 14.6 %all-to-all-start.1 = ((f32[8,96,128]{2,1,0:T(8,128)}), f32[8,96,128]{2,1,0:T(8,128)S(1)}, u32[]{:S(2)}, u32[]{:S(2)}) async-start(f32[8,96,128]{2,1,0:T(8,128)} %shard_map.42), calls=%async_computation.1 | async-start | bytes 786432 | tf_op jit(solution)/shard_map/all_to_all | solution.py:437
  91.2 8.3 %collective-permute-start.4 = (f32[6,96,128]{2,1,0:T(8,128)S(1)}, f32[6,96,128]{2,1,0:T(8,128)S(1)}, u32[]{:S(2)}, u32[]{:S(2)}) collective-permute-start(f32[6,96,128]{2,1,0:T(8,128)S(1)} %constant_dynamic-slice_fusion), channel_id=1, source_target_pairs={{12,96},{96,12},{36,120},{120,36},{60,144},{144,60},{84,168},{168,... | collective-permute-start | bytes 884744 | tf_op jit(solution)/shard_map/ppermute | solution.py:443

commit v2 on v1

--- a/solution.py
+++ b/solution.py
@@ -20,7 +20,7 @@
 
 def call(body, outs, scratch, where, *arrays, flops=1000000):
     many = isinstance(outs, list)
-    shapes = [jax.ShapeDtypeStruct(s, F32) for s in (outs if many else [outs])]
+    shapes = [pltpu.VMEM(s, F32) for s in (outs if many else [outs])]
     return pl.pallas_call(
         body,
         out_shape=shapes if many else shapes[0],
@@ -52,7 +52,9 @@
     last = c.shape[1] - 1
     full = harmonic(c, jnp.where(lane == last, 1.0, ahead(c, 1)))
     link = jnp.where(lane == last, 0.0, full)
-    first = jnp.where(lane == 0, harmonic(c, 1.0), 0.0)
+    first = jnp.where(iota((c.shape[0], 128), 1) == 0, harmonic(c[:, 0:128], 1.0), 0.0)
+    if c.shape[1] > 128:
+        first = jnp.concatenate([first, jnp.zeros((c.shape[0], c.shape[1] - 128), F32)], axis=1)
     return link, full + behind(link, 1) + first
 
 
@@ -64,16 +66,22 @@
 
 def pair_matrix(wide):
     shape = (wide, wide // 2)
-    return (lax.shift_right_logical(iota(shape, 0), 1) == iota(shape, 1)).astype(F32)
+    return (lax.shift_right_logical(iota(shape, 0), 1) == iota(shape, 1)).astype(jnp.bfloat16)
 
 
 def copy_matrix(narrow):
     shape = (narrow, narrow * 2)
-    return (iota(shape, 0) == lax.shift_right_logical(iota(shape, 1), 1)).astype(F32)
-
-
-def dot(a, b):
-    return jnp.dot(a, b, precision=lax.Precision.HIGHEST, preferred_element_type=F32)
+    return (iota(shape, 0) == lax.shift_right_logical(iota(shape, 1), 1)).astype(jnp.bfloat16)
+
+
+def dot(a, ones):
+    total = None
+    for _ in range(3):
+        part = a.astype(jnp.bfloat16)
+        a = a - part.astype(F32)
+        term = jnp.dot(part, ones, preferred_element_type=F32)
+        total = term if total is None else total + term
+    return total
 
 
 def pair_rows(s, x, start, count):
@@ -97,65 +105,101 @@
     return jnp.logical_and(at >= 0, at < count)
 
 
-def k_conduct(div, density, zones, out):
+def k_conduct(div, density, zones, out, dens, zone_ids, sems):
+    loads = []
     for z in range(4):
-        zone = zones[z]
+        loads.append(pltpu.make_async_copy(density.at[z], dens.at[z], sems.at[0, z]))
+        loads.append(pltpu.make_async_copy(zones.at[z], zone_ids.at[z], sems.at[1, z]))
+    loads += [pltpu.make_async_copy(div.at[z], out.at[1, z], sems.at[2, z]) for z in range(4)]
+    for load in loads:
+        load.start()
+    for z in range(4):
+        loads[2 * z].wait()
+        loads[2 * z + 1].wait()
+        zone = zone_ids[z]
         perm = jnp.where(zone == 0, PERMEABILITY[0], 0.0)
         for zone_id in range(1, 5):
             perm = jnp.where(zone == zone_id, PERMEABILITY[zone_id], perm)
-        out[0, z] = perm / density[z]
-        out[1, z] = div[z]
-
-
-def k_rows0(where, own, core, link, cond, div, left, right):
+        out[0, z] = perm / dens[z]
+    for load in loads[8:]:
+        load.wait()
+
+
+def conductance(divergence, density, zones):
+    shape = divergence.shape
+    return pl.pallas_call(
+        k_conduct,
+        out_shape=pltpu.VMEM((2,) + shape, F32),
+        in_specs=[pl.BlockSpec(memory_space=pl.ANY)] * 3,
+        out_specs=vmem(1)[0],
+        scratch_shapes=[pltpu.VMEM(shape, F32), pltpu.VMEM(shape, jnp.int32), pltpu.SemaphoreType.DMA((3, 4))],
+    )(divergence, density, zones)
+
+
+def stack0(where, own, core, link, put):
     h, high = where[0], where[2]
     odd = lax.rem(h, 2)
-    cond[4:8] = own[0]
-    div[4:8] = own[1]
+    for z in range(4, 8):
+        put(z, own, z - 4, None)
 
     @pl.when(odd == 0)
     def _():
-        cond[0:4] = link[0, 0]
-        div[0:4] = link[0, 1]
-        cond[8:12] = core[1, 0]
-        div[8:12] = core[1, 1]
+        for z in range(4):
+            put(z, link, z, h == 0)
+            put(z + 8, core.at[1], z, None)
 
     @pl.when(odd == 1)
     def _():
-        cond[0:4] = core[0, 0]
-        div[0:4] = core[0, 1]
-        cond[8:12] = link[1, 0]
-        div[8:12] = link[1, 1]
-
-    @pl.when(h == 0)
-    def _():
-        cond[0:4] = jnp.ones((4, 16, 512), F32)
-
-    @pl.when(h == high - 1)
-    def _():
-        cond[8:12] = jnp.ones((4, 16, 512), F32)
-
-    for z in range(10):
-        left[z, 0:4] = cond[z + 1, 0:4]
-        left[z, 4:8] = div[z + 1, 0:4]
-        right[z, 0:4] = cond[z + 1, 12:16]
-        right[z, 4:8] = div[z + 1, 12:16]
-
-
-def k_level0(where, cond, div, low, high, pre, w_out, g_out, cx_out, cy_out, cz_out, pack, c, g, w, cx, cy, cz, dg, p, rs, c1, st):
+        for z in range(4):
+            put(z, core.at[0], z, None)
+            put(z + 8, link, z, h == high - 1)
+
+
+MESSAGE0 = (
+    (4, 0, 0, 4, 3), (5, 1, 0, 4, 3), (6, 2, 0, 4, 3), (7, 3, 0, 4, 3),
+    (3, 4, 0, 3, 2), (2, 4, 5, 2, 1), (8, 5, 0, 3, 2), (9, 5, 5, 2, 1),
+    (1, 0, 7, 1, 0), (10, 3, 7, 1, 0),
+)
+
+
+def k_edges0(where, own, core, link, left, right):
+    places = {m[0]: m[1:] for m in MESSAGE0}
+
+    def put(z, block, layer, outside):
+        if z not in places:
+            return
+        group, at, n_cond, n_div = places[z]
+        for to, cond_first, div_first in ((left, 0, 0), (right, 16 - n_cond, 16 - n_div)):
+            rows = block[0, layer, cond_first : cond_first + n_cond]
+            to[group, at : at + n_cond] = rows if outside is None else jnp.where(outside, 1.0, rows)
+            if n_div:
+                to[group, at + n_cond : at + n_cond + n_div] = block[1, layer, div_first : div_first + n_div]
+
+    for group in range(1, 3):
+        left[group, 7:8] = jnp.zeros((1, 512), F32)
+        right[group, 7:8] = jnp.zeros((1, 512), F32)
+    stack0(where, own, core, link, put)
+
+
+def k_level0(where, own, core, near, low, high, pre, w_out, g_out, cx_out, cy_out, cz_out, pack, c, g, w, cx, cy, cz, dg, p, rs, c1, st):
     h, plan, n_h, n_p = where[0], where[1], where[2], where[3]
+
+    def put(z, block, layer, outside):
+        c[z, 4:20] = block[0, layer] if outside is None else jnp.where(outside, 1.0, block[0, layer])
+        g[z, 4:20] = block[1, layer]
+
+    stack0(where, own, core, near, put)
     for z in range(12):
-        c[z, 4:20] = cond[z]
-        if 1 <= z <= 10:
-            c[z, 0:4] = jnp.where(plan == 0, 1.0, low[z - 1, 0:4])
-            c[z, 20:24] = jnp.where(plan == n_p - 1, 1.0, high[z - 1, 0:4])
-        else:
-            c[z, 0:4] = jnp.ones((4, 512), F32)
-            c[z, 20:24] = jnp.ones((4, 512), F32)
-    for z in range(1, 11):
-        g[z, 4:20] = div[z]
-        g[z, 0:4] = low[z - 1, 4:8]
-        g[z, 20:24] = high[z - 1, 4:8]
+        for first in (0, 20):
+            c[z, first : first + 4] = jnp.ones((4, 512), F32)
+            g[z, first : first + 4] = jnp.zeros((4, 512), F32)
+    for z, group, at, n_cond, n_div in MESSAGE0:
+        mid, end = at + n_cond, at + n_cond + n_div
+        c[z, 4 - n_cond : 4] = jnp.where(plan == 0, 1.0, low[group, at:mid])
+        c[z, 20 : 20 + n_cond] = jnp.where(plan == n_p - 1, 1.0, high[group, at:mid])
+        if n_div:
+            g[z, 4 - n_div : 4] = low[group, mid:end]
+            g[z, 20 : 20 + n_div] = high[group, mid:end]
     row = iota((24, 512), 0) + (plan * 16 - 4)
     row_in = jnp.logical_and(row >= 0, row < n_p * 16).astype(F32) * OMEGA
     for z in range(11):
@@ -211,42 +255,44 @@
         pack[z, 8:16] = c1[z, 2:10, 0:256]
 
 
-def k_rows1(where, chip, link, third, g, c, left, right, s):
+def layers1(chip, two):
+    below = [two.at[0, 1, z] for z in range(2)] + [two.at[0, 0, z] for z in range(2)]
+    above = [two.at[1, 0, z] for z in range(2)] + [two.at[1, 1, z] for z in range(2)]
+    return below + [chip.at[z] for z in range(4)] + above
+
+
+def k_edges1(where, chip, two, edge):
     h, high = where[0], where[2]
     odd = lax.rem(h, 2)
-
-    @pl.when(odd == 0)
-    def _():
-        s[0:4] = link[0]
-        s[4:8] = chip[...]
-        s[8:10] = third[1]
-
-    @pl.when(odd == 1)
-    def _():
-        s[0:2] = third[0]
-        s[2:6] = chip[...]
-        s[6:10] = link[1]
+    for side in range(2):
+
+        @pl.when(odd == side)
+        def _():
+            for z, rows in enumerate(layers1(chip, two)):
+                keep = inside((h - side) * 2 - 4, z, high * 2)
+                edge[z, 0:4] = jnp.where(keep, rows[4 * side : 4 * side + 4], 0.0)
+                edge[z, 4:8] = jnp.where(keep, rows[4 * side + 8 : 4 * side + 12], 1.0)
+
+
+def k_level1(where, chip, two, sides, pre, w_out, g_out, cx_out, cy_out, cz_out, copies, c, g, w, cx, cy, cz, dg, rs, st):
+    h, plan, n_h, n_p = where[0], where[1], where[2], where[3]
+
+    odd = lax.rem(h, 2)
+    for side in range(2):
+
+        @pl.when(odd == side)
+        def _():
+            for z, rows in enumerate(layers1(chip, two)[2 * side : 2 * side + 10]):
+                keep = inside(h * 2 - 4, z, n_h * 2)
+                g[z, 4:12] = jnp.where(keep, rows[0:8], 0.0)
+                c[z, 4:12] = jnp.where(keep, rows[8:16], 1.0)
 
     for z in range(10):
-        keep = inside(h * 2 - 4, z, high * 2)
-        g[z] = jnp.where(keep, s[z, 0:8], 0.0)
-        c[z] = jnp.where(keep, s[z, 8:16], 1.0)
-    for z in range(10):
-        left[z, 0:4] = g[z, 0:4]
-        left[z, 4:8] = c[z, 0:4]
-        right[z, 0:4] = g[z, 4:8]
-        right[z, 4:8] = c[z, 4:8]
-
-
-def k_level1(where, g_in, c_in, low, high, pre, w_out, g_out, cx_out, cy_out, cz_out, copies, c, g, w, cx, cy, cz, dg, rs, st):
-    h, plan, n_h, n_p = where[0], where[1], where[2], where[3]
-    for z in range(10):
-        g[z, 4:12] = g_in[z]
-        c[z, 4:12] = c_in[z]
-        g[z, 0:4] = jnp.where(plan == 0, 0.0, low[z, 0:4])
-        c[z, 0:4] = jnp.where(plan == 0, 1.0, low[z, 4:8])
-        g[z, 12:16] = jnp.where(plan == n_p - 1, 0.0, high[z, 0:4])
-        c[z, 12:16] = jnp.where(plan == n_p - 1, 1.0, high[z, 4:8])
+        low, high = sides[0, 2 * odd + z], sides[1, 2 * odd + z]
+        g[z, 0:4] = jnp.where(plan == 0, 0.0, low[0:4])
+        c[z, 0:4] = jnp.where(plan == 0, 1.0, low[4:8])
+        g[z, 12:16] = jnp.where(plan == n_p - 1, 0.0, high[0:4])
+        c[z, 12:16] = jnp.where(plan == n_p - 1, 1.0, high[4:8])
     row = iota((16, 256), 0) + (plan * 8 - 4)
     row_in = jnp.logical_and(row >= 0, row < n_p * 8).astype(F32) * OMEGA
     for z in range(9):
@@ -296,22 +342,17 @@
         copies[i, 4:8] = tile_c
 
 
-def k_wide(tiles, copies):
-    n = tiles.shape[0]
-    for t in range(n):
-        copies[0, 4 * t : 4 * t + 4] = tiles[t, 0:4]
-        copies[0, 4 * n + 4 * t : 4 * n + 4 * t + 4] = tiles[t, 4:8]
-    for i in range(1, copies.shape[0]):
-        copies[i] = copies[0]
-
-
-def k_up(where, block, outer, pre1, w1, g1, cx1, cy1, cz1, pre0, w0, g0, cx0, cy0, cz0, out, s, c, g, w, cx, cy, cz, dg, pa, pb, p2, u1, q1, u0, q0, s1, s0):
+def k_up(where, block, outer, pre1, w1, g1, cx1, cy1, cz1, pre0, w0, g0, cx0, cy0, cz0, out, sems, s, c, g, w, cx, cy, cz, dg, pa, pb, p2, u1, q1, u0, q0, s1, s0, done):
     h, plan, n_h = where[0], where[1], where[2]
     wide = s.shape[1] // 2
-    s[0:6] = outer[0]
-    s[6:14] = block[...]
-    s[14:20] = outer[1]
-    q = lax.rem(h, 8)
+    tiles = wide // 4
+    for z in range(14):
+        for t in range(tiles):
+            at = tiles * (z % 2) + t
+            rows = block.at[at] if 6 <= z < 8 else outer.at[z // 8, z % 8 // 2 if z < 6 else (z - 8) // 2, at]
+            s[z, 4 * t : 4 * t + 4] = rows[0:4]
+            s[z, wide + 4 * t : wide + 4 * t + 4] = rows[4:8]
+    q = lax.rem(h, 2)
     for z in range(13):
         keep = inside(h - 6, z, n_h)
         g[z] = jnp.where(keep, s[q + z, 0:wide], 0.0)
@@ -323,7 +364,8 @@
         here = c[z]
         full = harmonic(here, jnp.where(row == wide - 1, 1.0, ahead(here, 0)))
         fx = jnp.where(row == wide - 1, 0.0, full)
-        first = jnp.where(row == 0, harmonic(here, 1.0), 0.0)
+        first = jnp.where(row[0:8] == 0, harmonic(here[0:8], 1.0), 0.0)
+        first = jnp.concatenate([first, jnp.zeros((wide - 8, 128), F32)], axis=0)
         link, both = y_faces(here)
         diag = cz[z - 1] + cz[z] + full + behind(fx, 0) + first + both
         cx[z] = fx
@@ -380,11 +422,16 @@
         here = q0[z - 2]
         total = spread(here, q0[z - 3], q0[z - 1], cz0[z - 3], cz0[z - 2], cx0[z - 3], cy0[z - 3])
         u0[z - 3, 0:24] = here * (1.0 / 3.0) + g0[z - 3] + w0[z - 3] * total
+    stores = []
     for z in range(4, 8):
         here = u0[z - 3, 0:24]
         total = spread(here, u0[z - 4, 0:24], u0[z - 2, 0:24], cz0[z - 3], cz0[z - 2], cx0[z - 3], cy0[z - 3])
         q0[z - 4] = here * (1.0 / 3.0) + g0[z - 3] + w0[z - 3] * total
-        out[z - 4] = q0[z - 4, 4:20]
+        done[z - 4] = q0[z - 4, 4:20]
+        stores.append(pltpu.make_async_copy(done.at[z - 4], out.at[z - 4], sems.at[z - 4]))
+        stores[-1].start()
+    for store in stores:
+        store.wait()
 
 
 def on_device(divergence, density, zones):
@@ -403,11 +450,11 @@
         down = [(i + 1, i) for i in range(n_p - 1)]
         return lax.ppermute(high_rows, "plan", up), lax.ppermute(low_rows, "plan", down)
 
-    own = call(k_conduct, (2, 4, 16, 512), [], None, divergence, density, zones)
+    own = conductance(divergence, density, zones)
+    swap = [(i, i + 1) for i in range(1, n_h - 1, 2)] + [(i + 1, i) for i in range(1, n_h - 1, 2)]
+    near = lax.ppermute(own, "height", swap)
     core = pair(own, cores)
-    link = pair(own, links)
-    tall = (12, 16, 512)
-    cond, div, left, right = call(k_rows0, [tall, tall, (10, 8, 512), (10, 8, 512)], [], where, own, core, link)
+    left, right = call(k_edges0, [(6, 8, 512)] * 2, [], where, own, core, near)
     low, high = beside(left, right)
     box = (12, 24, 512)
     eight, six, seven = (8, 24, 512), (6, 24, 512), (7, 24, 512)
@@ -415,39 +462,44 @@
         k_level0,
         [eight, six, six, six, six, seven, (2, 16, 256)],
         [box] * 6 + [(4, 24, 512), box, (4, 24, 512), (4, 16, 512), (10, 4, 24, 128)],
-        where, cond, div, low, high,
+        where, own, core, near, low, high,
     )
+    near = lax.ppermute(pack, "height", swap)
+    skip = [(i, i + 2) for i in range(0, n_h - 2, 2)] + [(i + 2, i) for i in range(1, n_h - 2, 2)]
+    beyond = lax.ppermute(pack, "height", skip)
     chip = pair(pack, cores).reshape(4, 16, 256)
-    link = pair(chip, links)
-    third = pair(jnp.where(odd == 0, link[0, 2:4], link[1, 0:2]), cores)
-    g1, c1, left, right = call(k_rows1, [(10, 8, 256)] * 4, [(10, 16, 256)], where, chip, link, third)
-    low, high = beside(left, right)
+    two = pair(jnp.stack([near, beyond]), cores)
+    edge = call(k_edges1, (12, 8, 256), [], where, chip, two)
+    across = [[(2 * i + 1) * n_p + t, 2 * i * n_p + (t + 1) % n_p] for i in range(n_h // 2) for t in range(n_p)]
+    edge = lax.all_gather(edge, ("height", "plan"), axis=0, tiled=False, axis_index_groups=across)
+    sides = pair(lax.dynamic_index_in_dim(edge, odd, 0, keepdims=False), cores)
     box = (10, 16, 256)
     eight, six, seven = (8, 16, 256), (6, 16, 256), (7, 16, 256)
     *level1, tiles = call(
         k_level1,
-        [eight, six, six, six, six, seven, (n_p, 8, 128)],
+        [eight, six, six, six, six, seven, (2 * n_p, 8, 128)],
         [box] * 6 + [(2, 16, 256), (2, 16, 256), (4, 2, 16, 128)],
-        where, g1, c1, low, high,
+        where, chip, two, sides,
     )
-    tiles = lax.all_to_all(tiles, "plan", split_axis=0, concat_axis=0, tiled=True)
+    groups = [[(2 * i + k) * n_p + t for k in range(2) for t in range(n_p)] for i in range(n_h // 2)]
+    block = lax.all_to_all(tiles, ("height", "plan"), split_axis=0, concat_axis=0, tiled=True, axis_index_groups=groups)
+    near = pair(block, links)
+    far = pair(near, [[i, (i + 5) % n_h] for i in range(1, n_h, 2)])
+    side = jnp.where(odd == 0, jnp.concatenate([far[0], near[0:1]]), jnp.concatenate([near[1:2], far[1]]))
+    outer = pair(side, cores)
     wide = n_p * 4
-    block = call(k_wide, (8, 2 * wide, 128), [], None, tiles)
-    rows = [[8 * y + i for i in range(8)] for y in range(n_h // 8)]
-    block = lax.all_to_all(block, "height", split_axis=0, concat_axis=0, tiled=True, axis_index_groups=rows)
-    cross = []
-    for y in range(n_h // 8 - 1):
-        for i in range(0, 8, 2):
-            cross += [(8 * y + i + 1, 8 * y + 8 + i), (8 * y + 8 + i, 8 * y + i + 1)]
-    part = lax.dynamic_slice_in_dim(block, 2 * odd, 6, 0)
-    outer = pair(lax.ppermute(part, "height", cross), cores)
     flat = (13, wide, 128)
-    return call(
+    arrays = (block, outer, *level1, *level0)
+    scratch = [(14, 2 * wide, 128)] + [flat] * 9
+    scratch += [(5, wide + 16, 128), (5, 16, 256), (8, 16, 256), (6, 32, 512), (8, 24, 512), (5, 2, 16, 128), (4, 4, 32, 128), (4, 16, 512)]
+    return pl.pallas_call(
         k_up,
-        (4, 16, 512),
-        [(20, 2 * wide, 128)] + [flat] * 9 + [(5, wide + 16, 128), (5, 16, 256), (8, 16, 256), (6, 32, 512), (8, 24, 512), (5, 2, 16, 128), (4, 4, 32, 128)],
-        where, block, outer, *level1, *level0,
-    )
+        out_shape=jax.ShapeDtypeStruct((4, 16, 512), F32),
+        in_specs=[smem()] + vmem(len(arrays)),
+        out_specs=pl.BlockSpec(memory_space=pl.ANY),
+        scratch_shapes=[pltpu.SemaphoreType.DMA((4,))] + [pltpu.VMEM(s, F32) for s in scratch],
+        compiler_params=pltpu.CompilerParams(vmem_limit_bytes=40 << 20),
+    )(where, *arrays)
 
 
 def solution(mesh):

time: 107 us -> 98.2 us (0.918)
  starting transfers between devices: 19 us -> 27.4 us
  waiting for transfers between devices: 26 us -> 18.3 us
  blocking collectives: 49.7 us -> 42.2 us
  local copies, waits for them, and re-layouts: 2.73 us -> 0.05 us
    all_to_all x1 -> x0, blocking collectives: 21.2 us -> none  [on_device(): lax.all_to_all(tiles, 'plan', split_axis=0, concat_axis=0, tiled=True)]
    ppermute x1 -> x3, starting transfers between devices: 1.92 us -> 13.2 us  [the longest x1 7.56 us: on_device(): beyond = lax.ppermute(pack, 'height', skip)]
    all_gather x6 -> x7, blocking collectives: 28.4 us -> 36.9 us  [pair(): lax.all_gather(x, 'height', axis=0, tiled=False, axis_index_groups=groups)]
    ppermute x2 -> x1, waiting for transfers between devices: 10.4 us -> 4.38 us  [beside(): lax.ppermute(low_rows, 'plan', down)]
    all_gather x0 -> x1, blocking collectives: none -> 5.29 us  [on_device(): lax.all_gather(edge, ('height', 'plan'), axis=0, tiled=False, axis_index_...]
    pallas_call x0 -> x2, Pallas kernels: none -> 4.43 us  [the longest x1 3.39 us: on_device(): pl.pallas_call(k_up, out_shape=jax.ShapeDtypeStruct((4, 16, 512), F32), i...]
    ppermute x2 -> x1, starting transfers between devices: 8.01 us -> 4 us  [beside(): lax.ppermute(high_rows, 'plan', up)]
    pallas_call x7 -> x4, Pallas kernels: 8.91 us -> 5.18 us  [call(): pl.pallas_call(body, out_shape=shapes if many else shapes[0], in_specs=([...]
  transfers between devices with their start and end apart: 6 -> 6, of which waited for: 6 -> 5; matrix products, arithmetic and copies ran while one was open for 0% -> 0% of each run, Pallas kernels for 0% -> 0%
where the time goes in v2:
time: 98.2 us; the launch traced here: 97.8 us
  blocking collectives  42.2 us (43%)
  starting transfers between devices  27.4 us (28%)
  waiting for transfers between devices  18.3 us (19%)
  Pallas kernels  9.61 us (10%)
    all_gather x7, blocking collectives, pair(): lax.all_gather(x, 'height', axis=0, tiled=False, axis_index_groups=groups)  36.9 us
    all_to_all x1, waiting for transfers between devices, on_device(): lax.all_to_all(tiles, ('height', 'plan'), split_axis=0, concat_axis=0, ti...  10.7 us
    all_to_all x1, starting transfers between devices, on_device(): lax.all_to_all(tiles, ('height', 'plan'), split_axis=0, concat_axis=0, ti...  8.96 us
    ppermute x1, starting transfers between devices, on_device(): beyond = lax.ppermute(pack, 'height', skip)  7.56 us
    all_gather x1, blocking collectives, on_device(): lax.all_gather(edge, ('height', 'plan'), axis=0, tiled=False, axis_index_...  5.29 us
    pallas_call x4, Pallas kernels, call(): pl.pallas_call(body, out_shape=shapes if many else shapes[0], in_specs=([...  5.18 us
    ppermute x1, waiting for transfers between devices, beside(): lax.ppermute(low_rows, 'plan', down)  4.38 us
    ppermute x1, starting transfers between devices, beside(): lax.ppermute(high_rows, 'plan', up)  4 us
  transfers between devices with their start and end apart: 6, of which 5 were waited for; matrix products, arithmetic and copies ran while one was open for 0% of the time, Pallas kernels for 0%

profile of v2, /device:TPU:33, one launch (start us, length us, event | category | flops | bytes accessed | tf_op | source)
XLA Modules:
  0.0 97.8 jit_solution(11089640872190475268)
XLA Ops:
  0.0 1.0 %shard_map.37.own = f32[2,4,16,512]{3,2,1,0:T(8,128)S(1)} custom-call(f32[4,16,512]{2,1,0:T(8,128)} %div.1, f32[4,16,512]{2,1,0:T(8,128)} %density.1, s32[4,16,512]{2,1,0:T(8,128)} %zones.1), custom_call_target="tpu_custom_call" | custom-call | tf_op jit(solution)/shard_map/pallas_call | solution.py:130
  1.0 3.7 %collective-permute-start = (f32[2,4,16,512]{3,2,1,0:T(8,128)S(1)}, f32[2,4,16,512]{3,2,1,0:T(8,128)S(1)}, u32[]{:S(2)}, u32[]{:S(2)}) collective-permute-start(f32[2,4,16,512]{3,2,1,0:T(8,128)S(1)} %shard_map.37.own), channel_id=1, source_target_pairs={{12,24},{36,48},{60,72},{84,96},{108,120},{132,144},{156,168},{180... | collective-permute-start | bytes 786440 | tf_op jit(solution)/shard_map/ppermute | solution.py:455
  4.7 0.1 pad_add_fusion.where
  4.8 2.8 %all-gather = f32[4,4,16,512]{3,2,1,0:T(8,128)S(1)} all-gather(f32[2,4,16,512]{3,2,1,0:T(8,128)S(1)} %shard_map.37.own), channel_id=2, replica_groups={{0,12},{24,36},{48,60},{72,84},{96,108},{120,132},{144,156},{168,180},{..., dimensions={0}, use_global_device_ids=true | all-gather | bytes 786432 | tf_op jit(solution)/shard_map/all_gather | solution.py:446
  7.6 1.2 %collective-permute-done.link.near = f32[2,4,16,512]{3,2,1,0:T(8,128)S(1)} collective-permute-done((f32[2,4,16,512]{3,2,1,0:T(8,128)S(1)}, f32[2,4,16,512]{3,2,1,0:T(8,128)S(1)}, u32[]{:S(2)}, u32[]{:S(2)}) %collective-permute-start) | collective-permute-done | bytes 262176 | tf_op jit(solution)/shard_map/ppermute | solution.py:455
  8.8 0.6 shard_map.38
  9.4 4.0 %collective-permute-start.1 = (f32[6,8,512]{2,1,0:T(8,128)S(1)}, f32[6,8,512]{2,1,0:T(8,128)S(1)}, u32[]{:S(2)}, u32[]{:S(2)}) collective-permute-start(f32[6,8,512]{2,1,0:T(8,128)S(1)} %get-tuple-element.21), channel_id=1, source_target_pairs={{0,1},{1,2},{2,3},{3,4},{4,5},{5,6},{6,7},{7,8},{8,9},{9,10},{10,1... | collective-permute-start | bytes 294920 | tf_op jit(solution)/shard_map/ppermute | solution.py:451
  13.4 1.3 %collective-permute-start.2 = (f32[6,8,512]{2,1,0:T(8,128)S(1)}, f32[6,8,512]{2,1,0:T(8,128)S(1)}, u32[]{:S(2)}, u32[]{:S(2)}) collective-permute-start(f32[6,8,512]{2,1,0:T(8,128)S(1)} %get-tuple-element.22), channel_id=1, source_target_pairs={{1,0},{2,1},{3,2},{4,3},{5,4},{6,5},{7,6},{8,7},{9,8},{10,9},{11,1... | collective-permute-start | bytes 294920 | tf_op jit(solution)/shard_map/ppermute | solution.py:451
  14.7 0.3 collective-permute-done.1.low
  15.0 4.4 %collective-permute-done.2.high = f32[6,8,512]{2,1,0:T(8,128)S(1)} collective-permute-done((f32[6,8,512]{2,1,0:T(8,128)S(1)}, f32[6,8,512]{2,1,0:T(8,128)S(1)}, u32[]{:S(2)}, u32[]{:S(2)}) %collective-permute-start.2) | collective-permute-done | bytes 98336 | tf_op jit(solution)/shard_map/ppermute | solution.py:451
  19.4 2.2 %shard_map.39 = (f32[8,24,512]{2,1,0:T(8,128)S(1)}, f32[6,24,512]{2,1,0:T(8,128)S(1)}, f32[6,24,512]{2,1,0:T(8,128)S(1)}, f32[6,24,512]{2,1,0:T(8,128)S(1)}, f32...) custom-call(s32[4]{0:T(128)S(1)} %pad_add_fusion.where, ...), custom_call_target="tpu_custom_call" | custom-call | tf_op jit(solution)/shard_map/pallas_call | solution.py:24
  21.6 7.6 %collective-permute-start.4 = (f32[2,16,256]{2,1,0:T(8,128)S(1)}, f32[2,16,256]{2,1,0:T(8,128)S(1)}, u32[]{:S(2)}, u32[]{:S(2)}) collective-permute-start(f32[2,16,256]{2,1,0:T(8,128)S(1)} %get-tuple-element.23), channel_id=1, source_target_pairs={{0,24},{24,48},{48,72},{72,96},{96,120},{120,144},{144,168},{168,1... | collective-permute-start | bytes 98312 | tf_op jit(solution)/shard_map/ppermute | solution.py:469
  29.1 1.9 %collective-permute-start.3 = (f32[2,16,256]{2,1,0:T(8,128)S(1)}, f32[2,16,256]{2,1,0:T(8,128)S(1)}, u32[]{:S(2)}, u32[]{:S(2)}) collective-permute-start(f32[2,16,256]{2,1,0:T(8,128)S(1)} %get-tuple-element.23), channel_id=1, source_target_pairs={{12,24},{36,48},{60,72},{84,96},{108,120},{132,144},{156,168},{180... | collective-permute-start | bytes 98312 | tf_op jit(solution)/shard_map/ppermute | solution.py:467
  31.1 1.9 %all-gather.1.chip = f32[4,16,256]{2,1,0:T(8,128)S(1)} all-gather(f32[2,16,256]{2,1,0:T(8,128)S(1)} %get-tuple-element.23), channel_id=3, replica_groups={{0,12},{24,36},{48,60},{72,84},{96,108},{120,132},{144,156},{168,180},{..., dimensions={0}, use_global_device_ids=true | all-gather | bytes 98304 | tf_op jit(solution)/shard_map/all_gather | solution.py:446
  33.0 0.0 collective-permute-done.4
  33.0 1.7 %collective-permute-done.3 = f32[2,16,256]{2,1,0:T(8,128)S(1)} collective-permute-done((f32[2,16,256]{2,1,0:T(8,128)S(1)}, f32[2,16,256]{2,1,0:T(8,128)S(1)}, u32[]{:S(2)}, u32[]{:S(2)}) %collective-permute-start.3) | collective-permute-done | bytes 32800 | tf_op jit(solution)/shard_map/ppermute | solution.py:467
  34.7 4.0 %all-gather.2 = f32[4,2,16,256]{3,2,1,0:T(8,128)S(1)} all-gather(f32[2,2,16,256]{3,2,1,0:T(8,128)S(1)} %pad_maximum_fusion), channel_id=4, replica_groups={{0,12},{24,36},{48,60},{72,84},{96,108},{120,132},{144,156},{168,180},{..., dimensions={0}, use_global_device_ids=true | all-gather | bytes 196608 | tf_op jit(solution)/shard_map/all_gather | solution.py:446
  38.7 0.6 shard_map.40
  39.3 5.3 %all-gather.3 = f32[24,8,256]{2,1,0:T(8,128)S(1)} all-gather(f32[12,8,256]{2,1,0:T(8,128)S(1)} %shard_map.40), channel_id=5, replica_groups={{12,1},{13,2},{14,3},{15,4},{16,5},{17,6},{18,7},{19,8},{20,9},{21,10},..., dimensions={0}, use_global_device_ids=true | all-gather | bytes 294912 | tf_op jit(solution)/shard_map/all_gather | solution.py:474
  44.6 8.9 %all_gather.52.sides = f32[2,12,8,256]{3,2,1,0:T(8,128)S(1)} all-gather(f32[1,12,8,256]{3,2,1,0:T(8,128)S(1)} %constant_dynamic-slice_fusion), channel_id=1, replica_groups={{0,12},{24,36},{48,60},{72,84},{96,108},{120,132},{144,156},{168,180},{..., dimensions={0}, use_global_device_ids=true | all-gather | bytes 294912 | tf_op jit(solution)/shard_map/all_gather | solution.py:446
  53.5 1.8 %shard_map.41 = (f32[8,16,256]{2,1,0:T(8,128)S(1)}, f32[6,16,256]{2,1,0:T(8,128)S(1)}, f32[6,16,256]{2,1,0:T(8,128)S(1)}, f32[6,16,256]{2,1,0:T(8,128)S(1)}, f32...) custom-call(s32[4]{0:T(128)S(1)} %pad_add_fusion.where, ...), custom_call_target="tpu_custom_call" | custom-call | tf_op jit(solution)/shard_map/pallas_call | solution.py:24
  55.4 9.0 %all-to-all-start = ((f32[24,8,128]{2,1,0:T(8,128)}), f32[24,8,128]{2,1,0:T(8,128)S(1)}, u32[]{:S(2)}, u32[]{:S(2)}) async-start(f32[24,8,128]{2,1,0:T(8,128)} %get-tuple-element.24), calls=%async_computation | async-start | bytes 196608 | tf_op jit(solution)/shard_map/all_to_all | solution.py:485
  64.3 10.7 %all-to-all-done.block = f32[24,8,128]{2,1,0:T(8,128)S(1)} async-done(((f32[24,8,128]{2,1,0:T(8,128)}), f32[24,8,128]{2,1,0:T(8,128)S(1)}, u32[]{:S(2)}, u32[]{:S(2)}) %all-to-all-start) | async-done | bytes 98336 | tf_op jit(solution)/shard_map/all_to_all | solution.py:485
  75.0 4.7 %all-gather.4 = f32[48,8,128]{2,1,0:T(8,128)S(1)} all-gather(f32[24,8,128]{2,1,0:T(8,128)S(1)} %all-to-all-done.block), channel_id=6, replica_groups={{12,24},{36,48},{60,72},{84,96},{108,120},{132,144},{156,168},{180,192}..., dimensions={0}, use_global_device_ids=true | all-gather | bytes 294912 | tf_op jit(solution)/shard_map/all_gather | solution.py:446
  79.8 7.0 %all-gather.5 = f32[4,24,8,128]{3,2,1,0:T(8,128)S(1)} all-gather(f32[2,24,8,128]{3,2,1,0:T(8,128)S(1)} %bitcast.20), channel_id=7, replica_groups={{12,72},{36,96},{60,120},{84,144},{108,168},{132,192},{156,216},{180,24..., dimensions={0}, use_global_device_ids=true | all-gather | bytes 589824 | tf_op jit(solution)/shard_map/all_gather | solution.py:446
  86.8 7.5 %all_gather.57.outer = f32[2,3,24,8,128]{4,3,2,1,0:T(8,128)S(1)} all-gather(f32[1,3,24,8,128]{4,3,2,1,0:T(8,128)S(1)} %maximum_select_fusion), channel_id=1, replica_groups={{0,12},{24,36},{48,60},{72,84},{96,108},{120,132},{144,156},{168,180},{..., dimensions={0}, use_global_device_ids=true | all-gather | bytes 884736 | tf_op jit(solution)/shard_map/all_gather | solution.py:446
  94.4 3.4 %shard_map.42 = f32[4,16,512]{2,1,0:T(8,128)} custom-call(s32[4]{0:T(128)S(1)} %pad_add_fusion.where, f32[24,8,128]{2,1,0:T(8,128)S(1)} %all-to-all-done.block, f32[2,3,24,8,128]{4,3,2,1,0:T(8,128)S(1)} %all_gather.57.outer, f32[8,16,256]{2,1,0:T(8,128)S(1)} %get-tuple-element.25.pre1, f32[6,16,256]{2,1,0:T(8,128)S(1)} %get-tuple-element.26.w1, ...), custom_call_target="tpu_custom_call" | custom-call | tf_op jit(solution)/shard_map/pallas_call | solution.py:495
  (5 shorter events, 0.1 us)
Async XLA Ops:
  1.0 7.7 %collective-permute-start = (f32[2,4,16,512]{3,2,1,0:T(8,128)S(1)}, f32[2,4,16,512]{3,2,1,0:T(8,128)S(1)}, u32[]{:S(2)}, u32[]{:S(2)}) collective-permute-start(f32[2,4,16,512]{3,2,1,0:T(8,128)S(1)} %shard_map.37.own), channel_id=1, source_target_pairs={{12,24},{36,48},{60,72},{84,96},{108,120},{132,144},{156,168},{180... | collective-permute-start | bytes 786440 | tf_op jit(solution)/shard_map/ppermute | solution.py:455
  9.4 5.6 %collective-permute-start.1 = (f32[6,8,512]{2,1,0:T(8,128)S(1)}, f32[6,8,512]{2,1,0:T(8,128)S(1)}, u32[]{:S(2)}, u32[]{:S(2)}) collective-permute-start(f32[6,8,512]{2,1,0:T(8,128)S(1)} %get-tuple-element.21), channel_id=1, source_target_pairs={{0,1},{1,2},{2,3},{3,4},{4,5},{5,6},{6,7},{7,8},{8,9},{9,10},{10,1... | collective-permute-start | bytes 294920 | tf_op jit(solution)/shard_map/ppermute | solution.py:451
  13.4 6.0 %collective-permute-start.2 = (f32[6,8,512]{2,1,0:T(8,128)S(1)}, f32[6,8,512]{2,1,0:T(8,128)S(1)}, u32[]{:S(2)}, u32[]{:S(2)}) collective-permute-start(f32[6,8,512]{2,1,0:T(8,128)S(1)} %get-tuple-element.22), channel_id=1, source_target_pairs={{1,0},{2,1},{3,2},{4,3},{5,4},{6,5},{7,6},{8,7},{9,8},{10,9},{11,1... | collective-permute-start | bytes 294920 | tf_op jit(solution)/shard_map/ppermute | solution.py:451
  21.6 11.4 %collective-permute-start.4 = (f32[2,16,256]{2,1,0:T(8,128)S(1)}, f32[2,16,256]{2,1,0:T(8,128)S(1)}, u32[]{:S(2)}, u32[]{:S(2)}) collective-permute-start(f32[2,16,256]{2,1,0:T(8,128)S(1)} %get-tuple-element.23), channel_id=1, source_target_pairs={{0,24},{24,48},{48,72},{72,96},{96,120},{120,144},{144,168},{168,1... | collective-permute-start | bytes 98312 | tf_op jit(solution)/shard_map/ppermute | solution.py:469
  29.1 5.5 %collective-permute-start.3 = (f32[2,16,256]{2,1,0:T(8,128)S(1)}, f32[2,16,256]{2,1,0:T(8,128)S(1)}, u32[]{:S(2)}, u32[]{:S(2)}) collective-permute-start(f32[2,16,256]{2,1,0:T(8,128)S(1)} %get-tuple-element.23), channel_id=1, source_target_pairs={{12,24},{36,48},{60,72},{84,96},{108,120},{132,144},{156,168},{180... | collective-permute-start | bytes 98312 | tf_op jit(solution)/shard_map/ppermute | solution.py:467
  55.4 19.7 %all-to-all-start = ((f32[24,8,128]{2,1,0:T(8,128)}), f32[24,8,128]{2,1,0:T(8,128)S(1)}, u32[]{:S(2)}, u32[]{:S(2)}) async-start(f32[24,8,128]{2,1,0:T(8,128)} %get-tuple-element.24), calls=%async_computation | async-start | bytes 196608 | tf_op jit(solution)/shard_map/all_to_all | solution.py:485

commit v3 on v2

--- a/solution.py
+++ b/solution.py
@@ -14,21 +14,21 @@
     return [pl.BlockSpec(memory_space=pltpu.VMEM)] * count
 
 
-def smem():
-    return pl.BlockSpec(memory_space=pltpu.SMEM)
-
-
-def call(body, outs, scratch, where, *arrays, flops=1000000):
+def position():
+    return lax.axis_index("height"), lax.axis_index("plan"), lax.axis_size("height"), lax.axis_size("plan")
+
+
+def call(body, outs, scratch, *arrays):
     many = isinstance(outs, list)
     shapes = [pltpu.VMEM(s, F32) for s in (outs if many else [outs])]
     return pl.pallas_call(
         body,
         out_shape=shapes if many else shapes[0],
-        in_specs=([] if where is None else [smem()]) + vmem(len(arrays)),
+        in_specs=vmem(len(arrays)),
         out_specs=vmem(len(shapes)) if many else vmem(1)[0],
         scratch_shapes=[pltpu.VMEM(s, F32) for s in scratch],
         compiler_params=pltpu.CompilerParams(vmem_limit_bytes=40 << 20),
-    )(*(() if where is None else (where,)), *arrays)
+    )(*arrays)
 
 
 def harmonic(a, b):
@@ -136,8 +136,8 @@
     )(divergence, density, zones)
 
 
-def stack0(where, own, core, link, put):
-    h, high = where[0], where[2]
+def stack0(own, core, link, put):
+    h, _, high, _ = position()
     odd = lax.rem(h, 2)
     for z in range(4, 8):
         put(z, own, z - 4, None)
@@ -155,51 +155,44 @@
             put(z + 8, link, z, h == high - 1)
 
 
-MESSAGE0 = (
-    (4, 0, 0, 4, 3), (5, 1, 0, 4, 3), (6, 2, 0, 4, 3), (7, 3, 0, 4, 3),
-    (3, 4, 0, 3, 2), (2, 4, 5, 2, 1), (8, 5, 0, 3, 2), (9, 5, 5, 2, 1),
-    (1, 0, 7, 1, 0), (10, 3, 7, 1, 0),
-)
-
-
-def k_edges0(where, own, core, link, left, right):
-    places = {m[0]: m[1:] for m in MESSAGE0}
-
-    def put(z, block, layer, outside):
-        if z not in places:
-            return
-        group, at, n_cond, n_div = places[z]
-        for to, cond_first, div_first in ((left, 0, 0), (right, 16 - n_cond, 16 - n_div)):
-            rows = block[0, layer, cond_first : cond_first + n_cond]
-            to[group, at : at + n_cond] = rows if outside is None else jnp.where(outside, 1.0, rows)
-            if n_div:
-                to[group, at + n_cond : at + n_cond + n_div] = block[1, layer, div_first : div_first + n_div]
-
-    for group in range(1, 3):
-        left[group, 7:8] = jnp.zeros((1, 512), F32)
-        right[group, 7:8] = jnp.zeros((1, 512), F32)
-    stack0(where, own, core, link, put)
-
-
-def k_level0(where, own, core, near, low, high, pre, w_out, g_out, cx_out, cy_out, cz_out, pack, c, g, w, cx, cy, cz, dg, p, rs, c1, st):
-    h, plan, n_h, n_p = where[0], where[1], where[2], where[3]
+def k_edges0(core, edge):
+    odd = lax.rem(lax.axis_index("height"), 2)
+    for side in range(2):
+
+        @pl.when(odd == side)
+        def _():
+            for z in range(8):
+                edge[z, 0:4] = core[z // 4, 0, z % 4, 12 * side : 12 * side + 4]
+                edge[z, 4:7] = core[z // 4, 1, z % 4, 13 * side : 13 * side + 3]
+                edge[z, 7:8] = jnp.zeros((1, 512), F32)
+
+
+def k_level0(own, core, near, sides, corner, pre, w_out, g_out, cx_out, cy_out, cz_out, pack, c, g, w, cx, cy, cz, dg, p, rs, c1, st):
+    h, plan, n_h, n_p = position()
 
     def put(z, block, layer, outside):
         c[z, 4:20] = block[0, layer] if outside is None else jnp.where(outside, 1.0, block[0, layer])
         g[z, 4:20] = block[1, layer]
 
-    stack0(where, own, core, near, put)
+    stack0(own, core, near, put)
     for z in range(12):
         for first in (0, 20):
             c[z, first : first + 4] = jnp.ones((4, 512), F32)
             g[z, first : first + 4] = jnp.zeros((4, 512), F32)
-    for z, group, at, n_cond, n_div in MESSAGE0:
-        mid, end = at + n_cond, at + n_cond + n_div
-        c[z, 4 - n_cond : 4] = jnp.where(plan == 0, 1.0, low[group, at:mid])
-        c[z, 20 : 20 + n_cond] = jnp.where(plan == n_p - 1, 1.0, high[group, at:mid])
-        if n_div:
-            g[z, 4 - n_div : 4] = low[group, mid:end]
-            g[z, 20 : 20 + n_div] = high[group, mid:end]
+    odd = lax.rem(h, 2)
+    for par in range(2):
+
+        @pl.when(odd == par)
+        def _():
+            for z in range(1, 11):
+                inner = z < 8 if par else z >= 4
+                at = z if par else z - 4
+                for side, first, end in ((0, 0, plan == 0), (1, 20, plan == n_p - 1)):
+                    rows = sides.at[side, at] if inner else corner.at[par, side, z - 8 if par else z - 1]
+                    out = end if inner else jnp.logical_or(end, h == (n_h - 1 if par else 0))
+                    c[z, first : first + 4] = jnp.where(out, 1.0, rows[0:4])
+                    g[z, first + 1 - side : first + 4 - side] = rows[4:7]
+
     row = iota((24, 512), 0) + (plan * 16 - 4)
     row_in = jnp.logical_and(row >= 0, row < n_p * 16).astype(F32) * OMEGA
     for z in range(11):
@@ -255,66 +248,61 @@
         pack[z, 8:16] = c1[z, 2:10, 0:256]
 
 
-def layers1(chip, two):
-    below = [two.at[0, 1, z] for z in range(2)] + [two.at[0, 0, z] for z in range(2)]
-    above = [two.at[1, 0, z] for z in range(2)] + [two.at[1, 1, z] for z in range(2)]
-    return below + [chip.at[z] for z in range(4)] + above
-
-
-def k_edges1(where, chip, two, edge):
-    h, high = where[0], where[2]
-    odd = lax.rem(h, 2)
+def k_edges1(chip, edge):
+    odd = lax.rem(lax.axis_index("height"), 2)
     for side in range(2):
 
         @pl.when(odd == side)
         def _():
-            for z, rows in enumerate(layers1(chip, two)):
-                keep = inside((h - side) * 2 - 4, z, high * 2)
-                edge[z, 0:4] = jnp.where(keep, rows[4 * side : 4 * side + 4], 0.0)
-                edge[z, 4:8] = jnp.where(keep, rows[4 * side + 8 : 4 * side + 12], 1.0)
-
-
-def k_level1(where, chip, two, sides, pre, w_out, g_out, cx_out, cy_out, cz_out, copies, c, g, w, cx, cy, cz, dg, rs, st):
-    h, plan, n_h, n_p = where[0], where[1], where[2], where[3]
-
-    odd = lax.rem(h, 2)
-    for side in range(2):
-
-        @pl.when(odd == side)
+            for z in range(4):
+                edge[z, 0:4] = chip[z, 4 * side : 4 * side + 4]
+                edge[z, 4:8] = chip[z, 4 * side + 8 : 4 * side + 12]
+
+
+def window1(even_layers, odd_layers, first, g, c):
+    h, plan, n_h, n_p = position()
+    for side, layers in ((0, even_layers), (1, odd_layers)):
+
+        @pl.when(lax.rem(h, 2) == side)
         def _():
-            for z, rows in enumerate(layers1(chip, two)[2 * side : 2 * side + 10]):
-                keep = inside(h * 2 - 4, z, n_h * 2)
+            for z, rows in enumerate(layers):
+                keep = inside(first, z, n_h * 2)
+                low, high = jnp.logical_and(keep, plan > 0), jnp.logical_and(keep, plan < n_p - 1)
                 g[z, 4:12] = jnp.where(keep, rows[0:8], 0.0)
                 c[z, 4:12] = jnp.where(keep, rows[8:16], 1.0)
-
-    for z in range(10):
-        low, high = sides[0, 2 * odd + z], sides[1, 2 * odd + z]
-        g[z, 0:4] = jnp.where(plan == 0, 0.0, low[0:4])
-        c[z, 0:4] = jnp.where(plan == 0, 1.0, low[4:8])
-        g[z, 12:16] = jnp.where(plan == n_p - 1, 0.0, high[0:4])
-        c[z, 12:16] = jnp.where(plan == n_p - 1, 1.0, high[4:8])
+                g[z, 0:4] = jnp.where(low, rows[16:20], 0.0)
+                c[z, 0:4] = jnp.where(low, rows[20:24], 1.0)
+                g[z, 12:16] = jnp.where(high, rows[24:28], 0.0)
+                c[z, 12:16] = jnp.where(high, rows[28:32], 1.0)
+
+
+def couple1(count, first, c, w, cx, cy, cz):
+    h, plan, n_h, n_p = position()
     row = iota((16, 256), 0) + (plan * 8 - 4)
     row_in = jnp.logical_and(row >= 0, row < n_p * 8).astype(F32) * OMEGA
-    for z in range(9):
+    for z in range(count - 1):
         cz[z] = harmonic(c[z], c[z + 1])
-    for z in range(1, 9):
+    diags = {}
+    for z in range(1, count - 1):
         here = c[z]
         fx = harmonic(here, ahead(here, 0))
         link, both = y_faces(here)
-        diag = cz[z - 1] + cz[z] + fx + behind(fx, 0) + both
+        diags[z] = cz[z - 1] + cz[z] + fx + behind(fx, 0) + both
         cx[z] = fx
         cy[z] = link
-        w[z] = jnp.where(inside(h * 2 - 4, z, n_h * 2), row_in, 0.0) / diag
-        if 4 <= z <= 5:
-            dg[z - 4] = diag
+        w[z] = jnp.where(inside(first, z, n_h * 2), row_in, 0.0) / diags[z]
+    return diags
+
+
+def k_level1_wide(full, two, pre, w_out, g_out, cx_out, cy_out, cz_out, c, g, w, cx, cy, cz):
+    first = lax.axis_index("height") * 2 - 4
+    layers = [two.at[0, z] for z in range(4)] + [full.at[z] for z in range(4)] + [two.at[1, z] for z in range(4)]
+    window1(layers[0:10], layers[2:12], first, g, c)
+    couple1(10, first, c, w, cx, cy, cz)
     for z in range(1, 9):
         here = g[z]
         total = spread(here, g[z - 1], g[z + 1], cz[z - 1], cz[z], cx[z], cy[z])
         pre[z - 1] = here * (1.0 / 3.0) + here + w[z] * total
-    for z in range(4, 6):
-        here = pre[z - 1]
-        total = spread(here, pre[z - 2], pre[z], cz[z - 1], cz[z], cx[z], cy[z])
-        rs[z - 4] = (g[z] - OMEGA * here + w[z] * total) * dg[z - 4] * 1.5
     for z in range(2, 8):
         w_out[z - 2] = w[z]
         g_out[z - 2] = g[z]
@@ -322,8 +310,25 @@
         cy_out[z - 2] = cy[z]
     for z in range(1, 8):
         cz_out[z - 1] = cz[z]
+
+
+def k_level1(full, near, copies, c, g, w, cx, cy, cz, p, rs, dg, st):
+    first = lax.axis_index("height") * 2 - 2
+    middle = [full.at[z] for z in range(4)]
+    window1([near.at[0, 2], near.at[0, 3]] + middle, middle + [near.at[1, 0], near.at[1, 1]], first, g, c)
+    diags = couple1(6, first, c, w, cx, cy, cz)
+    for z in range(2):
+        rs[z] = diags[z + 2]
+    for z in range(1, 5):
+        here = g[z]
+        total = spread(here, g[z - 1], g[z + 1], cz[z - 1], cz[z], cx[z], cy[z])
+        p[z] = here * (1.0 / 3.0) + here + w[z] * total
+    for z in range(2, 4):
+        here = p[z]
+        total = spread(here, p[z - 1], p[z + 1], cz[z - 1], cz[z], cx[z], cy[z])
+        rs[z - 2] = (g[z] - OMEGA * here + w[z] * total) * rs[z - 2] * 1.5
     rows = [pair_rows(st.at[0], rs[0] + rs[1], 0, 8)]
-    rows += [pair_rows(st.at[z + 1], c[2 * z + 2] + c[2 * z + 3], 0, 8) for z in range(3)]
+    rows += [pair_rows(st.at[z + 1], c[2 * z] + c[2 * z + 1], 0, 8) for z in range(3)]
     pairs = pair_matrix(256)
     both = jnp.concatenate(rows, axis=0)
     down = dot(both, pairs)
@@ -342,8 +347,8 @@
         copies[i, 4:8] = tile_c
 
 
-def k_up(where, block, outer, pre1, w1, g1, cx1, cy1, cz1, pre0, w0, g0, cx0, cy0, cz0, out, sems, s, c, g, w, cx, cy, cz, dg, pa, pb, p2, u1, q1, u0, q0, s1, s0, done):
-    h, plan, n_h = where[0], where[1], where[2]
+def k_up(block, outer, pre1, w1, g1, cx1, cy1, cz1, pre0, w0, g0, cx0, cy0, cz0, out, sems, s, c, g, w, cx, cy, cz, dg, pa, pb, p2, u1, q1, u0, q0, s1, s0, done):
+    h, plan, n_h, _ = position()
     wide = s.shape[1] // 2
     tiles = wide // 4
     for z in range(14):
@@ -436,51 +441,43 @@
 
 def on_device(divergence, density, zones):
     n_h, n_p = lax.axis_size("height"), lax.axis_size("plan")
-    h, plan = lax.axis_index("height"), lax.axis_index("plan")
-    odd = lax.rem(h, 2)
-    where = jnp.stack([h, plan, jnp.int32(n_h), jnp.int32(n_p)])
+    odd = lax.rem(lax.axis_index("height"), 2)
     cores = [[i, i + 1] for i in range(0, n_h, 2)]
     links = [[i, (i + 1) % n_h] for i in range(1, n_h, 2)]
 
     def pair(x, groups):
         return lax.all_gather(x, "height", axis=0, tiled=False, axis_index_groups=groups)
-
-    def beside(low_rows, high_rows):
-        up = [(i, i + 1) for i in range(n_p - 1)]
-        down = [(i + 1, i) for i in range(n_p - 1)]
-        return lax.ppermute(high_rows, "plan", up), lax.ppermute(low_rows, "plan", down)
 
     own = conductance(divergence, density, zones)
     swap = [(i, i + 1) for i in range(1, n_h - 1, 2)] + [(i + 1, i) for i in range(1, n_h - 1, 2)]
     near = lax.ppermute(own, "height", swap)
     core = pair(own, cores)
-    left, right = call(k_edges0, [(6, 8, 512)] * 2, [], where, own, core, near)
-    low, high = beside(left, right)
+    across = [[(2 * i + 1) * n_p + t, 2 * i * n_p + (t + 1) % n_p] for i in range(n_h // 2) for t in range(n_p)]
+
+    def both_sides(edge):
+        met = lax.all_gather(edge, ("height", "plan"), axis=0, tiled=False, axis_index_groups=across)
+        return pair(lax.dynamic_index_in_dim(met, odd, 0, keepdims=False), cores)
+
+    sides = both_sides(call(k_edges0, (8, 8, 512), [], core))
+    corner = pair(lax.dynamic_slice_in_dim(sides, 5 * odd, 3, 1), links)
     box = (12, 24, 512)
     eight, six, seven = (8, 24, 512), (6, 24, 512), (7, 24, 512)
     *level0, pack = call(
         k_level0,
         [eight, six, six, six, six, seven, (2, 16, 256)],
         [box] * 6 + [(4, 24, 512), box, (4, 24, 512), (4, 16, 512), (10, 4, 24, 128)],
-        where, own, core, near, low, high,
+        own, core, near, sides, corner,
     )
-    near = lax.ppermute(pack, "height", swap)
-    skip = [(i, i + 2) for i in range(0, n_h - 2, 2)] + [(i + 2, i) for i in range(1, n_h - 2, 2)]
-    beyond = lax.ppermute(pack, "height", skip)
     chip = pair(pack, cores).reshape(4, 16, 256)
-    two = pair(jnp.stack([near, beyond]), cores)
-    edge = call(k_edges1, (12, 8, 256), [], where, chip, two)
-    across = [[(2 * i + 1) * n_p + t, 2 * i * n_p + (t + 1) % n_p] for i in range(n_h // 2) for t in range(n_p)]
-    edge = lax.all_gather(edge, ("height", "plan"), axis=0, tiled=False, axis_index_groups=across)
-    sides = pair(lax.dynamic_index_in_dim(edge, odd, 0, keepdims=False), cores)
+    sides = both_sides(call(k_edges1, (4, 8, 256), [], chip))
+    full = jnp.concatenate([chip, sides[0], sides[1]], axis=1)
+    near = pair(full, links)
+    box = (6, 16, 256)
+    tiles = call(k_level1, (2 * n_p, 8, 128), [box] * 7 + [(2, 16, 256), (2, 16, 256), (4, 2, 16, 128)], full, near)
+    two = pair(lax.dynamic_index_in_dim(near, odd, 0, keepdims=False), cores)
     box = (10, 16, 256)
     eight, six, seven = (8, 16, 256), (6, 16, 256), (7, 16, 256)
-    *level1, tiles = call(
-        k_level1,
-        [eight, six, six, six, six, seven, (2 * n_p, 8, 128)],
-        [box] * 6 + [(2, 16, 256), (2, 16, 256), (4, 2, 16, 128)],
-        where, chip, two, sides,
-    )
+    level1 = call(k_level1_wide, [eight, six, six, six, six, seven], [box] * 6, full, two)
     groups = [[(2 * i + k) * n_p + t for k in range(2) for t in range(n_p)] for i in range(n_h // 2)]
     block = lax.all_to_all(tiles, ("height", "plan"), split_axis=0, concat_axis=0, tiled=True, axis_index_groups=groups)
     near = pair(block, links)
@@ -495,11 +492,11 @@
     return pl.pallas_call(
         k_up,
         out_shape=jax.ShapeDtypeStruct((4, 16, 512), F32),
-        in_specs=[smem()] + vmem(len(arrays)),
+        in_specs=vmem(len(arrays)),
         out_specs=pl.BlockSpec(memory_space=pl.ANY),
         scratch_shapes=[pltpu.SemaphoreType.DMA((4,))] + [pltpu.VMEM(s, F32) for s in scratch],
         compiler_params=pltpu.CompilerParams(vmem_limit_bytes=40 << 20),
-    )(where, *arrays)
+    )(*arrays)
 
 
 def solution(mesh):

time: 98.2 us -> 92.7 us (0.944)
  the two profiles are of different devices: /device:TPU:33 before, /device:TPU:1 now
where the time goes in v3:
time: 92.7 us; the launch traced here: 92.4 us
  blocking collectives  63.2 us (68%)
  starting transfers between devices  13.5 us (15%)
  waiting for transfers between devices  8.33 us (9%)
  Pallas kernels  7.15 us (8%)
    all_gather x10, blocking collectives, pair(): lax.all_gather(x, 'height', axis=0, tiled=False, axis_index_groups=groups)  53.8 us
    all_gather x2, blocking collectives, both_sides(): lax.all_gather(edge, ('height', 'plan'), axis=0, tiled=False, axis_index_...  9.37 us
    all_to_all x1, starting transfers between devices, on_device(): lax.all_to_all(tiles, ('height', 'plan'), split_axis=0, concat_axis=0, ti...  8.97 us
    all_to_all x1, waiting for transfers between devices, on_device(): lax.all_to_all(tiles, ('height', 'plan'), split_axis=0, concat_axis=0, ti...  8.33 us
    ppermute x1, starting transfers between devices, on_device(): near = lax.ppermute(own, 'height', swap)  4.51 us
    pallas_call x5, Pallas kernels, call(): pl.pallas_call(body, out_shape=shapes if many else shapes[0], in_specs=vm...  3.31 us
    pallas_call x1, Pallas kernels, on_device(): pl.pallas_call(k_up, out_shape=jax.ShapeDtypeStruct((4, 16, 512), F32), i...  2.8 us
  transfers between devices with their start and end apart: 2, of which 1 were waited for; matrix products, arithmetic and copies ran while one was open for 0% of the time, Pallas kernels for 0%

profile of v3, /device:TPU:1, one launch (start us, length us, event | category | flops | bytes accessed | tf_op | source)
XLA Modules:
  0.0 92.4 jit_solution(4050829793554888884)
XLA Ops:
  0.0 1.0 %shard_map.37.own = f32[2,4,16,512]{3,2,1,0:T(8,128)S(1)} custom-call(f32[4,16,512]{2,1,0:T(8,128)} %div.1, f32[4,16,512]{2,1,0:T(8,128)} %density.1, s32[4,16,512]{2,1,0:T(8,128)} %zones.1), custom_call_target="tpu_custom_call" | custom-call | tf_op jit(solution)/shard_map/pallas_call | solution.py:130
  1.0 4.5 %collective-permute-start = (f32[2,4,16,512]{3,2,1,0:T(8,128)S(1)}, f32[2,4,16,512]{3,2,1,0:T(8,128)S(1)}, u32[]{:S(2)}, u32[]{:S(2)}) collective-permute-start(f32[2,4,16,512]{3,2,1,0:T(8,128)S(1)} %shard_map.37.own), channel_id=1, source_target_pairs={{12,24},{36,48},{60,72},{84,96},{108,120},{132,144},{156,168},{180... | collective-permute-start | bytes 786440 | tf_op jit(solution)/shard_map/ppermute | solution.py:453
  5.6 8.5 %all-gather = f32[4,4,16,512]{3,2,1,0:T(8,128)S(1)} all-gather(f32[2,4,16,512]{3,2,1,0:T(8,128)S(1)} %shard_map.37.own), channel_id=2, replica_groups={{0,12},{24,36},{48,60},{72,84},{96,108},{120,132},{144,156},{168,180},{..., dimensions={0}, use_global_device_ids=true | all-gather | bytes 786432 | tf_op jit(solution)/shard_map/all_gather | solution.py:449
  14.1 5.1 %all-gather.1 = f32[16,8,512]{2,1,0:T(8,128)S(1)} all-gather(f32[8,8,512]{2,1,0:T(8,128)S(1)} %shard_map.38), channel_id=3, replica_groups={{12,1},{13,2},{14,3},{15,4},{16,5},{17,6},{18,7},{19,8},{20,9},{21,10},..., dimensions={0}, use_global_device_ids=true | all-gather | bytes 393216 | tf_op jit(solution)/shard_map/all_gather | solution.py:458
  19.2 6.4 %all_gather.68.sides = f32[2,8,8,512]{3,2,1,0:T(8,128)S(1)} all-gather(f32[1,8,8,512]{3,2,1,0:T(8,128)S(1)} %constant_dynamic-slice_fusion.3), channel_id=1, replica_groups={{0,12},{24,36},{48,60},{72,84},{96,108},{120,132},{144,156},{168,180},{..., dimensions={0}, use_global_device_ids=true | all-gather | bytes 393216 | tf_op jit(solution)/shard_map/all_gather | solution.py:449
  25.5 4.7 %all-gather.2 = f32[4,3,8,512]{3,2,1,0:T(8,128)S(1)} all-gather(f32[2,3,8,512]{3,2,1,0:T(8,128)S(1)} %constant_dynamic-slice_fusion.2), channel_id=4, replica_groups={{12,24},{36,48},{60,72},{84,96},{108,120},{132,144},{156,168},{180,192}..., dimensions={0}, use_global_device_ids=true | all-gather | bytes 294912 | tf_op jit(solution)/shard_map/all_gather | solution.py:449
  30.3 0.0 collective-permute-done.near
  30.3 1.7 %shard_map.39 = (f32[8,24,512]{2,1,0:T(8,128)S(1)}, f32[6,24,512]{2,1,0:T(8,128)S(1)}, f32[6,24,512]{2,1,0:T(8,128)S(1)}, f32[6,24,512]{2,1,0:T(8,128)S(1)}, f32...) custom-call(f32[2,4,16,512]{3,2,1,0:T(8,128)S(1)} %shard_map.37.own, ...), custom_call_target="tpu_custom_call" | custom-call | tf_op jit(solution)/shard_map/pallas_call | solution.py:24
  31.9 5.2 %all-gather.3.chip = f32[4,16,256]{2,1,0:T(8,128)S(1)} all-gather(f32[2,16,256]{2,1,0:T(8,128)S(1)} %get-tuple-element.18), channel_id=5, replica_groups={{0,12},{24,36},{48,60},{72,84},{96,108},{120,132},{144,156},{168,180},{..., dimensions={0}, use_global_device_ids=true | all-gather | bytes 98304 | tf_op jit(solution)/shard_map/all_gather | solution.py:449
  37.1 4.3 %all-gather.4 = f32[8,8,256]{2,1,0:T(8,128)S(1)} all-gather(f32[4,8,256]{2,1,0:T(8,128)S(1)} %shard_map.40), channel_id=6, replica_groups={{12,1},{13,2},{14,3},{15,4},{16,5},{17,6},{18,7},{19,8},{20,9},{21,10},..., dimensions={0}, use_global_device_ids=true | all-gather | bytes 98304 | tf_op jit(solution)/shard_map/all_gather | solution.py:458
  41.4 2.8 %all_gather.75 = f32[2,4,8,256]{3,2,1,0:T(8,128)S(1)} all-gather(f32[1,4,8,256]{3,2,1,0:T(8,128)S(1)} %constant_dynamic-slice_fusion.1), channel_id=1, replica_groups={{0,12},{24,36},{48,60},{72,84},{96,108},{120,132},{144,156},{168,180},{..., dimensions={0}, use_global_device_ids=true | all-gather | bytes 98304 | tf_op jit(solution)/shard_map/all_gather | solution.py:449
  44.2 5.1 %all-gather.5 = f32[8,32,256]{2,1,0:T(8,128)S(1)} all-gather(f32[4,32,256]{2,1,0:T(8,128)S(1)} %pad_maximum_fusion.full), channel_id=7, replica_groups={{12,24},{36,48},{60,72},{84,96},{108,120},{132,144},{156,168},{180,192}..., dimensions={0}, use_global_device_ids=true | all-gather | bytes 393216 | tf_op jit(solution)/shard_map/all_gather | solution.py:449
  49.3 1.3 %shard_map.41 = f32[24,8,128]{2,1,0:T(8,128)} custom-call(f32[4,32,256]{2,1,0:T(8,128)S(1)} %pad_maximum_fusion.full, f32[2,4,32,256]{3,2,1,0:T(8,128)S(1)} %bitcast.20), custom_call_target="tpu_custom_call" | custom-call | tf_op jit(solution)/shard_map/pallas_call | solution.py:24
  50.6 9.0 %all-to-all-start = ((f32[24,8,128]{2,1,0:T(8,128)}), f32[24,8,128]{2,1,0:T(8,128)S(1)}, u32[]{:S(2)}, u32[]{:S(2)}) async-start(f32[24,8,128]{2,1,0:T(8,128)} %shard_map.41), calls=%async_computation | async-start | bytes 196608 | tf_op jit(solution)/shard_map/all_to_all | solution.py:482
  59.6 2.0 %all_gather.83.two = f32[2,4,32,256]{3,2,1,0:T(8,128)S(1)} all-gather(f32[1,4,32,256]{3,2,1,0:T(8,128)S(1)} %constant_dynamic-slice_fusion), channel_id=1, replica_groups={{0,12},{24,36},{48,60},{72,84},{96,108},{120,132},{144,156},{168,180},{..., dimensions={0}, use_global_device_ids=true | all-gather | bytes 393216 | tf_op jit(solution)/shard_map/all_gather | solution.py:449
  61.6 0.3 shard_map.42
  61.9 8.3 %all-to-all-done.block = f32[24,8,128]{2,1,0:T(8,128)S(1)} async-done(((f32[24,8,128]{2,1,0:T(8,128)}), f32[24,8,128]{2,1,0:T(8,128)S(1)}, u32[]{:S(2)}, u32[]{:S(2)}) %all-to-all-start) | async-done | bytes 98336 | tf_op jit(solution)/shard_map/all_to_all | solution.py:482
  70.3 4.7 %all-gather.6 = f32[48,8,128]{2,1,0:T(8,128)S(1)} all-gather(f32[24,8,128]{2,1,0:T(8,128)S(1)} %all-to-all-done.block), channel_id=8, replica_groups={{12,24},{36,48},{60,72},{84,96},{108,120},{132,144},{156,168},{180,192}..., dimensions={0}, use_global_device_ids=true | all-gather | bytes 294912 | tf_op jit(solution)/shard_map/all_gather | solution.py:449
  75.0 7.0 %all-gather.7 = f32[4,24,8,128]{3,2,1,0:T(8,128)S(1)} all-gather(f32[2,24,8,128]{3,2,1,0:T(8,128)S(1)} %bitcast.23), channel_id=9, replica_groups={{12,72},{36,96},{60,120},{84,144},{108,168},{132,192},{156,216},{180,24..., dimensions={0}, use_global_device_ids=true | all-gather | bytes 589824 | tf_op jit(solution)/shard_map/all_gather | solution.py:449
  82.0 7.5 %all_gather.82.outer = f32[2,3,24,8,128]{4,3,2,1,0:T(8,128)S(1)} all-gather(f32[1,3,24,8,128]{4,3,2,1,0:T(8,128)S(1)} %maximum_select_fusion), channel_id=1, replica_groups={{0,12},{24,36},{48,60},{72,84},{96,108},{120,132},{144,156},{168,180},{..., dimensions={0}, use_global_device_ids=true | all-gather | bytes 884736 | tf_op jit(solution)/shard_map/all_gather | solution.py:449
  89.6 2.8 %shard_map.43 = f32[4,16,512]{2,1,0:T(8,128)} custom-call(f32[24,8,128]{2,1,0:T(8,128)S(1)} %all-to-all-done.block, f32[2,3,24,8,128]{4,3,2,1,0:T(8,128)S(1)} %all_gather.82.outer, f32[8,16,256]{2,1,0:T(8,128)S(1)} %get-tuple-element.19.pre1, f32[6,16,256]{2,1,0:T(8,128)S(1)} %get-tuple-element.20.w1, f32[6,16,256]{2,1,0:T(8,128)S(1)} %get-tuple-element.21.g1, ...), custom_call_target="tpu_custom_call" | custom-call | tf_op jit(solution)/shard_map/pallas_call | solution.py:492
  (11 shorter events, 0.2 us)
Async XLA Ops:
  1.0 29.2 %collective-permute-start = (f32[2,4,16,512]{3,2,1,0:T(8,128)S(1)}, f32[2,4,16,512]{3,2,1,0:T(8,128)S(1)}, u32[]{:S(2)}, u32[]{:S(2)}) collective-permute-start(f32[2,4,16,512]{3,2,1,0:T(8,128)S(1)} %shard_map.37.own), channel_id=1, source_target_pairs={{12,24},{36,48},{60,72},{84,96},{108,120},{132,144},{156,168},{180... | collective-permute-start | bytes 786440 | tf_op jit(solution)/shard_map/ppermute | solution.py:453
  50.6 19.7 %all-to-all-start = ((f32[24,8,128]{2,1,0:T(8,128)}), f32[24,8,128]{2,1,0:T(8,128)S(1)}, u32[]{:S(2)}, u32[]{:S(2)}) async-start(f32[24,8,128]{2,1,0:T(8,128)} %shard_map.41), calls=%async_computation | async-start | bytes 196608 | tf_op jit(solution)/shard_map/all_to_all | solution.py:482

commit v4 on v3

--- a/solution.py
+++ b/solution.py
@@ -136,23 +136,23 @@
     )(divergence, density, zones)
 
 
-def stack0(own, core, link, put):
+def stack0(core, near, put):
     h, _, high, _ = position()
     odd = lax.rem(h, 2)
-    for z in range(4, 8):
-        put(z, own, z - 4, None)
 
     @pl.when(odd == 0)
     def _():
         for z in range(4):
-            put(z, link, z, h == 0)
-            put(z + 8, core.at[1], z, None)
+            put(z, near[0, z], near[0, 4 + z], h == 0)
+            put(z + 4, core[0, 0, z], core[0, 1, z], None)
+            put(z + 8, core[1, 0, z], core[1, 1, z], None)
 
     @pl.when(odd == 1)
     def _():
         for z in range(4):
-            put(z, core.at[0], z, None)
-            put(z + 8, link, z, h == high - 1)
+            put(z, core[0, 0, z], core[0, 1, z], None)
+            put(z + 4, core[1, 0, z], core[1, 1, z], None)
+            put(z + 8, near[1, z], near[1, 4 + z], h == high - 1)
 
 
 def k_edges0(core, edge):
@@ -167,14 +167,14 @@
                 edge[z, 7:8] = jnp.zeros((1, 512), F32)
 
 
-def k_level0(own, core, near, sides, corner, pre, w_out, g_out, cx_out, cy_out, cz_out, pack, c, g, w, cx, cy, cz, dg, p, rs, c1, st):
+def k_level0(core, near, sides, pre, w_out, g_out, cx_out, cy_out, cz_out, pack, c, g, w, cx, cy, cz, dg, p, rs, c1, st):
     h, plan, n_h, n_p = position()
 
-    def put(z, block, layer, outside):
-        c[z, 4:20] = block[0, layer] if outside is None else jnp.where(outside, 1.0, block[0, layer])
-        g[z, 4:20] = block[1, layer]
-
-    stack0(own, core, near, put)
+    def put(z, cond, div, outside):
+        c[z, 4:20] = cond if outside is None else jnp.where(outside, 1.0, cond)
+        g[z, 4:20] = div
+
+    stack0(core, near, put)
     for z in range(12):
         for first in (0, 20):
             c[z, first : first + 4] = jnp.ones((4, 512), F32)
@@ -188,7 +188,7 @@
                 inner = z < 8 if par else z >= 4
                 at = z if par else z - 4
                 for side, first, end in ((0, 0, plan == 0), (1, 20, plan == n_p - 1)):
-                    rows = sides.at[side, at] if inner else corner.at[par, side, z - 8 if par else z - 1]
+                    rows = sides.at[side, at] if inner else near.at[par, z if par else z + 7, pl.ds(8 * side, 8)]
                     out = end if inner else jnp.logical_or(end, h == (n_h - 1 if par else 0))
                     c[z, first : first + 4] = jnp.where(out, 1.0, rows[0:4])
                     g[z, first + 1 - side : first + 4 - side] = rows[4:7]
@@ -354,7 +354,7 @@
     for z in range(14):
         for t in range(tiles):
             at = tiles * (z % 2) + t
-            rows = block.at[at] if 6 <= z < 8 else outer.at[z // 8, z % 8 // 2 if z < 6 else (z - 8) // 2, at]
+            rows = block.at[at] if 6 <= z < 8 else outer.at[z // 8, z % 8 // 2, at]
             s[z, 4 * t : 4 * t + 4] = rows[0:4]
             s[z, wide + 4 * t : wide + 4 * t + 4] = rows[4:8]
     q = lax.rem(h, 2)
@@ -443,47 +443,55 @@
     n_h, n_p = lax.axis_size("height"), lax.axis_size("plan")
     odd = lax.rem(lax.axis_index("height"), 2)
     cores = [[i, i + 1] for i in range(0, n_h, 2)]
-    links = [[i, (i + 1) % n_h] for i in range(1, n_h, 2)]
-
-    def pair(x, groups):
-        return lax.all_gather(x, "height", axis=0, tiled=False, axis_index_groups=groups)
-
+
+    def reach(step, others):
+        pairs = [(i, i + step) for i in range(1, n_h - step, 2)] + others
+        ends = sorted(set(range(n_h)) - {i for both in pairs for i in both})
+        groups = [[i * n_p + t, j * n_p + t] for i, j in pairs for t in range(n_p)]
+        return groups + [[i * n_p + t, i * n_p + t + 1] for i in ends for t in range(0, n_p, 2)]
+
+    def meet(x, groups):
+        return lax.all_gather(x, ("height", "plan"), axis=0, tiled=False, axis_index_groups=groups)
+
+    def pair(x):
+        return lax.all_gather(x, "height", axis=0, tiled=False, axis_index_groups=cores)
+
+    links, leaps = reach(1, []), reach(5, [(0, 4), (n_h - 5, n_h - 1)])
     own = conductance(divergence, density, zones)
-    swap = [(i, i + 1) for i in range(1, n_h - 1, 2)] + [(i + 1, i) for i in range(1, n_h - 1, 2)]
-    near = lax.ppermute(own, "height", swap)
-    core = pair(own, cores)
+    core = pair(own)
     across = [[(2 * i + 1) * n_p + t, 2 * i * n_p + (t + 1) % n_p] for i in range(n_h // 2) for t in range(n_p)]
 
     def both_sides(edge):
-        met = lax.all_gather(edge, ("height", "plan"), axis=0, tiled=False, axis_index_groups=across)
-        return pair(lax.dynamic_index_in_dim(met, odd, 0, keepdims=False), cores)
+        return pair(lax.dynamic_index_in_dim(meet(edge, across), odd, 0, keepdims=False))
 
     sides = both_sides(call(k_edges0, (8, 8, 512), [], core))
-    corner = pair(lax.dynamic_slice_in_dim(sides, 5 * odd, 3, 1), links)
+    corner = lax.dynamic_slice_in_dim(sides, 5 * odd, 3, 1)
+    corner = jnp.concatenate([corner[0], corner[1]], axis=1)
+    near = meet(jnp.concatenate([own.reshape(8, 16, 512), corner], axis=0), links)
     box = (12, 24, 512)
     eight, six, seven = (8, 24, 512), (6, 24, 512), (7, 24, 512)
     *level0, pack = call(
         k_level0,
         [eight, six, six, six, six, seven, (2, 16, 256)],
         [box] * 6 + [(4, 24, 512), box, (4, 24, 512), (4, 16, 512), (10, 4, 24, 128)],
-        own, core, near, sides, corner,
+        core, near, sides,
     )
-    chip = pair(pack, cores).reshape(4, 16, 256)
+    chip = pair(pack).reshape(4, 16, 256)
     sides = both_sides(call(k_edges1, (4, 8, 256), [], chip))
     full = jnp.concatenate([chip, sides[0], sides[1]], axis=1)
-    near = pair(full, links)
+    near = meet(full, links)
     box = (6, 16, 256)
     tiles = call(k_level1, (2 * n_p, 8, 128), [box] * 7 + [(2, 16, 256), (2, 16, 256), (4, 2, 16, 128)], full, near)
-    two = pair(lax.dynamic_index_in_dim(near, odd, 0, keepdims=False), cores)
+    two = pair(lax.dynamic_index_in_dim(near, odd, 0, keepdims=False))
     box = (10, 16, 256)
     eight, six, seven = (8, 16, 256), (6, 16, 256), (7, 16, 256)
     level1 = call(k_level1_wide, [eight, six, six, six, six, seven], [box] * 6, full, two)
     groups = [[(2 * i + k) * n_p + t for k in range(2) for t in range(n_p)] for i in range(n_h // 2)]
     block = lax.all_to_all(tiles, ("height", "plan"), split_axis=0, concat_axis=0, tiled=True, axis_index_groups=groups)
-    near = pair(block, links)
-    far = pair(near, [[i, (i + 5) % n_h] for i in range(1, n_h, 2)])
+    near = meet(block, links)
+    far = meet(near, leaps)
     side = jnp.where(odd == 0, jnp.concatenate([far[0], near[0:1]]), jnp.concatenate([near[1:2], far[1]]))
-    outer = pair(side, cores)
+    outer = pair(side)
     wide = n_p * 4
     flat = (13, wide, 128)
     arrays = (block, outer, *level1, *level0)

time: 92.7 us -> 91.4 us (0.986)
  the two profiles are of different devices: /device:TPU:1 before, /device:TPU:33 now
where the time goes in v4:
time: 91.4 us; the launch traced here: 91 us
  blocking collectives  66.3 us (73%)
  starting transfers between devices  8.98 us (10%)
  waiting for transfers between devices  8.33 us (9%)
  Pallas kernels  7.15 us (8%)
    all_gather x6, blocking collectives, meet(): lax.all_gather(x, ('height', 'plan'), axis=0, tiled=False, axis_index_gro...  34.5 us
    all_gather x6, blocking collectives, pair(): lax.all_gather(x, 'height', axis=0, tiled=False, axis_index_groups=cores)  31.8 us
    all_to_all x1, starting transfers between devices, on_device(): lax.all_to_all(tiles, ('height', 'plan'), split_axis=0, concat_axis=0, ti...  8.98 us
    all_to_all x1, waiting for transfers between devices, on_device(): lax.all_to_all(tiles, ('height', 'plan'), split_axis=0, concat_axis=0, ti...  8.33 us
    pallas_call x5, Pallas kernels, call(): pl.pallas_call(body, out_shape=shapes if many else shapes[0], in_specs=vm...  3.31 us
    pallas_call x1, Pallas kernels, on_device(): pl.pallas_call(k_up, out_shape=jax.ShapeDtypeStruct((4, 16, 512), F32), i...  2.8 us
  transfers between devices with their start and end apart: 1, of which 1 were waited for; matrix products, arithmetic and copies ran while one was open for 0% of the time, Pallas kernels for 0%

profile of v4, /device:TPU:33, one launch (start us, length us, event | category | flops | bytes accessed | tf_op | source)
XLA Modules:
  0.0 91.0 jit_solution(17089958474027944742)
XLA Ops:
  0.0 1.0 %shard_map.37 = f32[2,4,16,512]{3,2,1,0:T(8,128)S(1)} custom-call(f32[4,16,512]{2,1,0:T(8,128)} %div.1, f32[4,16,512]{2,1,0:T(8,128)} %density.1, s32[4,16,512]{2,1,0:T(8,128)} %zones.1), custom_call_target="tpu_custom_call" | custom-call | tf_op jit(solution)/shard_map/pallas_call | solution.py:130
  1.0 2.5 %all-gather = f32[4,4,16,512]{3,2,1,0:T(8,128)S(1)} all-gather(f32[2,4,16,512]{3,2,1,0:T(8,128)S(1)} %shard_map.37), channel_id=2, replica_groups={{0,12},{24,36},{48,60},{72,84},{96,108},{120,132},{144,156},{168,180},{..., dimensions={0}, use_global_device_ids=true | all-gather | bytes 786432 | tf_op jit(solution)/shard_map/all_gather | solution.py:457
  3.6 5.7 %all-gather.1 = f32[16,8,512]{2,1,0:T(8,128)S(1)} all-gather(f32[8,8,512]{2,1,0:T(8,128)S(1)} %shard_map.38), channel_id=3, replica_groups={{12,1},{13,2},{14,3},{15,4},{16,5},{17,6},{18,7},{19,8},{20,9},{21,10},..., dimensions={0}, use_global_device_ids=true | all-gather | bytes 393216 | tf_op jit(solution)/shard_map/all_gather | solution.py:454
  9.2 12.1 %all_gather.68.sides = f32[2,8,8,512]{3,2,1,0:T(8,128)S(1)} all-gather(f32[1,8,8,512]{3,2,1,0:T(8,128)S(1)} %constant_dynamic-slice_fusion.2), channel_id=1, replica_groups={{0,12},{24,36},{48,60},{72,84},{96,108},{120,132},{144,156},{168,180},{..., dimensions={0}, use_global_device_ids=true | all-gather | bytes 393216 | tf_op jit(solution)/shard_map/all_gather | solution.py:457
  21.4 7.8 %all-gather.2 = f32[22,16,512]{2,1,0:T(8,128)S(1)} all-gather(f32[11,16,512]{2,1,0:T(8,128)S(1)} %maximum_maximum_fusion), channel_id=4, replica_groups={{12,24},{13,25},{14,26},{15,27},{16,28},{17,29},{18,30},{19,31},{20,32}..., dimensions={0}, use_global_device_ids=true | all-gather | bytes 1081344 | tf_op jit(solution)/shard_map/all_gather | solution.py:454
  29.2 1.7 %shard_map.39 = (f32[8,24,512]{2,1,0:T(8,128)S(1)}, f32[6,24,512]{2,1,0:T(8,128)S(1)}, f32[6,24,512]{2,1,0:T(8,128)S(1)}, f32[6,24,512]{2,1,0:T(8,128)S(1)}, f32...) custom-call(f32[2,2,4,16,512]{4,3,2,1,0:T(8,128)S(1)} %bitcast.24, ...), custom_call_target="tpu_custom_call" | custom-call | tf_op jit(solution)/shard_map/pallas_call | solution.py:24
  30.8 4.9 %all-gather.3.chip = f32[4,16,256]{2,1,0:T(8,128)S(1)} all-gather(f32[2,16,256]{2,1,0:T(8,128)S(1)} %get-tuple-element.18), channel_id=5, replica_groups={{0,12},{24,36},{48,60},{72,84},{96,108},{120,132},{144,156},{168,180},{..., dimensions={0}, use_global_device_ids=true | all-gather | bytes 98304 | tf_op jit(solution)/shard_map/all_gather | solution.py:457
  35.7 4.3 %all-gather.4 = f32[8,8,256]{2,1,0:T(8,128)S(1)} all-gather(f32[4,8,256]{2,1,0:T(8,128)S(1)} %shard_map.40), channel_id=6, replica_groups={{12,1},{13,2},{14,3},{15,4},{16,5},{17,6},{18,7},{19,8},{20,9},{21,10},..., dimensions={0}, use_global_device_ids=true | all-gather | bytes 98304 | tf_op jit(solution)/shard_map/all_gather | solution.py:454
  40.0 2.8 %all_gather.75 = f32[2,4,8,256]{3,2,1,0:T(8,128)S(1)} all-gather(f32[1,4,8,256]{3,2,1,0:T(8,128)S(1)} %constant_dynamic-slice_fusion.1), channel_id=1, replica_groups={{0,12},{24,36},{48,60},{72,84},{96,108},{120,132},{144,156},{168,180},{..., dimensions={0}, use_global_device_ids=true | all-gather | bytes 98304 | tf_op jit(solution)/shard_map/all_gather | solution.py:457
  42.8 5.1 %all-gather.5 = f32[8,32,256]{2,1,0:T(8,128)S(1)} all-gather(f32[4,32,256]{2,1,0:T(8,128)S(1)} %pad_maximum_fusion.full), channel_id=7, replica_groups={{12,24},{13,25},{14,26},{15,27},{16,28},{17,29},{18,30},{19,31},{20,32}..., dimensions={0}, use_global_device_ids=true | all-gather | bytes 393216 | tf_op jit(solution)/shard_map/all_gather | solution.py:454
  47.9 1.3 %shard_map.41 = f32[24,8,128]{2,1,0:T(8,128)} custom-call(f32[4,32,256]{2,1,0:T(8,128)S(1)} %pad_maximum_fusion.full, f32[2,4,32,256]{3,2,1,0:T(8,128)S(1)} %bitcast.27), custom_call_target="tpu_custom_call" | custom-call | tf_op jit(solution)/shard_map/pallas_call | solution.py:24
  49.2 9.0 %all-to-all-start = ((f32[24,8,128]{2,1,0:T(8,128)}), f32[24,8,128]{2,1,0:T(8,128)S(1)}, u32[]{:S(2)}, u32[]{:S(2)}) async-start(f32[24,8,128]{2,1,0:T(8,128)} %shard_map.41), calls=%async_computation | async-start | bytes 196608 | tf_op jit(solution)/shard_map/all_to_all | solution.py:490
  58.2 2.0 %all_gather.83.two = f32[2,4,32,256]{3,2,1,0:T(8,128)S(1)} all-gather(f32[1,4,32,256]{3,2,1,0:T(8,128)S(1)} %constant_dynamic-slice_fusion), channel_id=1, replica_groups={{0,12},{24,36},{48,60},{72,84},{96,108},{120,132},{144,156},{168,180},{..., dimensions={0}, use_global_device_ids=true | all-gather | bytes 393216 | tf_op jit(solution)/shard_map/all_gather | solution.py:457
  60.2 0.3 shard_map.42
  60.5 8.3 %all-to-all-done.block = f32[24,8,128]{2,1,0:T(8,128)S(1)} async-done(((f32[24,8,128]{2,1,0:T(8,128)}), f32[24,8,128]{2,1,0:T(8,128)S(1)}, u32[]{:S(2)}, u32[]{:S(2)}) %all-to-all-start) | async-done | bytes 98336 | tf_op jit(solution)/shard_map/all_to_all | solution.py:490
  68.9 4.7 %all-gather.6 = f32[48,8,128]{2,1,0:T(8,128)S(1)} all-gather(f32[24,8,128]{2,1,0:T(8,128)S(1)} %all-to-all-done.block), channel_id=8, replica_groups={{12,24},{13,25},{14,26},{15,27},{16,28},{17,29},{18,30},{19,31},{20,32}..., dimensions={0}, use_global_device_ids=true | all-gather | bytes 294912 | tf_op jit(solution)/shard_map/all_gather | solution.py:454
  73.6 7.0 %all-gather.7 = f32[4,24,8,128]{3,2,1,0:T(8,128)S(1)} all-gather(f32[2,24,8,128]{3,2,1,0:T(8,128)S(1)} %bitcast.29), channel_id=9, replica_groups={{12,72},{13,73},{14,74},{15,75},{16,76},{17,77},{18,78},{19,79},{20,80}..., dimensions={0}, use_global_device_ids=true | all-gather | bytes 589824 | tf_op jit(solution)/shard_map/all_gather | solution.py:454
  80.7 7.5 %all_gather.82.outer = f32[2,3,24,8,128]{4,3,2,1,0:T(8,128)S(1)} all-gather(f32[1,3,24,8,128]{4,3,2,1,0:T(8,128)S(1)} %maximum_select_fusion), channel_id=1, replica_groups={{0,12},{24,36},{48,60},{72,84},{96,108},{120,132},{144,156},{168,180},{..., dimensions={0}, use_global_device_ids=true | all-gather | bytes 884736 | tf_op jit(solution)/shard_map/all_gather | solution.py:457
  88.2 2.8 %shard_map.43 = f32[4,16,512]{2,1,0:T(8,128)} custom-call(f32[24,8,128]{2,1,0:T(8,128)S(1)} %all-to-all-done.block, f32[2,3,24,8,128]{4,3,2,1,0:T(8,128)S(1)} %all_gather.82.outer, f32[8,16,256]{2,1,0:T(8,128)S(1)} %get-tuple-element.19.pre1, f32[6,16,256]{2,1,0:T(8,128)S(1)} %get-tuple-element.20.w1, f32[6,16,256]{2,1,0:T(8,128)S(1)} %get-tuple-element.21.g1, ...), custom_call_target="tpu_custom_call" | custom-call | tf_op jit(solution)/shard_map/pallas_call | solution.py:500
  (12 shorter events, 0.2 us)
Async XLA Ops:
  49.2 19.7 %all-to-all-start = ((f32[24,8,128]{2,1,0:T(8,128)}), f32[24,8,128]{2,1,0:T(8,128)S(1)}, u32[]{:S(2)}, u32[]{:S(2)}) async-start(f32[24,8,128]{2,1,0:T(8,128)} %shard_map.41), calls=%async_computation | async-start | bytes 196608 | tf_op jit(solution)/shard_map/all_to_all | solution.py:490

commit v5 on v4

--- a/solution.py
+++ b/solution.py
@@ -136,14 +136,42 @@
     )(divergence, density, zones)
 
 
+BESIDE = ((1, 112, 3, 2), (2, 122, 2, 1), (3, 128, 1, 0))
+MESSAGE = 136
+
+
+def k_message0(core, sides, out):
+    odd = lax.rem(lax.axis_index("height"), 2)
+    out[128:136] = jnp.zeros((8, 512), F32)
+    for par in range(2):
+
+        @pl.when(odd == par)
+        def _():
+            for d in range(1, 5):
+                out[16 * d - 16 : 16 * d] = core[par, 0, 4 - d if par else d - 1]
+                if d < 4:
+                    out[48 + 16 * d : 64 + 16 * d] = core[par, 1, 4 - d if par else d - 1]
+            for d, at, n_cond, n_div in BESIDE:
+                layer = 8 - d if par else d - 1
+                for side in range(2):
+                    cond, div = (0, 4) if side else (4 - n_cond, 7 - n_div)
+                    out[at : at + n_cond] = sides[side, layer, cond : cond + n_cond]
+                    if n_div:
+                        out[at + n_cond : at + n_cond + n_div] = sides[side, layer, div : div + n_div]
+                    at += n_cond + n_div
+
+
 def stack0(core, near, put):
     h, _, high, _ = position()
     odd = lax.rem(h, 2)
 
+    def far(par, d):
+        return near[par, 16 * d - 16 : 16 * d], near[par, 48 + 16 * d : 64 + 16 * d] if d < 4 else None
+
     @pl.when(odd == 0)
     def _():
         for z in range(4):
-            put(z, near[0, z], near[0, 4 + z], h == 0)
+            put(z, *far(0, 4 - z), h == 0)
             put(z + 4, core[0, 0, z], core[0, 1, z], None)
             put(z + 8, core[1, 0, z], core[1, 1, z], None)
 
@@ -152,7 +180,7 @@
         for z in range(4):
             put(z, core[0, 0, z], core[0, 1, z], None)
             put(z + 4, core[1, 0, z], core[1, 1, z], None)
-            put(z + 8, near[1, z], near[1, 4 + z], h == high - 1)
+            put(z + 8, *far(1, z + 1), h == high - 1)
 
 
 def k_edges0(core, edge):
@@ -172,7 +200,8 @@
 
     def put(z, cond, div, outside):
         c[z, 4:20] = cond if outside is None else jnp.where(outside, 1.0, cond)
-        g[z, 4:20] = div
+        if div is not None:
+            g[z, 4:20] = div
 
     stack0(core, near, put)
     for z in range(12):
@@ -184,14 +213,21 @@
 
         @pl.when(odd == par)
         def _():
-            for z in range(1, 11):
-                inner = z < 8 if par else z >= 4
-                at = z if par else z - 4
+            for z in range(1, 8) if par else range(4, 11):
                 for side, first, end in ((0, 0, plan == 0), (1, 20, plan == n_p - 1)):
-                    rows = sides.at[side, at] if inner else near.at[par, z if par else z + 7, pl.ds(8 * side, 8)]
-                    out = end if inner else jnp.logical_or(end, h == (n_h - 1 if par else 0))
-                    c[z, first : first + 4] = jnp.where(out, 1.0, rows[0:4])
+                    rows = sides.at[side, z if par else z - 4]
+                    c[z, first : first + 4] = jnp.where(end, 1.0, rows[0:4])
                     g[z, first + 1 - side : first + 4 - side] = rows[4:7]
+            for d, at, n_cond, n_div in BESIDE:
+                z = 7 + d if par else 4 - d
+                for side, end in ((0, plan == 0), (1, plan == n_p - 1)):
+                    out = jnp.logical_or(end, h == (n_h - 1 if par else 0))
+                    first = 20 if side else 4 - n_cond
+                    c[z, first : first + n_cond] = jnp.where(out, 1.0, near[par, at : at + n_cond])
+                    first = 20 if side else 4 - n_div
+                    if n_div:
+                        g[z, first : first + n_div] = near[par, at + n_cond : at + n_cond + n_div]
+                    at += n_cond + n_div
 
     row = iota((24, 512), 0) + (plan * 16 - 4)
     row_in = jnp.logical_and(row >= 0, row < n_p * 16).astype(F32) * OMEGA
@@ -465,9 +501,7 @@
         return pair(lax.dynamic_index_in_dim(meet(edge, across), odd, 0, keepdims=False))
 
     sides = both_sides(call(k_edges0, (8, 8, 512), [], core))
-    corner = lax.dynamic_slice_in_dim(sides, 5 * odd, 3, 1)
-    corner = jnp.concatenate([corner[0], corner[1]], axis=1)
-    near = meet(jnp.concatenate([own.reshape(8, 16, 512), corner], axis=0), links)
+    near = meet(call(k_message0, (MESSAGE, 512), [], core, sides), links)
     box = (12, 24, 512)
     eight, six, seven = (8, 24, 512), (6, 24, 512), (7, 24, 512)
     *level0, pack = call(

time: 91.4 us -> 90.5 us (level)
    pallas_call x5 -> x6, Pallas kernels: 3.31 us -> 3.33 us  [call(): pl.pallas_call(body, out_shape=shapes if many else shapes[0], in_specs=vm...]
where the time goes in v5:
time: 90.5 us; the launch traced here: 90.1 us
  blocking collectives  65.4 us (72%)
  starting transfers between devices  8.98 us (10%)
  waiting for transfers between devices  8.33 us (9%)
  Pallas kernels  7.17 us (8%)
    all_gather x6, blocking collectives, meet(): lax.all_gather(x, ('height', 'plan'), axis=0, tiled=False, axis_index_gro...  33.7 us
    all_gather x6, blocking collectives, pair(): lax.all_gather(x, 'height', axis=0, tiled=False, axis_index_groups=cores)  31.8 us
    all_to_all x1, starting transfers between devices, on_device(): lax.all_to_all(tiles, ('height', 'plan'), split_axis=0, concat_axis=0, ti...  8.98 us
    all_to_all x1, waiting for transfers between devices, on_device(): lax.all_to_all(tiles, ('height', 'plan'), split_axis=0, concat_axis=0, ti...  8.33 us
    pallas_call x6, Pallas kernels, call(): pl.pallas_call(body, out_shape=shapes if many else shapes[0], in_specs=vm...  3.33 us
    pallas_call x1, Pallas kernels, on_device(): pl.pallas_call(k_up, out_shape=jax.ShapeDtypeStruct((4, 16, 512), F32), i...  2.8 us
  transfers between devices with their start and end apart: 1, of which 1 were waited for; matrix products, arithmetic and copies ran while one was open for 0% of the time, Pallas kernels for 0%

profile of v5, /device:TPU:33, one launch (start us, length us, event | category | flops | bytes accessed | tf_op | source)
XLA Modules:
  0.0 90.1 jit_solution(5361647595134705174)
XLA Ops:
  0.0 1.0 %shard_map.37 = f32[2,4,16,512]{3,2,1,0:T(8,128)S(1)} custom-call(f32[4,16,512]{2,1,0:T(8,128)} %div.1, f32[4,16,512]{2,1,0:T(8,128)} %density.1, s32[4,16,512]{2,1,0:T(8,128)} %zones.1), custom_call_target="tpu_custom_call" | custom-call | tf_op jit(solution)/shard_map/pallas_call | solution.py:130
  1.0 2.5 %all-gather = f32[4,4,16,512]{3,2,1,0:T(8,128)S(1)} all-gather(f32[2,4,16,512]{3,2,1,0:T(8,128)S(1)} %shard_map.37), channel_id=2, replica_groups={{0,12},{24,36},{48,60},{72,84},{96,108},{120,132},{144,156},{168,180},{..., dimensions={0}, use_global_device_ids=true | all-gather | bytes 786432 | tf_op jit(solution)/shard_map/all_gather | solution.py:493
  3.6 5.7 %all-gather.1 = f32[16,8,512]{2,1,0:T(8,128)S(1)} all-gather(f32[8,8,512]{2,1,0:T(8,128)S(1)} %shard_map.38), channel_id=3, replica_groups={{12,1},{13,2},{14,3},{15,4},{16,5},{17,6},{18,7},{19,8},{20,9},{21,10},..., dimensions={0}, use_global_device_ids=true | all-gather | bytes 393216 | tf_op jit(solution)/shard_map/all_gather | solution.py:490
  9.2 12.1 %all_gather.68.sides = f32[2,8,8,512]{3,2,1,0:T(8,128)S(1)} all-gather(f32[1,8,8,512]{3,2,1,0:T(8,128)S(1)} %constant_dynamic-slice_fusion.2), channel_id=1, replica_groups={{0,12},{24,36},{48,60},{72,84},{96,108},{120,132},{144,156},{168,180},{..., dimensions={0}, use_global_device_ids=true | all-gather | bytes 393216 | tf_op jit(solution)/shard_map/all_gather | solution.py:493
  21.3 6.9 %all-gather.2 = f32[272,512]{1,0:T(8,128)S(1)} all-gather(f32[136,512]{1,0:T(8,128)S(1)} %shard_map.39), channel_id=4, replica_groups={{12,24},{13,25},{14,26},{15,27},{16,28},{17,29},{18,30},{19,31},{20,32}..., dimensions={0}, use_global_device_ids=true | all-gather | bytes 835584 | tf_op jit(solution)/shard_map/all_gather | solution.py:490
  28.3 1.6 %shard_map.40 = (f32[8,24,512]{2,1,0:T(8,128)S(1)}, f32[6,24,512]{2,1,0:T(8,128)S(1)}, f32[6,24,512]{2,1,0:T(8,128)S(1)}, f32[6,24,512]{2,1,0:T(8,128)S(1)}, f32...) custom-call(f32[2,2,4,16,512]{4,3,2,1,0:T(8,128)S(1)} %bitcast.20, ...), custom_call_target="tpu_custom_call" | custom-call | tf_op jit(solution)/shard_map/pallas_call | solution.py:24
  29.9 4.9 %all-gather.3.chip = f32[4,16,256]{2,1,0:T(8,128)S(1)} all-gather(f32[2,16,256]{2,1,0:T(8,128)S(1)} %get-tuple-element.18), channel_id=5, replica_groups={{0,12},{24,36},{48,60},{72,84},{96,108},{120,132},{144,156},{168,180},{..., dimensions={0}, use_global_device_ids=true | all-gather | bytes 98304 | tf_op jit(solution)/shard_map/all_gather | solution.py:493
  34.9 4.3 %all-gather.4 = f32[8,8,256]{2,1,0:T(8,128)S(1)} all-gather(f32[4,8,256]{2,1,0:T(8,128)S(1)} %shard_map.41), channel_id=6, replica_groups={{12,1},{13,2},{14,3},{15,4},{16,5},{17,6},{18,7},{19,8},{20,9},{21,10},..., dimensions={0}, use_global_device_ids=true | all-gather | bytes 98304 | tf_op jit(solution)/shard_map/all_gather | solution.py:490
  39.2 2.8 %all_gather.75 = f32[2,4,8,256]{3,2,1,0:T(8,128)S(1)} all-gather(f32[1,4,8,256]{3,2,1,0:T(8,128)S(1)} %constant_dynamic-slice_fusion.1), channel_id=1, replica_groups={{0,12},{24,36},{48,60},{72,84},{96,108},{120,132},{144,156},{168,180},{..., dimensions={0}, use_global_device_ids=true | all-gather | bytes 98304 | tf_op jit(solution)/shard_map/all_gather | solution.py:493
  42.0 5.1 %all-gather.5 = f32[8,32,256]{2,1,0:T(8,128)S(1)} all-gather(f32[4,32,256]{2,1,0:T(8,128)S(1)} %pad_maximum_fusion.full), channel_id=7, replica_groups={{12,24},{13,25},{14,26},{15,27},{16,28},{17,29},{18,30},{19,31},{20,32}..., dimensions={0}, use_global_device_ids=true | all-gather | bytes 393216 | tf_op jit(solution)/shard_map/all_gather | solution.py:490
  47.0 1.3 %shard_map.42 = f32[24,8,128]{2,1,0:T(8,128)} custom-call(f32[4,32,256]{2,1,0:T(8,128)S(1)} %pad_maximum_fusion.full, f32[2,4,32,256]{3,2,1,0:T(8,128)S(1)} %bitcast.22), custom_call_target="tpu_custom_call" | custom-call | tf_op jit(solution)/shard_map/pallas_call | solution.py:24
  48.3 9.0 %all-to-all-start = ((f32[24,8,128]{2,1,0:T(8,128)}), f32[24,8,128]{2,1,0:T(8,128)S(1)}, u32[]{:S(2)}, u32[]{:S(2)}) async-start(f32[24,8,128]{2,1,0:T(8,128)} %shard_map.42), calls=%async_computation | async-start | bytes 196608 | tf_op jit(solution)/shard_map/all_to_all | solution.py:524
  57.3 2.0 %all_gather.83.two = f32[2,4,32,256]{3,2,1,0:T(8,128)S(1)} all-gather(f32[1,4,32,256]{3,2,1,0:T(8,128)S(1)} %constant_dynamic-slice_fusion), channel_id=1, replica_groups={{0,12},{24,36},{48,60},{72,84},{96,108},{120,132},{144,156},{168,180},{..., dimensions={0}, use_global_device_ids=true | all-gather | bytes 393216 | tf_op jit(solution)/shard_map/all_gather | solution.py:493
  59.3 0.3 shard_map.43
  59.7 8.3 %all-to-all-done.block = f32[24,8,128]{2,1,0:T(8,128)S(1)} async-done(((f32[24,8,128]{2,1,0:T(8,128)}), f32[24,8,128]{2,1,0:T(8,128)S(1)}, u32[]{:S(2)}, u32[]{:S(2)}) %all-to-all-start) | async-done | bytes 98336 | tf_op jit(solution)/shard_map/all_to_all | solution.py:524
  68.0 4.7 %all-gather.6 = f32[48,8,128]{2,1,0:T(8,128)S(1)} all-gather(f32[24,8,128]{2,1,0:T(8,128)S(1)} %all-to-all-done.block), channel_id=8, replica_groups={{12,24},{13,25},{14,26},{15,27},{16,28},{17,29},{18,30},{19,31},{20,32}..., dimensions={0}, use_global_device_ids=true | all-gather | bytes 294912 | tf_op jit(solution)/shard_map/all_gather | solution.py:490
  72.7 7.0 %all-gather.7 = f32[4,24,8,128]{3,2,1,0:T(8,128)S(1)} all-gather(f32[2,24,8,128]{3,2,1,0:T(8,128)S(1)} %bitcast.24), channel_id=9, replica_groups={{12,72},{13,73},{14,74},{15,75},{16,76},{17,77},{18,78},{19,79},{20,80}..., dimensions={0}, use_global_device_ids=true | all-gather | bytes 589824 | tf_op jit(solution)/shard_map/all_gather | solution.py:490
  79.8 7.5 %all_gather.82.outer = f32[2,3,24,8,128]{4,3,2,1,0:T(8,128)S(1)} all-gather(f32[1,3,24,8,128]{4,3,2,1,0:T(8,128)S(1)} %maximum_select_fusion), channel_id=1, replica_groups={{0,12},{24,36},{48,60},{72,84},{96,108},{120,132},{144,156},{168,180},{..., dimensions={0}, use_global_device_ids=true | all-gather | bytes 884736 | tf_op jit(solution)/shard_map/all_gather | solution.py:493
  87.3 2.8 %shard_map.44 = f32[4,16,512]{2,1,0:T(8,128)} custom-call(f32[24,8,128]{2,1,0:T(8,128)S(1)} %all-to-all-done.block, f32[2,3,24,8,128]{4,3,2,1,0:T(8,128)S(1)} %all_gather.82.outer, f32[8,16,256]{2,1,0:T(8,128)S(1)} %get-tuple-element.19.pre1, f32[6,16,256]{2,1,0:T(8,128)S(1)} %get-tuple-element.20.w1, f32[6,16,256]{2,1,0:T(8,128)S(1)} %get-tuple-element.21.g1, ...), custom_call_target="tpu_custom_call" | custom-call | tf_op jit(solution)/shard_map/pallas_call | solution.py:534
  (11 shorter events, 0.2 us)
Async XLA Ops:
  48.3 19.7 %all-to-all-start = ((f32[24,8,128]{2,1,0:T(8,128)}), f32[24,8,128]{2,1,0:T(8,128)S(1)}, u32[]{:S(2)}, u32[]{:S(2)}) async-start(f32[24,8,128]{2,1,0:T(8,128)} %shard_map.42), calls=%async_computation | async-start | bytes 196608 | tf_op jit(solution)/shard_map/all_to_all | solution.py:524

commit v6 on v5

--- a/solution.py
+++ b/solution.py
@@ -495,7 +495,9 @@
     links, leaps = reach(1, []), reach(5, [(0, 4), (n_h - 5, n_h - 1)])
     own = conductance(divergence, density, zones)
     core = pair(own)
-    across = [[(2 * i + 1) * n_p + t, 2 * i * n_p + (t + 1) % n_p] for i in range(n_h // 2) for t in range(n_p)]
+    across = [[(2 * i + 1) * n_p + t, 2 * i * n_p + t + 1] for i in range(n_h // 2) for t in range(n_p - 1)]
+    across += [[(2 * i + 1) * n_p + n_p - 1, (2 * i + 3) * n_p + n_p - 1] for i in range(0, n_h // 2, 2)]
+    across += [[2 * i * n_p, (2 * i + 2) * n_p] for i in range(0, n_h // 2, 2)]
 
     def both_sides(edge):
         return pair(lax.dynamic_index_in_dim(meet(edge, across), odd, 0, keepdims=False))

time: 90.5 us -> 90.5 us (level)
  starting transfers between devices: 8.98 us -> 19.7 us
  blocking collectives: 65.4 us -> 54.7 us
    all_gather x6, blocking collectives: 31.8 us -> 20.8 us  [pair(): lax.all_gather(x, 'height', axis=0, tiled=False, axis_index_groups=cores)]
    all_to_all x1, starting transfers between devices: 8.98 us -> 19.7 us  [on_device(): lax.all_to_all(tiles, ('height', 'plan'), split_axis=0, concat_axis=0, ti...]
where the time goes in v6:
time: 90.5 us; the launch traced here: 90.1 us
  blocking collectives  54.7 us (60%)
  starting transfers between devices  19.7 us (22%)
  waiting for transfers between devices  8.33 us (9%)
  Pallas kernels  7.17 us (8%)
    all_gather x6, blocking collectives, meet(): lax.all_gather(x, ('height', 'plan'), axis=0, tiled=False, axis_index_gro...  33.9 us
    all_gather x6, blocking collectives, pair(): lax.all_gather(x, 'height', axis=0, tiled=False, axis_index_groups=cores)  20.8 us
    all_to_all x1, starting transfers between devices, on_device(): lax.all_to_all(tiles, ('height', 'plan'), split_axis=0, concat_axis=0, ti...  19.7 us
    all_to_all x1, waiting for transfers between devices, on_device(): lax.all_to_all(tiles, ('height', 'plan'), split_axis=0, concat_axis=0, ti...  8.33 us
    pallas_call x6, Pallas kernels, call(): pl.pallas_call(body, out_shape=shapes if many else shapes[0], in_specs=vm...  3.33 us
    pallas_call x1, Pallas kernels, on_device(): pl.pallas_call(k_up, out_shape=jax.ShapeDtypeStruct((4, 16, 512), F32), i...  2.8 us
  transfers between devices with their start and end apart: 1, of which 1 were waited for; matrix products, arithmetic and copies ran while one was open for 0% of the time, Pallas kernels for 0%

profile of v6, /device:TPU:33, one launch (start us, length us, event | category | flops | bytes accessed | tf_op | source)
XLA Modules:
  0.0 90.1 jit_solution(12892434486222381456)
XLA Ops:
  0.0 1.0 %shard_map.37 = f32[2,4,16,512]{3,2,1,0:T(8,128)S(1)} custom-call(f32[4,16,512]{2,1,0:T(8,128)} %div.1, f32[4,16,512]{2,1,0:T(8,128)} %density.1, s32[4,16,512]{2,1,0:T(8,128)} %zones.1), custom_call_target="tpu_custom_call" | custom-call | tf_op jit(solution)/shard_map/pallas_call | solution.py:130
  1.0 2.5 %all-gather = f32[4,4,16,512]{3,2,1,0:T(8,128)S(1)} all-gather(f32[2,4,16,512]{3,2,1,0:T(8,128)S(1)} %shard_map.37), channel_id=2, replica_groups={{0,12},{24,36},{48,60},{72,84},{96,108},{120,132},{144,156},{168,180},{..., dimensions={0}, use_global_device_ids=true | all-gather | bytes 786432 | tf_op jit(solution)/shard_map/all_gather | solution.py:493
  3.6 5.7 %all-gather.1 = f32[16,8,512]{2,1,0:T(8,128)S(1)} all-gather(f32[8,8,512]{2,1,0:T(8,128)S(1)} %shard_map.38), channel_id=3, replica_groups={{12,1},{13,2},{14,3},{15,4},{16,5},{17,6},{18,7},{19,8},{20,9},{21,10},..., dimensions={0}, use_global_device_ids=true | all-gather | bytes 393216 | tf_op jit(solution)/shard_map/all_gather | solution.py:490
  9.2 2.0 %all_gather.68.sides = f32[2,8,8,512]{3,2,1,0:T(8,128)S(1)} all-gather(f32[1,8,8,512]{3,2,1,0:T(8,128)S(1)} %constant_dynamic-slice_fusion.2), channel_id=1, replica_groups={{0,12},{24,36},{48,60},{72,84},{96,108},{120,132},{144,156},{168,180},{..., dimensions={0}, use_global_device_ids=true | all-gather | bytes 393216 | tf_op jit(solution)/shard_map/all_gather | solution.py:493
  11.3 6.9 %all-gather.2 = f32[272,512]{1,0:T(8,128)S(1)} all-gather(f32[136,512]{1,0:T(8,128)S(1)} %shard_map.39), channel_id=4, replica_groups={{12,24},{13,25},{14,26},{15,27},{16,28},{17,29},{18,30},{19,31},{20,32}..., dimensions={0}, use_global_device_ids=true | all-gather | bytes 835584 | tf_op jit(solution)/shard_map/all_gather | solution.py:490
  18.2 1.6 %shard_map.40 = (f32[8,24,512]{2,1,0:T(8,128)S(1)}, f32[6,24,512]{2,1,0:T(8,128)S(1)}, f32[6,24,512]{2,1,0:T(8,128)S(1)}, f32[6,24,512]{2,1,0:T(8,128)S(1)}, f32...) custom-call(f32[2,2,4,16,512]{4,3,2,1,0:T(8,128)S(1)} %bitcast.20, ...), custom_call_target="tpu_custom_call" | custom-call | tf_op jit(solution)/shard_map/pallas_call | solution.py:24
  19.9 4.9 %all-gather.3.chip = f32[4,16,256]{2,1,0:T(8,128)S(1)} all-gather(f32[2,16,256]{2,1,0:T(8,128)S(1)} %get-tuple-element.18), channel_id=5, replica_groups={{0,12},{24,36},{48,60},{72,84},{96,108},{120,132},{144,156},{168,180},{..., dimensions={0}, use_global_device_ids=true | all-gather | bytes 98304 | tf_op jit(solution)/shard_map/all_gather | solution.py:493
  24.8 4.6 %all-gather.4 = f32[8,8,256]{2,1,0:T(8,128)S(1)} all-gather(f32[4,8,256]{2,1,0:T(8,128)S(1)} %shard_map.41), channel_id=6, replica_groups={{12,1},{13,2},{14,3},{15,4},{16,5},{17,6},{18,7},{19,8},{20,9},{21,10},..., dimensions={0}, use_global_device_ids=true | all-gather | bytes 98304 | tf_op jit(solution)/shard_map/all_gather | solution.py:490
  29.3 1.9 %all_gather.75 = f32[2,4,8,256]{3,2,1,0:T(8,128)S(1)} all-gather(f32[1,4,8,256]{3,2,1,0:T(8,128)S(1)} %constant_dynamic-slice_fusion.1), channel_id=1, replica_groups={{0,12},{24,36},{48,60},{72,84},{96,108},{120,132},{144,156},{168,180},{..., dimensions={0}, use_global_device_ids=true | all-gather | bytes 98304 | tf_op jit(solution)/shard_map/all_gather | solution.py:493
  31.2 5.1 %all-gather.5 = f32[8,32,256]{2,1,0:T(8,128)S(1)} all-gather(f32[4,32,256]{2,1,0:T(8,128)S(1)} %pad_maximum_fusion.full), channel_id=7, replica_groups={{12,24},{13,25},{14,26},{15,27},{16,28},{17,29},{18,30},{19,31},{20,32}..., dimensions={0}, use_global_device_ids=true | all-gather | bytes 393216 | tf_op jit(solution)/shard_map/all_gather | solution.py:490
  36.3 1.3 %shard_map.42 = f32[24,8,128]{2,1,0:T(8,128)} custom-call(f32[4,32,256]{2,1,0:T(8,128)S(1)} %pad_maximum_fusion.full, f32[2,4,32,256]{3,2,1,0:T(8,128)S(1)} %bitcast.22), custom_call_target="tpu_custom_call" | custom-call | tf_op jit(solution)/shard_map/pallas_call | solution.py:24
  37.6 19.7 %all-to-all-start = ((f32[24,8,128]{2,1,0:T(8,128)}), f32[24,8,128]{2,1,0:T(8,128)S(1)}, u32[]{:S(2)}, u32[]{:S(2)}) async-start(f32[24,8,128]{2,1,0:T(8,128)} %shard_map.42), calls=%async_computation | async-start | bytes 196608 | tf_op jit(solution)/shard_map/all_to_all | solution.py:526
  57.3 2.0 %all_gather.83.two = f32[2,4,32,256]{3,2,1,0:T(8,128)S(1)} all-gather(f32[1,4,32,256]{3,2,1,0:T(8,128)S(1)} %constant_dynamic-slice_fusion), channel_id=1, replica_groups={{0,12},{24,36},{48,60},{72,84},{96,108},{120,132},{144,156},{168,180},{..., dimensions={0}, use_global_device_ids=true | all-gather | bytes 393216 | tf_op jit(solution)/shard_map/all_gather | solution.py:493
  59.3 0.3 shard_map.43
  59.7 8.3 %all-to-all-done.block = f32[24,8,128]{2,1,0:T(8,128)S(1)} async-done(((f32[24,8,128]{2,1,0:T(8,128)}), f32[24,8,128]{2,1,0:T(8,128)S(1)}, u32[]{:S(2)}, u32[]{:S(2)}) %all-to-all-start) | async-done | bytes 98336 | tf_op jit(solution)/shard_map/all_to_all | solution.py:526
  68.0 4.7 %all-gather.6 = f32[48,8,128]{2,1,0:T(8,128)S(1)} all-gather(f32[24,8,128]{2,1,0:T(8,128)S(1)} %all-to-all-done.block), channel_id=8, replica_groups={{12,24},{13,25},{14,26},{15,27},{16,28},{17,29},{18,30},{19,31},{20,32}..., dimensions={0}, use_global_device_ids=true | all-gather | bytes 294912 | tf_op jit(solution)/shard_map/all_gather | solution.py:490
  72.7 7.0 %all-gather.7 = f32[4,24,8,128]{3,2,1,0:T(8,128)S(1)} all-gather(f32[2,24,8,128]{3,2,1,0:T(8,128)S(1)} %bitcast.24), channel_id=9, replica_groups={{12,72},{13,73},{14,74},{15,75},{16,76},{17,77},{18,78},{19,79},{20,80}..., dimensions={0}, use_global_device_ids=true | all-gather | bytes 589824 | tf_op jit(solution)/shard_map/all_gather | solution.py:490
  79.8 7.5 %all_gather.82.outer = f32[2,3,24,8,128]{4,3,2,1,0:T(8,128)S(1)} all-gather(f32[1,3,24,8,128]{4,3,2,1,0:T(8,128)S(1)} %maximum_select_fusion), channel_id=1, replica_groups={{0,12},{24,36},{48,60},{72,84},{96,108},{120,132},{144,156},{168,180},{..., dimensions={0}, use_global_device_ids=true | all-gather | bytes 884736 | tf_op jit(solution)/shard_map/all_gather | solution.py:493
  87.3 2.8 %shard_map.44 = f32[4,16,512]{2,1,0:T(8,128)} custom-call(f32[24,8,128]{2,1,0:T(8,128)S(1)} %all-to-all-done.block, f32[2,3,24,8,128]{4,3,2,1,0:T(8,128)S(1)} %all_gather.82.outer, f32[8,16,256]{2,1,0:T(8,128)S(1)} %get-tuple-element.19.pre1, f32[6,16,256]{2,1,0:T(8,128)S(1)} %get-tuple-element.20.w1, f32[6,16,256]{2,1,0:T(8,128)S(1)} %get-tuple-element.21.g1, ...), custom_call_target="tpu_custom_call" | custom-call | tf_op jit(solution)/shard_map/pallas_call | solution.py:536
  (11 shorter events, 0.2 us)
Async XLA Ops:
  37.6 30.4 %all-to-all-start = ((f32[24,8,128]{2,1,0:T(8,128)}), f32[24,8,128]{2,1,0:T(8,128)S(1)}, u32[]{:S(2)}, u32[]{:S(2)}) async-start(f32[24,8,128]{2,1,0:T(8,128)} %shard_map.42), calls=%async_computation | async-start | bytes 196608 | tf_op jit(solution)/shard_map/all_to_all | solution.py:526

commit v7 on v6

--- a/solution.py
+++ b/solution.py
@@ -20,7 +20,7 @@
 
 def call(body, outs, scratch, *arrays):
     many = isinstance(outs, list)
-    shapes = [pltpu.VMEM(s, F32) for s in (outs if many else [outs])]
+    shapes = [pltpu.VMEM(s, F32) if isinstance(s, tuple) else s for s in (outs if many else [outs])]
     return pl.pallas_call(
         body,
         out_shape=shapes if many else shapes[0],
@@ -195,7 +195,7 @@
                 edge[z, 7:8] = jnp.zeros((1, 512), F32)
 
 
-def k_level0(core, near, sides, pre, w_out, g_out, cx_out, cy_out, cz_out, pack, c, g, w, cx, cy, cz, dg, p, rs, c1, st):
+def k_level0(core, near, sides, p, w, g, cx, cy, cz, pack, c, dg, rs, c1, st):
     h, plan, n_h, n_p = position()
 
     def put(z, cond, div, outside):
@@ -254,15 +254,6 @@
         here = p[z]
         total = spread(here, p[z - 1], p[z + 1], cz[z - 1], cz[z], cx[z], cy[z])
         rs[z - 4] = rs[z - 4] - dg[z - 4] * here + total
-    for z in range(2, 10):
-        pre[z - 2] = p[z]
-    for z in range(3, 9):
-        w_out[z - 3] = w[z]
-        g_out[z - 3] = g[z]
-        cx_out[z - 3] = cx[z]
-        cy_out[z - 3] = cy[z]
-    for z in range(2, 9):
-        cz_out[z - 2] = cz[z]
     rows = [pair_rows(st.at[z], rs[2 * z] + rs[2 * z + 1], 4, 8) for z in range(2)]
     for z in range(4):
         sums = c[2 * z + 2] + c[2 * z + 3]
@@ -330,10 +321,12 @@
     return diags
 
 
-def k_level1_wide(full, two, pre, w_out, g_out, cx_out, cy_out, cz_out, c, g, w, cx, cy, cz):
+def k_level1_wide(full, two, pre, w_out, g_out, cx_out, cy_out, cz_out, twice2, twice1, c, g, w, cx, cy, cz):
     first = lax.axis_index("height") * 2 - 4
     layers = [two.at[0, z] for z in range(4)] + [full.at[z] for z in range(4)] + [two.at[1, z] for z in range(4)]
     window1(layers[0:10], layers[2:12], first, g, c)
+    twice2[...] = copy_matrix(128)
+    twice1[...] = copy_matrix(256)
     couple1(10, first, c, w, cx, cy, cz)
     for z in range(1, 9):
         here = g[z]
@@ -383,7 +376,7 @@
         copies[i, 4:8] = tile_c
 
 
-def k_up(block, outer, pre1, w1, g1, cx1, cy1, cz1, pre0, w0, g0, cx0, cy0, cz0, out, sems, s, c, g, w, cx, cy, cz, dg, pa, pb, p2, u1, q1, u0, q0, s1, s0, done):
+def k_up(block, outer, pre1, w1, g1, cx1, cy1, cz1, twice2, twice1, pre0, w0, g0, cx0, cy0, cz0, out, sems, s, c, g, w, cx, cy, cz, dg, pa, pb, p2, u1, q1, u0, q0, s1, s0, done):
     h, plan, n_h, _ = position()
     wide = s.shape[1] // 2
     tiles = wide // 4
@@ -433,7 +426,7 @@
         p2[z - 4, wide + 8 : wide + 16] = jnp.zeros((8, 128), F32)
         p2[z - 4, 8 : wide + 8] = here + line
     rows = jnp.concatenate([p2[z, pl.ds(plan * 4 + 6, 8), :] for z in range(5)], axis=0)
-    rows = dot(rows, copy_matrix(128))
+    rows = dot(rows, twice2[...])
     for z in range(5):
         u1[z] = copy_rows(s1.at[z], rows[8 * z : 8 * z + 8])
     for z in range(1, 9):
@@ -454,20 +447,20 @@
     for z in range(4):
         q1[z] = low[z]
     rows = jnp.concatenate([q1[z] for z in range(4)], axis=0)
-    rows = dot(rows, copy_matrix(256))
+    rows = dot(rows, twice1[...])
     for z in range(4):
         u0[z] = copy_rows(s0.at[z], rows[16 * z : 16 * z + 16])
     for z in range(2, 10):
-        q0[z - 2] = pre0[z - 2] + u0[z // 2 - 1, 4:28]
+        q0[z - 2] = pre0[z] + u0[z // 2 - 1, 4:28]
     for z in range(3, 9):
         here = q0[z - 2]
-        total = spread(here, q0[z - 3], q0[z - 1], cz0[z - 3], cz0[z - 2], cx0[z - 3], cy0[z - 3])
-        u0[z - 3, 0:24] = here * (1.0 / 3.0) + g0[z - 3] + w0[z - 3] * total
+        total = spread(here, q0[z - 3], q0[z - 1], cz0[z - 1], cz0[z], cx0[z], cy0[z])
+        u0[z - 3, 0:24] = here * (1.0 / 3.0) + g0[z] + w0[z] * total
     stores = []
     for z in range(4, 8):
         here = u0[z - 3, 0:24]
-        total = spread(here, u0[z - 4, 0:24], u0[z - 2, 0:24], cz0[z - 3], cz0[z - 2], cx0[z - 3], cy0[z - 3])
-        q0[z - 4] = here * (1.0 / 3.0) + g0[z - 3] + w0[z - 3] * total
+        total = spread(here, u0[z - 4, 0:24], u0[z - 2, 0:24], cz0[z - 1], cz0[z], cx0[z], cy0[z])
+        q0[z - 4] = here * (1.0 / 3.0) + g0[z] + w0[z] * total
         done[z - 4] = q0[z - 4, 4:20]
         stores.append(pltpu.make_async_copy(done.at[z - 4], out.at[z - 4], sems.at[z - 4]))
         stores[-1].start()
@@ -508,8 +501,8 @@
     eight, six, seven = (8, 24, 512), (6, 24, 512), (7, 24, 512)
     *level0, pack = call(
         k_level0,
-        [eight, six, six, six, six, seven, (2, 16, 256)],
-        [box] * 6 + [(4, 24, 512), box, (4, 24, 512), (4, 16, 512), (10, 4, 24, 128)],
+        [box] * 6 + [(2, 16, 256)],
+        [box, (4, 24, 512), (4, 24, 512), (4, 16, 512), (10, 4, 24, 128)],
         core, near, sides,
     )
     chip = pair(pack).reshape(4, 16, 256)
@@ -521,7 +514,8 @@
     two = pair(lax.dynamic_index_in_dim(near, odd, 0, keepdims=False))
     box = (10, 16, 256)
     eight, six, seven = (8, 16, 256), (6, 16, 256), (7, 16, 256)
-    level1 = call(k_level1_wide, [eight, six, six, six, six, seven], [box] * 6, full, two)
+    twice = [pltpu.VMEM((128, 256), jnp.bfloat16), pltpu.VMEM((256, 512), jnp.bfloat16)]
+    level1 = call(k_level1_wide, [eight, six, six, six, six, seven, *twice], [box] * 6, full, two)
     groups = [[(2 * i + k) * n_p + t for k in range(2) for t in range(n_p)] for i in range(n_h // 2)]
     block = lax.all_to_all(tiles, ("height", "plan"), split_axis=0, concat_axis=0, tiled=True, axis_index_groups=groups)
     near = meet(block, links)

time: 90.5 us -> 90.8 us (level)
  local copies, waits for them, and re-layouts: 0.08 us -> 3.96 us
  waiting for transfers between devices: 8.33 us -> 4.46 us
    unnamed x0 -> x28, local copies, waits for them, and re-layouts: none -> 3.88 us
    all_to_all x1, waiting for transfers between devices: 8.33 us -> 4.46 us  [on_device(): lax.all_to_all(tiles, ('height', 'plan'), split_axis=0, concat_axis=0, ti...]
where the time goes in v7:
time: 90.8 us; the launch traced here: 90.5 us
  blocking collectives  54.8 us (60%)
  starting transfers between devices  19.7 us (22%)
  Pallas kernels  7.27 us (8%)
  waiting for transfers between devices  4.46 us (5%)
  local copies, waits for them, and re-layouts  3.96 us (4%)
    all_gather x6, blocking collectives, meet(): lax.all_gather(x, ('height', 'plan'), axis=0, tiled=False, axis_index_gro...  33.9 us
    all_gather x6, blocking collectives, pair(): lax.all_gather(x, 'height', axis=0, tiled=False, axis_index_groups=cores)  20.9 us
    all_to_all x1, starting transfers between devices, on_device(): lax.all_to_all(tiles, ('height', 'plan'), split_axis=0, concat_axis=0, ti...  19.7 us
    all_to_all x1, waiting for transfers between devices, on_device(): lax.all_to_all(tiles, ('height', 'plan'), split_axis=0, concat_axis=0, ti...  4.46 us
    unnamed x28, local copies, waits for them, and re-layouts  3.88 us
    pallas_call x6, Pallas kernels, call(): pl.pallas_call(body, out_shape=shapes if many else shapes[0], in_specs=vm...  3.37 us
    pallas_call x1, Pallas kernels, on_device(): pl.pallas_call(k_up, out_shape=jax.ShapeDtypeStruct((4, 16, 512), F32), i...  2.87 us
  transfers between devices with their start and end apart: 1, of which 1 were waited for; matrix products, arithmetic and copies ran while one was open for 0% of the time, Pallas kernels for 0%

profile of v7, /device:TPU:33, one launch (start us, length us, event | category | flops | bytes accessed | tf_op | source)
XLA Modules:
  0.0 90.5 jit_solution(893953457358710643)
XLA Ops:
  0.0 1.0 %shard_map.37 = f32[2,4,16,512]{3,2,1,0:T(8,128)S(1)} custom-call(f32[4,16,512]{2,1,0:T(8,128)} %div.1, f32[4,16,512]{2,1,0:T(8,128)} %density.1, s32[4,16,512]{2,1,0:T(8,128)} %zones.1), custom_call_target="tpu_custom_call" | custom-call | tf_op jit(solution)/shard_map/pallas_call | solution.py:130
  1.0 2.5 %all-gather = f32[4,4,16,512]{3,2,1,0:T(8,128)S(1)} all-gather(f32[2,4,16,512]{3,2,1,0:T(8,128)S(1)} %shard_map.37), channel_id=2, replica_groups={{0,12},{24,36},{48,60},{72,84},{96,108},{120,132},{144,156},{168,180},{..., dimensions={0}, use_global_device_ids=true | all-gather | bytes 786432 | tf_op jit(solution)/shard_map/all_gather | solution.py:486
  3.6 5.7 %all-gather.1 = f32[16,8,512]{2,1,0:T(8,128)S(1)} all-gather(f32[8,8,512]{2,1,0:T(8,128)S(1)} %shard_map.38), channel_id=3, replica_groups={{12,1},{13,2},{14,3},{15,4},{16,5},{17,6},{18,7},{19,8},{20,9},{21,10},..., dimensions={0}, use_global_device_ids=true | all-gather | bytes 393216 | tf_op jit(solution)/shard_map/all_gather | solution.py:483
  9.2 2.0 %all_gather.68.sides = f32[2,8,8,512]{3,2,1,0:T(8,128)S(1)} all-gather(f32[1,8,8,512]{3,2,1,0:T(8,128)S(1)} %constant_dynamic-slice_fusion.2), channel_id=1, replica_groups={{0,12},{24,36},{48,60},{72,84},{96,108},{120,132},{144,156},{168,180},{..., dimensions={0}, use_global_device_ids=true | all-gather | bytes 393216 | tf_op jit(solution)/shard_map/all_gather | solution.py:486
  11.3 6.9 %all-gather.2 = f32[272,512]{1,0:T(8,128)S(1)} all-gather(f32[136,512]{1,0:T(8,128)S(1)} %shard_map.39), channel_id=4, replica_groups={{12,24},{13,25},{14,26},{15,27},{16,28},{17,29},{18,30},{19,31},{20,32}..., dimensions={0}, use_global_device_ids=true | all-gather | bytes 835584 | tf_op jit(solution)/shard_map/all_gather | solution.py:483
  18.2 1.7 %shard_map.40 = (f32[12,24,512]{2,1,0:T(8,128)S(1)}, f32[12,24,512]{2,1,0:T(8,128)S(1)}, f32[12,24,512]{2,1,0:T(8,128)S(1)}, f32[12,24,512]{2,1,0:T(8,128)S(1)},...) custom-call(f32[2,2,4,16,512]{4,3,2,1,0:T(8,128)S(1)} %bitcast.20, ...), custom_call_target="tpu_custom_call" | custom-call | tf_op jit(solution)/shard_map/pallas_call | solution.py:24
  19.9 0.0 copy-start
  19.9 4.9 %all-gather.3.chip = f32[4,16,256]{2,1,0:T(8,128)S(1)} all-gather(f32[2,16,256]{2,1,0:T(8,128)S(1)} %get-tuple-element.20), channel_id=5, replica_groups={{0,12},{24,36},{48,60},{72,84},{96,108},{120,132},{144,156},{168,180},{..., dimensions={0}, use_global_device_ids=true | all-gather | bytes 98304 | tf_op jit(solution)/shard_map/all_gather | solution.py:486
  24.8 4.6 %all-gather.4 = f32[8,8,256]{2,1,0:T(8,128)S(1)} all-gather(f32[4,8,256]{2,1,0:T(8,128)S(1)} %shard_map.41), channel_id=6, replica_groups={{12,1},{13,2},{14,3},{15,4},{16,5},{17,6},{18,7},{19,8},{20,9},{21,10},..., dimensions={0}, use_global_device_ids=true | all-gather | bytes 98304 | tf_op jit(solution)/shard_map/all_gather | solution.py:483
  29.4 1.9 %all_gather.75 = f32[2,4,8,256]{3,2,1,0:T(8,128)S(1)} all-gather(f32[1,4,8,256]{3,2,1,0:T(8,128)S(1)} %constant_dynamic-slice_fusion.1), channel_id=1, replica_groups={{0,12},{24,36},{48,60},{72,84},{96,108},{120,132},{144,156},{168,180},{..., dimensions={0}, use_global_device_ids=true | all-gather | bytes 98304 | tf_op jit(solution)/shard_map/all_gather | solution.py:486
  31.3 5.1 %all-gather.5 = f32[8,32,256]{2,1,0:T(8,128)S(1)} all-gather(f32[4,32,256]{2,1,0:T(8,128)S(1)} %pad_maximum_fusion.full), channel_id=7, replica_groups={{12,24},{13,25},{14,26},{15,27},{16,28},{17,29},{18,30},{19,31},{20,32}..., dimensions={0}, use_global_device_ids=true | all-gather | bytes 393216 | tf_op jit(solution)/shard_map/all_gather | solution.py:483
  36.3 0.0 copy-done
  36.4 1.3 %shard_map.42 = f32[24,8,128]{2,1,0:T(8,128)} custom-call(f32[4,32,256]{2,1,0:T(8,128)S(1)} %pad_maximum_fusion.full, f32[2,4,32,256]{3,2,1,0:T(8,128)S(1)} %bitcast.22), custom_call_target="tpu_custom_call" | custom-call | tf_op jit(solution)/shard_map/pallas_call | solution.py:24
  37.6 19.7 %all-to-all-start = ((f32[24,8,128]{2,1,0:T(8,128)}), f32[24,8,128]{2,1,0:T(8,128)S(1)}, u32[]{:S(2)}, u32[]{:S(2)}) async-start(f32[24,8,128]{2,1,0:T(8,128)} %shard_map.42), calls=%async_computation | async-start | bytes 196608 | tf_op jit(solution)/shard_map/all_to_all | solution.py:520
  57.4 2.0 %all_gather.83.two = f32[2,4,32,256]{3,2,1,0:T(8,128)S(1)} all-gather(f32[1,4,32,256]{3,2,1,0:T(8,128)S(1)} %constant_dynamic-slice_fusion), channel_id=1, replica_groups={{0,12},{24,36},{48,60},{72,84},{96,108},{120,132},{144,156},{168,180},{..., dimensions={0}, use_global_device_ids=true | all-gather | bytes 393216 | tf_op jit(solution)/shard_map/all_gather | solution.py:486
  59.4 0.4 shard_map.43
  59.7 0.0 copy-start.2
  59.7 0.6 copy-done.2
  60.4 0.0 copy-start.4
  60.4 0.6 copy-done.4
  61.0 0.0 copy-start.6
  61.0 0.6 copy-done.6
  61.7 0.0 copy-start.8
  61.7 0.6 copy-done.8
  62.3 0.0 copy-start.10
  62.3 0.6 copy-done.10
  62.9 0.0 copy-start.12
  62.9 0.6 copy-done.12
  63.6 4.5 %all-to-all-done.block = f32[24,8,128]{2,1,0:T(8,128)S(1)} async-done(((f32[24,8,128]{2,1,0:T(8,128)}), f32[24,8,128]{2,1,0:T(8,128)S(1)}, u32[]{:S(2)}, u32[]{:S(2)}) %all-to-all-start) | async-done | bytes 98336 | tf_op jit(solution)/shard_map/all_to_all | solution.py:520
  68.0 4.7 %all-gather.6 = f32[48,8,128]{2,1,0:T(8,128)S(1)} all-gather(f32[24,8,128]{2,1,0:T(8,128)S(1)} %all-to-all-done.block), channel_id=8, replica_groups={{12,24},{13,25},{14,26},{15,27},{16,28},{17,29},{18,30},{19,31},{20,32}..., dimensions={0}, use_global_device_ids=true | all-gather | bytes 294912 | tf_op jit(solution)/shard_map/all_gather | solution.py:483
  72.8 7.0 %all-gather.7 = f32[4,24,8,128]{3,2,1,0:T(8,128)S(1)} all-gather(f32[2,24,8,128]{3,2,1,0:T(8,128)S(1)} %bitcast.24), channel_id=9, replica_groups={{12,72},{13,73},{14,74},{15,75},{16,76},{17,77},{18,78},{19,79},{20,80}..., dimensions={0}, use_global_device_ids=true | all-gather | bytes 589824 | tf_op jit(solution)/shard_map/all_gather | solution.py:483
  79.8 0.0 copy-start.7
  79.8 0.0 copy-start.9
  79.8 0.0 copy-start.11
  79.8 0.0 copy-start.1
  79.9 0.0 copy-start.3
  79.9 0.0 copy-start.5
  79.9 0.0 copy-start.13
  79.9 7.7 %all_gather.82.outer = f32[2,3,24,8,128]{4,3,2,1,0:T(8,128)S(1)} all-gather(f32[1,3,24,8,128]{4,3,2,1,0:T(8,128)S(1)} %maximum_select_fusion), channel_id=1, replica_groups={{0,12},{24,36},{48,60},{72,84},{96,108},{120,132},{144,156},{168,180},{..., dimensions={0}, use_global_device_ids=true | all-gather | bytes 884736 | tf_op jit(solution)/shard_map/all_gather | solution.py:486
  87.6 0.0 copy-done.7
  87.6 0.0 copy-done.9
  87.6 0.0 copy-done.11
  87.6 0.0 copy-done.1
  87.6 0.0 copy-done.3
  87.6 0.0 copy-done.5
  87.6 0.0 copy-done.13
  87.6 2.9 %shard_map.44 = f32[4,16,512]{2,1,0:T(8,128)} custom-call(f32[24,8,128]{2,1,0:T(8,128)S(1)} %all-to-all-done.block, f32[2,3,24,8,128]{4,3,2,1,0:T(8,128)S(1)} %all_gather.82.outer, f32[8,16,256]{2,1,0:T(8,128)S(1)} %copy-done.3, f32[6,16,256]{2,1,0:T(8,128)S(1)} %copy-done.5, f32[6,16,256]{2,1,0:T(8,128)S(1)} %copy-done.7, f32[6,16,256]{2,1,0:T(8,128)S(1)} %copy-done.9, ...), custom_call_target="tpu_custom_call" | custom-call | tf_op jit(solution)/shard_map/pallas_call | solution.py:530
  (11 shorter events, 0.2 us)
Async XLA Ops:
  19.9 16.5 %copy-start = (f32[12,24,512]{2,1,0:T(8,128)}, f32[12,24,512]{2,1,0:T(8,128)S(1)}, u32[]{:S(2)}) copy-start(f32[12,24,512]{2,1,0:T(8,128)S(1)} %get-tuple-element.34.cz0) | copy-start | bytes 1769476
  37.6 30.4 %all-to-all-start = ((f32[24,8,128]{2,1,0:T(8,128)}), f32[24,8,128]{2,1,0:T(8,128)S(1)}, u32[]{:S(2)}, u32[]{:S(2)}) async-start(f32[24,8,128]{2,1,0:T(8,128)} %shard_map.42), calls=%async_computation | async-start | bytes 196608 | tf_op jit(solution)/shard_map/all_to_all | solution.py:520
  59.7 0.7 copy-start.2
  60.4 0.6 copy-start.4
  61.0 0.6 copy-start.6
  61.7 0.7 copy-start.8
  62.3 0.6 copy-start.10
  62.9 0.6 copy-start.12
  79.8 7.8 %copy-start.7 = (f32[6,16,256]{2,1,0:T(8,128)S(1)}, f32[6,16,256]{2,1,0:T(8,128)}, u32[]{:S(2)}) copy-start(f32[6,16,256]{2,1,0:T(8,128)} %copy-done.6) | copy-start | bytes 294916
  79.8 7.8 %copy-start.9 = (f32[6,16,256]{2,1,0:T(8,128)S(1)}, f32[6,16,256]{2,1,0:T(8,128)}, u32[]{:S(2)}) copy-start(f32[6,16,256]{2,1,0:T(8,128)} %copy-done.8) | copy-start | bytes 294916
  79.8 7.8 %copy-start.11 = (f32[6,16,256]{2,1,0:T(8,128)S(1)}, f32[6,16,256]{2,1,0:T(8,128)}, u32[]{:S(2)}) copy-start(f32[6,16,256]{2,1,0:T(8,128)} %copy-done.10) | copy-start | bytes 294916
  79.8 7.7 %copy-start.1 = (f32[12,24,512]{2,1,0:T(8,128)S(1)}, f32[12,24,512]{2,1,0:T(8,128)}, u32[]{:S(2)}) copy-start(f32[12,24,512]{2,1,0:T(8,128)} %copy-done) | copy-start | bytes 1769476
  79.9 7.7 %copy-start.3 = (f32[8,16,256]{2,1,0:T(8,128)S(1)}, f32[8,16,256]{2,1,0:T(8,128)}, u32[]{:S(2)}) copy-start(f32[8,16,256]{2,1,0:T(8,128)} %copy-done.2) | copy-start | bytes 393220
  79.9 7.7 %copy-start.5 = (f32[6,16,256]{2,1,0:T(8,128)S(1)}, f32[6,16,256]{2,1,0:T(8,128)}, u32[]{:S(2)}) copy-start(f32[6,16,256]{2,1,0:T(8,128)} %copy-done.4) | copy-start | bytes 294916
  79.9 7.7 %copy-start.13 = (bf16[128,256]{1,0:T(8,128)(2,1)S(1)}, bf16[128,256]{1,0:T(8,128)(2,1)}, u32[]{:S(2)}) copy-start(bf16[128,256]{1,0:T(8,128)(2,1)} %copy-done.12) | copy-start | bytes 196612

commit v8 on v6

--- a/solution.py
+++ b/solution.py
@@ -387,10 +387,11 @@
     h, plan, n_h, _ = position()
     wide = s.shape[1] // 2
     tiles = wide // 4
+    places = ((0, 0), (1, 0), (0, 1), None, (1, 1), (0, 2), (1, 2))
     for z in range(14):
         for t in range(tiles):
             at = tiles * (z % 2) + t
-            rows = block.at[at] if 6 <= z < 8 else outer.at[z // 8, z % 8 // 2, at]
+            rows = block.at[at] if 6 <= z < 8 else outer.at[*places[z // 2], at]
             s[z, 4 * t : 4 * t + 4] = rows[0:4]
             s[z, wide + 4 * t : wide + 4 * t + 4] = rows[4:8]
     q = lax.rem(h, 2)
@@ -524,9 +525,9 @@
     level1 = call(k_level1_wide, [eight, six, six, six, six, seven], [box] * 6, full, two)
     groups = [[(2 * i + k) * n_p + t for k in range(2) for t in range(n_p)] for i in range(n_h // 2)]
     block = lax.all_to_all(tiles, ("height", "plan"), split_axis=0, concat_axis=0, tiled=True, axis_index_groups=groups)
-    near = meet(block, links)
-    far = meet(near, leaps)
-    side = jnp.where(odd == 0, jnp.concatenate([far[0], near[0:1]]), jnp.concatenate([near[1:2], far[1]]))
+    far = meet(block, leaps)
+    near = meet(far, links)
+    side = jnp.where(odd == 0, jnp.stack([near[1, 0], near[0, 0], near[0, 1]]), jnp.stack([near[1, 0], near[1, 1], near[0, 1]]))
     outer = pair(side)
     wide = n_p * 4
     flat = (13, wide, 128)

time: 90.5 us -> 90.5 us (level)
  no operation moved by 1% of the time
where the time goes in v8:
time: 90.5 us; the launch traced here: 90.1 us
  blocking collectives  54.7 us (60%)
  starting transfers between devices  19.7 us (22%)
  waiting for transfers between devices  8.33 us (9%)
  Pallas kernels  7.17 us (8%)
    all_gather x6, blocking collectives, meet(): lax.all_gather(x, ('height', 'plan'), axis=0, tiled=False, axis_index_gro...  33.9 us
    all_gather x6, blocking collectives, pair(): lax.all_gather(x, 'height', axis=0, tiled=False, axis_index_groups=cores)  20.8 us
    all_to_all x1, starting transfers between devices, on_device(): lax.all_to_all(tiles, ('height', 'plan'), split_axis=0, concat_axis=0, ti...  19.7 us
    all_to_all x1, waiting for transfers between devices, on_device(): lax.all_to_all(tiles, ('height', 'plan'), split_axis=0, concat_axis=0, ti...  8.33 us
    pallas_call x6, Pallas kernels, call(): pl.pallas_call(body, out_shape=shapes if many else shapes[0], in_specs=vm...  3.33 us
    pallas_call x1, Pallas kernels, on_device(): pl.pallas_call(k_up, out_shape=jax.ShapeDtypeStruct((4, 16, 512), F32), i...  2.8 us
  transfers between devices with their start and end apart: 1, of which 1 were waited for; matrix products, arithmetic and copies ran while one was open for 0% of the time, Pallas kernels for 0%

profile of v8, /device:TPU:33, one launch (start us, length us, event | category | flops | bytes accessed | tf_op | source)
XLA Modules:
  0.0 90.1 jit_solution(16753037062936466500)
XLA Ops:
  0.0 1.0 %shard_map.37 = f32[2,4,16,512]{3,2,1,0:T(8,128)S(1)} custom-call(f32[4,16,512]{2,1,0:T(8,128)} %div.1, f32[4,16,512]{2,1,0:T(8,128)} %density.1, s32[4,16,512]{2,1,0:T(8,128)} %zones.1), custom_call_target="tpu_custom_call" | custom-call | tf_op jit(solution)/shard_map/pallas_call | solution.py:130
  1.0 2.5 %all-gather = f32[4,4,16,512]{3,2,1,0:T(8,128)S(1)} all-gather(f32[2,4,16,512]{3,2,1,0:T(8,128)S(1)} %shard_map.37), channel_id=2, replica_groups={{0,12},{24,36},{48,60},{72,84},{96,108},{120,132},{144,156},{168,180},{..., dimensions={0}, use_global_device_ids=true | all-gather | bytes 786432 | tf_op jit(solution)/shard_map/all_gather | solution.py:494
  3.6 5.7 %all-gather.1 = f32[16,8,512]{2,1,0:T(8,128)S(1)} all-gather(f32[8,8,512]{2,1,0:T(8,128)S(1)} %shard_map.38), channel_id=3, replica_groups={{12,1},{13,2},{14,3},{15,4},{16,5},{17,6},{18,7},{19,8},{20,9},{21,10},..., dimensions={0}, use_global_device_ids=true | all-gather | bytes 393216 | tf_op jit(solution)/shard_map/all_gather | solution.py:491
  9.2 2.0 %all_gather.68.sides = f32[2,8,8,512]{3,2,1,0:T(8,128)S(1)} all-gather(f32[1,8,8,512]{3,2,1,0:T(8,128)S(1)} %constant_dynamic-slice_fusion.2), channel_id=1, replica_groups={{0,12},{24,36},{48,60},{72,84},{96,108},{120,132},{144,156},{168,180},{..., dimensions={0}, use_global_device_ids=true | all-gather | bytes 393216 | tf_op jit(solution)/shard_map/all_gather | solution.py:494
  11.3 6.9 %all-gather.2 = f32[272,512]{1,0:T(8,128)S(1)} all-gather(f32[136,512]{1,0:T(8,128)S(1)} %shard_map.39), channel_id=4, replica_groups={{12,24},{13,25},{14,26},{15,27},{16,28},{17,29},{18,30},{19,31},{20,32}..., dimensions={0}, use_global_device_ids=true | all-gather | bytes 835584 | tf_op jit(solution)/shard_map/all_gather | solution.py:491
  18.2 1.6 %shard_map.40 = (f32[8,24,512]{2,1,0:T(8,128)S(1)}, f32[6,24,512]{2,1,0:T(8,128)S(1)}, f32[6,24,512]{2,1,0:T(8,128)S(1)}, f32[6,24,512]{2,1,0:T(8,128)S(1)}, f32...) custom-call(f32[2,2,4,16,512]{4,3,2,1,0:T(8,128)S(1)} %bitcast.17, ...), custom_call_target="tpu_custom_call" | custom-call | tf_op jit(solution)/shard_map/pallas_call | solution.py:24
  19.9 4.9 %all-gather.3.chip = f32[4,16,256]{2,1,0:T(8,128)S(1)} all-gather(f32[2,16,256]{2,1,0:T(8,128)S(1)} %get-tuple-element.18), channel_id=5, replica_groups={{0,12},{24,36},{48,60},{72,84},{96,108},{120,132},{144,156},{168,180},{..., dimensions={0}, use_global_device_ids=true | all-gather | bytes 98304 | tf_op jit(solution)/shard_map/all_gather | solution.py:494
  24.8 4.6 %all-gather.4 = f32[8,8,256]{2,1,0:T(8,128)S(1)} all-gather(f32[4,8,256]{2,1,0:T(8,128)S(1)} %shard_map.41), channel_id=6, replica_groups={{12,1},{13,2},{14,3},{15,4},{16,5},{17,6},{18,7},{19,8},{20,9},{21,10},..., dimensions={0}, use_global_device_ids=true | all-gather | bytes 98304 | tf_op jit(solution)/shard_map/all_gather | solution.py:491
  29.3 1.9 %all_gather.75 = f32[2,4,8,256]{3,2,1,0:T(8,128)S(1)} all-gather(f32[1,4,8,256]{3,2,1,0:T(8,128)S(1)} %constant_dynamic-slice_fusion.1), channel_id=1, replica_groups={{0,12},{24,36},{48,60},{72,84},{96,108},{120,132},{144,156},{168,180},{..., dimensions={0}, use_global_device_ids=true | all-gather | bytes 98304 | tf_op jit(solution)/shard_map/all_gather | solution.py:494
  31.2 5.1 %all-gather.5 = f32[8,32,256]{2,1,0:T(8,128)S(1)} all-gather(f32[4,32,256]{2,1,0:T(8,128)S(1)} %pad_maximum_fusion.full), channel_id=7, replica_groups={{12,24},{13,25},{14,26},{15,27},{16,28},{17,29},{18,30},{19,31},{20,32}..., dimensions={0}, use_global_device_ids=true | all-gather | bytes 393216 | tf_op jit(solution)/shard_map/all_gather | solution.py:491
  36.3 1.3 %shard_map.42 = f32[24,8,128]{2,1,0:T(8,128)} custom-call(f32[4,32,256]{2,1,0:T(8,128)S(1)} %pad_maximum_fusion.full, f32[2,4,32,256]{3,2,1,0:T(8,128)S(1)} %bitcast.19), custom_call_target="tpu_custom_call" | custom-call | tf_op jit(solution)/shard_map/pallas_call | solution.py:24
  37.6 19.7 %all-to-all-start = ((f32[24,8,128]{2,1,0:T(8,128)}), f32[24,8,128]{2,1,0:T(8,128)S(1)}, u32[]{:S(2)}, u32[]{:S(2)}) async-start(f32[24,8,128]{2,1,0:T(8,128)} %shard_map.42), calls=%async_computation | async-start | bytes 196608 | tf_op jit(solution)/shard_map/all_to_all | solution.py:527
  57.3 2.0 %all_gather.83.two = f32[2,4,32,256]{3,2,1,0:T(8,128)S(1)} all-gather(f32[1,4,32,256]{3,2,1,0:T(8,128)S(1)} %constant_dynamic-slice_fusion), channel_id=1, replica_groups={{0,12},{24,36},{48,60},{72,84},{96,108},{120,132},{144,156},{168,180},{..., dimensions={0}, use_global_device_ids=true | all-gather | bytes 393216 | tf_op jit(solution)/shard_map/all_gather | solution.py:494
  59.3 0.3 shard_map.43
  59.7 8.3 %all-to-all-done.block = f32[24,8,128]{2,1,0:T(8,128)S(1)} async-done(((f32[24,8,128]{2,1,0:T(8,128)}), f32[24,8,128]{2,1,0:T(8,128)S(1)}, u32[]{:S(2)}, u32[]{:S(2)}) %all-to-all-start) | async-done | bytes 98336 | tf_op jit(solution)/shard_map/all_to_all | solution.py:527
  68.0 5.9 %all-gather.6 = f32[48,8,128]{2,1,0:T(8,128)S(1)} all-gather(f32[24,8,128]{2,1,0:T(8,128)S(1)} %all-to-all-done.block), channel_id=8, replica_groups={{12,72},{13,73},{14,74},{15,75},{16,76},{17,77},{18,78},{19,79},{20,80}..., dimensions={0}, use_global_device_ids=true | all-gather | bytes 294912 | tf_op jit(solution)/shard_map/all_gather | solution.py:491
  73.9 5.8 %all-gather.7 = f32[4,24,8,128]{3,2,1,0:T(8,128)S(1)} all-gather(f32[2,24,8,128]{3,2,1,0:T(8,128)S(1)} %bitcast.22), channel_id=9, replica_groups={{12,24},{13,25},{14,26},{15,27},{16,28},{17,29},{18,30},{19,31},{20,32}..., dimensions={0}, use_global_device_ids=true | all-gather | bytes 589824 | tf_op jit(solution)/shard_map/all_gather | solution.py:491
  79.8 7.5 %all_gather.82.outer = f32[2,3,24,8,128]{4,3,2,1,0:T(8,128)S(1)} all-gather(f32[1,3,24,8,128]{4,3,2,1,0:T(8,128)S(1)} %maximum_select_fusion), channel_id=1, replica_groups={{0,12},{24,36},{48,60},{72,84},{96,108},{120,132},{144,156},{168,180},{..., dimensions={0}, use_global_device_ids=true | all-gather | bytes 884736 | tf_op jit(solution)/shard_map/all_gather | solution.py:494
  87.3 2.8 %shard_map.44 = f32[4,16,512]{2,1,0:T(8,128)} custom-call(f32[24,8,128]{2,1,0:T(8,128)S(1)} %all-to-all-done.block, f32[2,3,24,8,128]{4,3,2,1,0:T(8,128)S(1)} %all_gather.82.outer, f32[8,16,256]{2,1,0:T(8,128)S(1)} %get-tuple-element.19.pre1, f32[6,16,256]{2,1,0:T(8,128)S(1)} %get-tuple-element.20.w1, f32[6,16,256]{2,1,0:T(8,128)S(1)} %get-tuple-element.21.g1, ...), custom_call_target="tpu_custom_call" | custom-call | tf_op jit(solution)/shard_map/pallas_call | solution.py:537
  (11 shorter events, 0.2 us)
Async XLA Ops:
  37.6 30.4 %all-to-all-start = ((f32[24,8,128]{2,1,0:T(8,128)}), f32[24,8,128]{2,1,0:T(8,128)S(1)}, u32[]{:S(2)}, u32[]{:S(2)}) async-start(f32[24,8,128]{2,1,0:T(8,128)} %shard_map.42), calls=%async_computation | async-start | bytes 196608 | tf_op jit(solution)/shard_map/all_to_all | solution.py:527
